TPU v7x, 256 devices: a whole 4x4x8 slice. The times are simulated.
256 devices in a mesh: outer: 16 (over x, y), inner: 16 (over z, core).
Axes of the slice: x: 4, y: 4, z: 8, core: 2. Of those that a mesh axis runs over, the one named last changes fastest.
Arguments:
- queries: bfloat16 [65536, 16, 128], P(('outer', 'inner')), may hold values from -6 to 6
- key_rows: bfloat16 [65536, 16, 128], P(('outer', 'inner')), may hold values from -6 to 6
- value_rows: bfloat16 [65536, 16, 128], P(('outer', 'inner')), may hold values from -6 to 6
- key_scale: bfloat16 [65536, 16], P(('outer', 'inner')), may hold values from 0.5 to 2
- value_scale: bfloat16 [65536, 16], P(('outer', 'inner')), may hold values from 0.5 to 2
- cluster_label: int32 [16, 65536, 1], P(None, ('outer', 'inner')), may hold values from 0 to 127; in each aligned block of 256 rows (0 to 255, 256 to 511, ..., all dimensions but the last counted through in order) at most 4 rows name the same one
Outputs:
- attended: bfloat16 [65536, 16, 128], P(('outer', 'inner'))
Inputs may be any that keep to these rules, and one draw needn't show every extreme that they name: `cluster_label`: among the 256 rows of one device for one head, no label occurs more than 4 times, and some label occurs exactly 4 times.
All inputs are finite; a program needn't handle non-finite values.
Results may differ from a plain program's by a relative error of at most 0.0033.
Values may be sent and summed in bfloat16 or wider, within the bound.
No kernel may reach another device: no remote copies, remote signals or barrier semaphores. Data moves between devices by JAX's collectives and lax.ppermute only.
A program may use at most 64 MiB of HBM per device.

v0:
```python
import jax
import jax.numpy as jnp
from jax import lax
from jax.sharding import PartitionSpec as P

COARSE = 16
FINE = 8


def attend(query_block, key_block, value_block, key_factor, value_factor, position):
    factor = query_block.shape[-1] ** (-0.5)
    scores = jnp.dot(query_block, key_block.T, preferred_element_type=jnp.float32)
    scores = scores * (key_factor.astype(jnp.float32) * factor)[None, :]
    visible = (position[None, :] >= 0) & (position[None, :] <= position[:, None])
    highest = jnp.max(jnp.where(visible, scores, jnp.float32(-1e30)), axis=1, keepdims=True)
    unnormed = jnp.where(visible, jnp.exp(scores - highest), jnp.float32(0.0))
    denominator = jnp.sum(unnormed, axis=1)
    weights = (unnormed * value_factor.astype(jnp.float32)[None, :]).astype(jnp.bfloat16)
    numerator = jnp.dot(weights, value_block, preferred_element_type=jnp.float32)
    safe = jnp.where(denominator > 0, denominator, jnp.float32(1.0))
    return (numerator / safe[:, None]).astype(jnp.bfloat16)


def attend_items(query_part, key_part, value_part, key_factor, value_factor, position):
    leading = query_part.shape[:3]
    slots = query_part.shape[3]
    width = query_part.shape[4]
    total = leading[0] * leading[1] * leading[2]

    def single(inputs):
        return attend(*inputs)

    results = lax.map(
        single,
        (
            query_part.reshape(total, slots, width),
            key_part.reshape(total, slots, width),
            value_part.reshape(total, slots, width),
            key_factor.reshape(total, slots),
            value_factor.reshape(total, slots),
            position.reshape(total, slots),
        ),
    )
    return results.reshape(leading + (slots, width))


def shards(queries, key_rows, value_rows, key_scale, value_scale, cluster_label):
    outer_count = lax.axis_size("outer")
    inner_count = lax.axis_size("inner")
    tok_rows, heads, width = queries.shape
    cluster_count = COARSE * FINE
    capacity = max(2, 2 * tok_rows // cluster_count)
    labels = cluster_label[:, :, 0].T
    member = (
        labels[:, :, None] == jnp.arange(cluster_count, dtype=jnp.int32)[None, None, :]
    ).astype(jnp.int32)
    rank = jnp.sum(jnp.cumsum(member, axis=0) * member, axis=2) - 1
    slot = (labels * heads + jnp.arange(heads, dtype=jnp.int32)[None, :]) * capacity + rank
    flat = slot.reshape(-1)
    total = cluster_count * heads * capacity
    item_count = cluster_count * heads // (outer_count * inner_count)
    layout = (outer_count, inner_count, item_count, capacity)
    source = (
        jnp.full((total,), -1, jnp.int32)
        .at[flat]
        .set(jnp.arange(tok_rows * heads, dtype=jnp.int32))
    )
    filled_slot = source >= 0
    source_row = jnp.maximum(source, 0)

    def place(array):
        rows = array.reshape((tok_rows * heads,) + array.shape[2:])
        picked = rows[source_row]
        mask = filled_slot.reshape((total,) + (1,) * (picked.ndim - 1))
        kept = jnp.where(mask, picked, jnp.zeros((), array.dtype))
        return kept.reshape(layout + array.shape[2:])

    device = lax.axis_index("outer") * inner_count + lax.axis_index("inner")
    position_rows = jnp.where(filled_slot, device * tok_rows + source_row // heads, -1).reshape(
        layout
    )
    outgoing = (
        place(queries),
        place(key_rows),
        place(value_rows),
        place(key_scale),
        place(value_scale),
        position_rows,
    )
    arrived = (
        lax.all_to_all(
            lax.all_to_all(outgoing[0], "outer", split_axis=0, concat_axis=3, tiled=True),
            "inner",
            split_axis=1,
            concat_axis=3,
            tiled=True,
        ),
        lax.all_to_all(
            lax.all_to_all(outgoing[1], "outer", split_axis=0, concat_axis=3, tiled=True),
            "inner",
            split_axis=1,
            concat_axis=3,
            tiled=True,
        ),
        lax.all_to_all(
            lax.all_to_all(outgoing[2], "outer", split_axis=0, concat_axis=3, tiled=True),
            "inner",
            split_axis=1,
            concat_axis=3,
            tiled=True,
        ),
        lax.all_to_all(
            lax.all_to_all(outgoing[3], "outer", split_axis=0, concat_axis=3, tiled=True),
            "inner",
            split_axis=1,
            concat_axis=3,
            tiled=True,
        ),
        lax.all_to_all(
            lax.all_to_all(outgoing[4], "outer", split_axis=0, concat_axis=3, tiled=True),
            "inner",
            split_axis=1,
            concat_axis=3,
            tiled=True,
        ),
        lax.all_to_all(
            lax.all_to_all(outgoing[5], "outer", split_axis=0, concat_axis=3, tiled=True),
            "inner",
            split_axis=1,
            concat_axis=3,
            tiled=True,
        ),
    )
    answered = attend_items(*arrived)
    returned = lax.all_to_all(
        lax.all_to_all(answered, "inner", split_axis=3, concat_axis=1, tiled=True),
        "outer",
        split_axis=3,
        concat_axis=0,
        tiled=True,
    )
    rows_back = returned.reshape(total, width)
    return rows_back[flat].reshape(tok_rows, heads, width)


def solution(mesh):
    placed = (
        P(("outer", "inner"), None, None),
        P(("outer", "inner"), None, None),
        P(("outer", "inner"), None, None),
        P(("outer", "inner"), None),
        P(("outer", "inner"), None),
        P(None, ("outer", "inner"), None),
    )
    return jax.shard_map(
        shards,
        mesh=mesh,
        in_specs=placed,
        out_specs=P(("outer", "inner"), None, None),
        check_vma=False,
    )
```

profile of v0, /device:TPU:1, one launch (start us, length us, event | category | flops | bytes accessed | tf_op | source)
XLA Modules:
  0.0 725.7 jit_solution(17662441475299198069)
XLA Ops:
  5.6 15.5 %scatter_custom_fusion = s32[8192]{0:T(1024)S(1)} fusion(s32[4096]{0:T(1024)S(1)} %bitcast.189, s32[4096]{0:T(1024)S(1)} %iota.12, s32[]{:T(128)} %constant.67.clone.1), kind=kCustom, calls=%fused_computation.58 | custom fusion | bytes 32772 | tf_op jit(solution)/shard_map/scatter | solution.py:66
  21.5 50.7 %gather_fusion.3 = bf16[8192]{0:T(1024)(128)(2,1)S(1)} fusion(bf16[4096]{0:T(1024)(128)(2,1)S(1)} %reshape.142, s32[8192]{0:T(1024)S(1)} %maximum_clamp_fusion), kind=kCustom, calls=%fused_computation.3 | custom fusion | bytes 65536 | tf_op jit(solution)/shard_map/gather | solution.py:73
  72.5 50.7 %gather_fusion.2 = bf16[8192]{0:T(1024)(128)(2,1)S(1)} fusion(bf16[4096]{0:T(1024)(128)(2,1)S(1)} %reshape.139, s32[8192]{0:T(1024)S(1)} %maximum_clamp_fusion), kind=kCustom, calls=%fused_computation.2 | custom fusion | bytes 65536 | tf_op jit(solution)/shard_map/gather | solution.py:73
  126.0 7.6 %all-to-all-start.6 = ((bf16[16,2,256]{2,1,0:T(2,128)(2,1)}), bf16[16,2,256]{2,1,0:T(2,128)(2,1)S(1)}, u32[]{:S(2)}, u32[]{:S(2)}) async-start(bf16[16,2,256]{2,1,0:T(2,128)(2,1)} %reshape.219), calls=%async_computation.6 | async-start | bytes 32768 | tf_op jit(solution)/shard_map/all_to_all | solution.py:113
  136.4 3.7 all-to-all-done.6
  140.0 3.5 all-to-all-start.8
  146.3 3.6 all-to-all-done.8
  149.9 3.5 all-to-all-start
  154.4 5.4 all-to-all-done
  159.8 12.9 %all-to-all-start.7 = ((bf16[16,2,256]{2,1,0:T(2,128)(2,1)}), bf16[16,2,256]{2,1,0:T(2,128)(2,1)S(1)}, u32[]{:S(2)}, u32[]{:S(2)}) async-start(bf16[16,2,256]{2,1,0:T(2,128)(2,1)} %reshape.221), calls=%async_computation.7 | async-start | bytes 32768 | tf_op jit(solution)/shard_map/all_to_all | solution.py:112
  173.7 6.3 all-to-all-done.7
  180.0 3.7 all-to-all-start.9
  186.4 29.2 %gather_fusion = bf16[8192,128]{1,0:T(8,128)(2,1)} fusion(bf16[4096,128]{1,0:T(8,128)(2,1)S(1)} %bitcast.156, s32[8192]{0:T(1024)S(1)} %maximum_clamp_fusion), kind=kCustom, calls=%fused_computation | custom fusion | bytes 4227072 | tf_op jit(solution)/shard_map/gather | solution.py:73
  215.6 29.2 %gather_fusion.1 = bf16[8192,128]{1,0:T(8,128)(2,1)} fusion(bf16[4096,128]{1,0:T(8,128)(2,1)S(1)} %bitcast.157, s32[8192]{0:T(1024)S(1)} %maximum_clamp_fusion), kind=kCustom, calls=%fused_computation.1 | custom fusion | bytes 4227072 | tf_op jit(solution)/shard_map/gather | solution.py:73
  244.8 29.2 %gather_fusion.4 = bf16[8192,128]{1,0:T(8,128)(2,1)} fusion(bf16[4096,128]{1,0:T(8,128)(2,1)S(1)} %bitcast.158, s32[8192]{0:T(1024)S(1)} %maximum_clamp_fusion), kind=kCustom, calls=%fused_computation.4 | custom fusion | bytes 4227072 | tf_op jit(solution)/shard_map/gather | solution.py:73
  276.3 7.3 %all-to-all-start.1 = ((s32[16,1,512]{2,1,0:T(1,128)}), s32[16,1,512]{2,1,0:T(1,128)S(1)}, u32[]{:S(2)}, u32[]{:S(2)}) async-start(s32[16,1,512]{2,1,0:T(1,128)} %reshape.217), calls=%async_computation.1 | async-start | bytes 65536 | tf_op jit(solution)/shard_map/all_to_all | solution.py:126
  283.6 5.9 copy_select_fusion
  291.0 31.7 %all_to_all.231 = bf16[16,16,8,4,128]{4,2,3,1,0:T(8,128)(2,1)} all-to-all(bf16[16,16,8,4,128]{4,2,3,1,0:T(8,128)(2,1)} %get-tuple-element.96), channel_id=1, replica_groups=mesh['outer'=16,'inner'=16] {'outer'}, dimensions={0} | all-to-all | bytes 4194304 | tf_op jit(solution)/shard_map/all_to_all | solution.py:92
  322.7 29.8 %all_to_all.232 = bf16[16,16,8,4,128]{4,2,3,1,0:T(8,128)(2,1)} all-to-all(bf16[16,16,8,4,128]{4,2,3,1,0:T(8,128)(2,1)S(1)} %copy-done.5), channel_id=1, replica_groups=mesh['outer'=16,'inner'=16] {'outer'}, dimensions={0} | all-to-all | bytes 4194304 | tf_op jit(solution)/shard_map/all_to_all | solution.py:99
  352.5 4.7 all-to-all-start.10
  357.2 3.5 copy.54
  360.6 21.8 %all-to-all-done.10 = bf16[16,16,8,4,128]{4,2,3,1,0:T(8,128)(2,1)S(1)} async-done(((bf16[16,16,8,4,128]{4,2,3,1,0:T(8,128)(2,1)}), bf16[16,16,8,4,128]{4,2,3,1,0:T(8,128)(2,1)S(1)}, u32[]{:S(2)}, u32[]{:S(2)}) %all-to-all-start.10) | async-done | bytes 2097184 | tf_op jit(solution)/shard_map/all_to_all | solution.py:106
  383.9 10.8 %all-to-all-start.3 = ((bf16[1,16,8,64,128]{4,2,3,0,1:T(8,128)(2,1)}), bf16[1,16,8,64,128]{4,2,3,0,1:T(8,128)(2,1)S(1)}, u32[]{:S(2)}, u32[]{:S(2)}) async-start(bf16[1,16,8,64,128]{4,2,3,0,1:T(8,128)(2,1)} %bitcast.165), calls=%async_computation.3 | async-start | bytes 4194304 | tf_op jit(solution)/shard_map/all_to_all | solution.py:91
  394.6 3.5 copy.57
  398.1 45.5 %all-to-all-done.3 = bf16[1,16,8,64,128]{4,2,3,0,1:T(8,128)(2,1)S(1)} async-done(((bf16[1,16,8,64,128]{4,2,3,0,1:T(8,128)(2,1)}), bf16[1,16,8,64,128]{4,2,3,0,1:T(8,128)(2,1)S(1)}, u32[]{:S(2)}, u32[]{:S(2)}) %all-to-all-start.3) | async-done | bytes 2097184 | tf_op jit(solution)/shard_map/all_to_all | solution.py:91
  443.6 5.0 all-to-all-start.5
  448.6 3.5 copy.68
  452.0 45.6 %all-to-all-done.5 = bf16[1,16,8,64,128]{4,2,3,0,1:T(8,128)(2,1)} async-done(((bf16[1,16,8,64,128]{4,2,3,0,1:T(8,128)(2,1)}), bf16[1,16,8,64,128]{4,2,3,0,1:T(8,128)(2,1)}, u32[]{:S(2)}, u32[]{:S(2)}) %all-to-all-start.5) | async-done | bytes 2097184 | tf_op jit(solution)/shard_map/all_to_all | solution.py:98
  497.6 5.0 all-to-all-start.11
  504.0 1.7 copy.70
  505.6 1.9 copy.71
  507.5 44.2 %all-to-all-done.11 = bf16[1,16,8,64,128]{4,2,3,0,1:T(8,128)(2,1)} async-done(((bf16[1,16,8,64,128]{4,2,3,0,1:T(8,128)(2,1)}), bf16[1,16,8,64,128]{4,2,3,0,1:T(8,128)(2,1)}, u32[]{:S(2)}, u32[]{:S(2)}) %all-to-all-start.11) | async-done | bytes 2097184 | tf_op jit(solution)/shard_map/all_to_all | solution.py:105
  551.7 3.2 copy.72
  554.8 60.4 %while.10 = (s32[]{:T(128)}, bf16[8,1024,128]{2,1,0:T(8,128)(2,1)}, s32[8,1024]{1,0:T(8,128)S(1)}, bf16[8,1024,128]{2,1,0:T(8,128)(2,1)}, bf16[8,1024,128]{2,1,0...) while((s32[]{:T(128)}, bf16[8,1024,128]{2,1,0:T(8,128)(2,1)}, ...), condition=%wide.region_7.8_spmd, body=%wide.region_4.7_spmd.sunk | while | flops 556011520 | bytes 13723753 | solution.py:33
  554.9 2.1 select_reduce_fusion.2
  557.0 1.7 fusion.30
  558.7 3.6 fusion.31
  562.4 2.1 select_reduce_fusion.2
  564.6 1.7 fusion.30
  566.3 3.6 fusion.31
  570.0 2.1 select_reduce_fusion.2
  572.1 1.7 fusion.30
  573.8 3.6 fusion.31
  577.5 2.1 select_reduce_fusion.2
  579.6 1.7 fusion.30
  581.4 3.6 fusion.31
  585.1 2.1 select_reduce_fusion.2
  587.2 1.7 fusion.30
  588.9 3.6 fusion.31
  592.6 2.1 select_reduce_fusion.2
  594.7 1.7 fusion.30
  596.5 3.6 fusion.31
  600.1 2.1 select_reduce_fusion.2
  602.3 1.7 fusion.30
  604.0 3.6 fusion.31
  607.7 2.1 select_reduce_fusion.2
  609.8 1.7 fusion.30
  611.6 3.6 fusion.31
  615.2 2.9 copy.87
  618.1 55.8 %all_to_all.233 = bf16[1,1,8,1024,128]{4,2,1,0,3:T(8,128)(2,1)S(1)} all-to-all(bf16[1,1,8,1024,128]{4,2,1,0,3:T(8,128)(2,1)S(1)} %bitcast.168), channel_id=1, replica_groups=mesh['outer'=16,'inner'=16] {'inner'}, dimensions={3} | all-to-all | bytes 4194304 | tf_op jit(solution)/shard_map/all_to_all | solution.py:136
  673.9 1.9 copy.86
  675.9 3.7 all-to-all-start.13
  679.6 29.4 %all-to-all-done.13 = bf16[1,16,8,64,128]{4,2,1,0,3:T(8,128)(2,1)S(1)} async-done(((bf16[1,16,8,64,128]{4,2,1,0,3:T(8,128)(2,1)}), bf16[1,16,8,64,128]{4,2,1,0,3:T(8,128)(2,1)S(1)}, u32[]{:S(2)}, u32[]{:S(2)}) %all-to-all-start.13) | async-done | bytes 2097184 | tf_op jit(solution)/shard_map/all_to_all | solution.py:135
  710.7 15.0 %gather_fusion.5 = bf16[4096,128]{1,0:T(8,128)(2,1)} fusion(bf16[8192,128]{1,0:T(8,128)(2,1)S(1)} %bitcast.159, s32[4096]{0:T(1024)S(1)} %broadcast_clamp_fusion), kind=kCustom, calls=%fused_computation.5 | custom fusion | bytes 2113536 | tf_op jit(solution)/shard_map/gather | solution.py:143
  (114 shorter events, 27.5 us)
Async XLA Ops:
  0.0 186.4 %copy-start = (bf16[256,16,128]{2,1,0:T(8,128)(2,1)S(1)}, bf16[256,16,128]{2,1,0:T(8,128)(2,1)}, u32[]{:S(2)}) copy-start(bf16[256,16,128]{2,1,0:T(8,128)(2,1)} %param.8) | copy-start | bytes 3145732
  3.9 1.5 copy-start.7
  3.9 17.3 %copy-start.8 = (bf16[256,16]{0,1:T(8,128)(2,1)S(1)}, bf16[256,16]{0,1:T(8,128)(2,1)}, u32[]{:S(2)}) copy-start(bf16[256,16]{0,1:T(8,128)(2,1)} %param.12) | copy-start | bytes 24580
  21.4 50.8 %copy-start.9 = (bf16[256,16]{0,1:T(8,128)(2,1)S(1)}, bf16[256,16]{0,1:T(8,128)(2,1)}, u32[]{:S(2)}) copy-start(bf16[256,16]{0,1:T(8,128)(2,1)} %param.11) | copy-start | bytes 24580
  126.0 14.0 %all-to-all-start.6 = ((bf16[16,2,256]{2,1,0:T(2,128)(2,1)}), bf16[16,2,256]{2,1,0:T(2,128)(2,1)S(1)}, u32[]{:S(2)}, u32[]{:S(2)}) async-start(bf16[16,2,256]{2,1,0:T(2,128)(2,1)} %reshape.219), calls=%async_computation.6 | async-start | bytes 32768 | tf_op jit(solution)/shard_map/all_to_all | solution.py:113
  140.0 9.9 %all-to-all-start.8 = ((bf16[16,2,256]{2,1,0:T(2,128)(2,1)}), bf16[16,2,256]{2,1,0:T(2,128)(2,1)S(1)}, u32[]{:S(2)}, u32[]{:S(2)}) async-start(bf16[16,2,256]{2,1,0:T(2,128)(2,1)} %reshape.223), calls=%async_computation.8 | async-start | bytes 32768 | tf_op jit(solution)/shard_map/all_to_all | solution.py:120
  149.9 9.9 %all-to-all-start = ((s32[16,1,512]{2,1,0:T(1,128)}), s32[16,1,512]{2,1,0:T(1,128)S(1)}, u32[]{:S(2)}, u32[]{:S(2)}) async-start(s32[16,1,512]{2,1,0:T(1,128)} %reshape.215), calls=%async_computation | async-start | bytes 65536 | tf_op jit(solution)/shard_map/all_to_all | solution.py:127
  159.8 20.2 %all-to-all-start.7 = ((bf16[16,2,256]{2,1,0:T(2,128)(2,1)}), bf16[16,2,256]{2,1,0:T(2,128)(2,1)S(1)}, u32[]{:S(2)}, u32[]{:S(2)}) async-start(bf16[16,2,256]{2,1,0:T(2,128)(2,1)} %reshape.221), calls=%async_computation.7 | async-start | bytes 32768 | tf_op jit(solution)/shard_map/all_to_all | solution.py:112
  180.0 96.3 %all-to-all-start.9 = ((bf16[16,2,256]{2,1,0:T(2,128)(2,1)}), bf16[16,2,256]{2,1,0:T(2,128)(2,1)S(1)}, u32[]{:S(2)}, u32[]{:S(2)}) async-start(bf16[16,2,256]{2,1,0:T(2,128)(2,1)} %reshape.225), calls=%async_computation.9 | async-start | bytes 32768 | tf_op jit(solution)/shard_map/all_to_all | solution.py:119
  186.4 29.2 %copy-start.2 = (bf16[256,16,128]{2,1,0:T(8,128)(2,1)S(1)}, bf16[256,16,128]{2,1,0:T(8,128)(2,1)}, u32[]{:S(2)}) copy-start(bf16[256,16,128]{2,1,0:T(8,128)(2,1)} %param.9) | copy-start | bytes 3145732
  215.6 29.2 %copy-start.3 = (bf16[256,16,128]{2,1,0:T(8,128)(2,1)S(1)}, bf16[256,16,128]{2,1,0:T(8,128)(2,1)}, u32[]{:S(2)}) copy-start(bf16[256,16,128]{2,1,0:T(8,128)(2,1)} %param.10) | copy-start | bytes 3145732
  244.8 38.8 %copy-start.4 = (bf16[8192,128]{1,0:T(8,128)(2,1)S(1)}, bf16[8192,128]{1,0:T(8,128)(2,1)}, u32[]{:S(2)}) copy-start(bf16[8192,128]{1,0:T(8,128)(2,1)} %gather_fusion) | copy-start | bytes 6291460
  276.3 14.7 %all-to-all-start.1 = ((s32[16,1,512]{2,1,0:T(1,128)}), s32[16,1,512]{2,1,0:T(1,128)S(1)}, u32[]{:S(2)}, u32[]{:S(2)}) async-start(s32[16,1,512]{2,1,0:T(1,128)} %reshape.217), calls=%async_computation.1 | async-start | bytes 65536 | tf_op jit(solution)/shard_map/all_to_all | solution.py:126
  291.0 31.7 %copy-start.5 = (bf16[16,16,8,4,128]{4,2,3,1,0:T(8,128)(2,1)S(1)}, bf16[16,16,8,4,128]{4,2,3,1,0:T(8,128)(2,1)}, u32[]{:S(2)}) copy-start(bf16[16,16,8,4,128]{4,2,3,1,0:T(8,128)(2,1)} %get-tuple-element.95) | copy-start | bytes 6291460
  352.5 30.0 %all-to-all-start.10 = ((bf16[16,16,8,4,128]{4,2,3,1,0:T(8,128)(2,1)}), bf16[16,16,8,4,128]{4,2,3,1,0:T(8,128)(2,1)S(1)}, u32[]{:S(2)}, u32[]{:S(2)}) async-start(bf16[16,16,8,4,128]{4,2,3,1,0:T(8,128)(2,1)} %get-tuple-element.94), calls=%async_computation.10 | async-start | bytes 4194304 | tf_op jit(solution)/shard_map/all_to_all | solution.py:106
  382.5 1.4 copy-start.6
  383.9 59.7 %all-to-all-start.3 = ((bf16[1,16,8,64,128]{4,2,3,0,1:T(8,128)(2,1)}), bf16[1,16,8,64,128]{4,2,3,0,1:T(8,128)(2,1)S(1)}, u32[]{:S(2)}, u32[]{:S(2)}) async-start(bf16[1,16,8,64,128]{4,2,3,0,1:T(8,128)(2,1)} %bitcast.165), calls=%async_computation.3 | async-start | bytes 4194304 | tf_op jit(solution)/shard_map/all_to_all | solution.py:91
  443.6 54.0 %all-to-all-start.5 = ((bf16[1,16,8,64,128]{4,2,3,0,1:T(8,128)(2,1)}), bf16[1,16,8,64,128]{4,2,3,0,1:T(8,128)(2,1)}, u32[]{:S(2)}, u32[]{:S(2)}) async-start(bf16[1,16,8,64,128]{4,2,3,0,1:T(8,128)(2,1)} %bitcast.166), calls=%async_computation.5 | async-start | bytes 4194304 | tf_op jit(solution)/shard_map/all_to_all | solution.py:98
  497.6 54.0 %all-to-all-start.11 = ((bf16[1,16,8,64,128]{4,2,3,0,1:T(8,128)(2,1)}), bf16[1,16,8,64,128]{4,2,3,0,1:T(8,128)(2,1)}, u32[]{:S(2)}, u32[]{:S(2)}) async-start(bf16[1,16,8,64,128]{4,2,3,0,1:T(8,128)(2,1)} %bitcast.164), calls=%async_computation.11 | async-start | bytes 4194304 | tf_op jit(solution)/shard_map/all_to_all | solution.py:105
  675.9 33.2 %all-to-all-start.13 = ((bf16[1,16,8,64,128]{4,2,1,0,3:T(8,128)(2,1)}), bf16[1,16,8,64,128]{4,2,1,0,3:T(8,128)(2,1)S(1)}, u32[]{:S(2)}, u32[]{:S(2)}) async-start(bf16[1,16,8,64,128]{4,2,1,0,3:T(8,128)(2,1)} %bitcast.167), calls=%async_computation.13 | async-start | bytes 4194304 | tf_op jit(solution)/shard_map/all_to_all | solution.py:135
  710.6 15.0 %copy-start.1 = (bf16[256,16,128]{2,1,0:T(8,128)(2,1)S(1)}, bf16[256,16,128]{2,1,0:T(8,128)(2,1)}, u32[]{:S(2)}) copy-start(bf16[256,16,128]{2,1,0:T(8,128)(2,1)} %param.8) | copy-start | bytes 3145732
where the time goes:
time: 727 us; the launch traced here: 726 us
  local copies, waits for them, and re-layouts  263 us (36%)
  waiting for transfers between devices  207 us (28%)
  blocking collectives  117 us (16%)
  starting transfers between devices  67.5 us (9%)
  matrix products  46 us (6%)
  other arithmetic  23.8 us (3%)
    gather x5, local copies, waits for them, and re-layouts, place(): picked = rows[source_row]  189 us
    all_to_all x1, blocking collectives, shards(): lax.all_to_all(answered, 'inner', split_axis=3, concat_axis=1, tiled=True)  55.8 us
    all_to_all x1, waiting for transfers between devices, shards(): lax.all_to_all(lax.all_to_all(outgoing[1], 'outer', split_axis=0, concat_...  45.6 us
    all_to_all x1, waiting for transfers between devices, shards(): lax.all_to_all(lax.all_to_all(outgoing[0], 'outer', split_axis=0, concat_...  45.5 us
    all_to_all x1, waiting for transfers between devices, shards(): lax.all_to_all(lax.all_to_all(outgoing[2], 'outer', split_axis=0, concat_...  44.2 us
    all_to_all x1, blocking collectives, shards(): lax.all_to_all(outgoing[0], 'outer', split_axis=0, concat_axis=3, tiled=T...  31.7 us
    all_to_all x1, blocking collectives, shards(): lax.all_to_all(outgoing[1], 'outer', split_axis=0, concat_axis=3, tiled=T...  29.8 us
    all_to_all x1, waiting for transfers between devices, shards(): lax.all_to_all(lax.all_to_all(answered, 'inner', split_axis=3, concat_axi...  29.4 us
  transfers between devices with their start and end apart: 11, of which 10 were waited for; matrix products, arithmetic and copies ran while one was open for 17% of the time, Pallas kernels for 0%

commit v1 on v0

v1 whole, which is shorter than its diff:
```python
import jax
import jax.numpy as jnp
from jax import lax
from jax.experimental import pallas as pl
from jax.experimental.pallas import tpu as pltpu
from jax.sharding import PartitionSpec as P

COARSE = 16
FINE = 8
CAP = 4
CLUSTERS = COARSE * FINE
SLOTS = CLUSTERS * CAP
CHUNK = FINE * CAP
BOTH = ("outer", "inner")
NT = (((1,), (1,)), ((), ()))
NEG = -1e30
LOG2E = 1.4426950408889634


def iota(shape, axis):
    return lax.broadcasted_iota(jnp.int32, shape, axis)


def one_hot(condition):
    return jnp.where(condition, 1.0, 0.0).astype(jnp.bfloat16)


def matmul(a, b):
    return jnp.dot(a, b, preferred_element_type=jnp.float32)


def matmul_nt(a, b):
    return lax.dot_general(a, b, NT, preferred_element_type=jnp.float32)


def swap_matrix(major, minor, unit):
    total = major * minor * unit
    row, column = iota((total, total), 0), iota((total, total), 1)
    b, a, u = row // (major * unit), (row // unit) % major, row % unit
    return one_hot(column == (a * minor + b) * unit + u)


def slots_kernel(label_ref, key_scale_ref, value_scale_ref, slot_ref, scale_ref):
    heads, rows = label_ref.shape
    eye = one_hot(iota((heads, heads), 0) == iota((heads, heads), 1))
    key_rows = matmul_nt(eye, key_scale_ref[...])
    value_rows = matmul_nt(eye, value_scale_ref[...])
    before = one_hot(iota((rows, rows), 0) < iota((rows, rows), 1))
    for h in range(heads):
        label = label_ref[h : h + 1, :]
        member = iota((CLUSTERS, rows), 0) == label
        count = matmul(one_hot(member), before)
        rank = jnp.sum(jnp.where(member, count, 0.0), axis=0, keepdims=True).astype(jnp.int32)
        slot_ref[h : h + 1, :] = label * CAP + rank
        coarse = one_hot(iota((COARSE, rows), 0) == label // FINE)
        here = iota((CHUNK, rows), 0) == (label % FINE) * CAP + rank
        scales = jnp.concatenate(
            [
                jnp.where(here, key_rows[h : h + 1, :], 0.0),
                jnp.where(here, value_rows[h : h + 1, :], 0.0),
                jnp.zeros((128 - 2 * CHUNK, rows), jnp.float32),
            ],
            axis=0,
        ).astype(jnp.bfloat16)
        scale_ref[pl.ds(h, COARSE, stride=heads), :] = matmul_nt(coarse, scales)


HALF = 8


def place_kernel(slot_ref, q_ref, k_ref, v_ref, out_ref, by_head):
    step = pl.program_id(0)
    rows, _, width = q_ref.shape
    group = 256 // HALF
    swap = swap_matrix(group, HALF, 1)
    for a, ref in enumerate((q_ref, k_ref, v_ref)):
        for g in range(rows // group):
            block = ref[g * group : (g + 1) * group].reshape(256, width)
            turned = matmul(swap, block).astype(jnp.bfloat16).reshape(HALF, group, width)
            by_head[:, g * group : (g + 1) * group, a * width : (a + 1) * width] = turned
    for h in range(HALF):
        slot = slot_ref[pl.ds(step * HALF + h, 1), :]
        pick = one_hot(iota((SLOTS, rows), 0) == slot)
        placed = matmul(pick, by_head[h]).astype(jnp.bfloat16)
        for a in range(3):
            out_ref[:, h, a * CHUNK : (a + 1) * CHUNK, :] = placed[
                :, a * width : (a + 1) * width
            ].reshape(COARSE, CHUNK, width)


def attend_kernel(message_ref, scale_ref, out_ref, qs, ks, vs, os, scales):
    f = pl.program_id(0)
    sources, _, width = message_ref.shape
    total = sources * CAP
    batch = 256 // CHUNK
    unit = batch * CAP

    @pl.when(f == 0)
    def _():
        swap = swap_matrix(batch, FINE, CAP)

        @pl.loop(0, sources // batch)
        def _(g):
            for a, ref in enumerate((qs, ks, vs)):
                block = message_ref[pl.ds(g * batch, batch), a * CHUNK : (a + 1) * CHUNK, :]
                turned = matmul(swap, block.reshape(256, width)).astype(jnp.bfloat16)
                ref[:, pl.ds(pl.multiple_of(g * unit, unit), unit), :] = turned.reshape(
                    FINE, unit, width
                )

        spread = one_hot(iota((total, sources), 0) // CAP == iota((total, sources), 1))
        table = matmul(spread, scale_ref[...].astype(jnp.bfloat16))
        lane, row = iota((total, 128), 1), iota((total, 128), 0)
        table = jnp.where(lane % CAP == row % CAP, table, 0.0).astype(jnp.bfloat16)
        gather = one_hot(iota((2 * FINE, 128), 0) == iota((2 * FINE, 128), 1) // CAP)
        scales[...] = matmul_nt(gather, table)

    key_scale = scales[pl.ds(f, 1), :]
    value_scale = scales[pl.ds(FINE + f, 1), :]
    factor = key_scale * (width**-0.5 * LOG2E)
    bias = jnp.where(key_scale > 0.0, 0.0, NEG)
    tile = 256
    ahead = iota((tile, tile), 1) > iota((tile, tile), 0)
    for t in range(total // tile):
        here = slice(t * tile, (t + 1) * tile)
        query = qs[f, here, :]
        pieces = []
        for u in range(t + 1):
            there = slice(u * tile, (u + 1) * tile)
            score = matmul_nt(query, ks[f, there, :])
            score = score * factor[:, there] + bias[:, there]
            if u == t:
                score = jnp.where(ahead, NEG, score)
            pieces.append(score)
        highest = pieces[0]
        for piece in pieces[1:]:
            highest = jnp.maximum(highest, piece)
        highest = jnp.max(highest, axis=1, keepdims=True)
        below, result = None, None
        for u, piece in enumerate(pieces):
            there = slice(u * tile, (u + 1) * tile)
            unnormed = jnp.exp2(piece - highest)
            weights = (unnormed * value_scale[:, there]).astype(jnp.bfloat16)
            term = matmul(weights, vs[f, there, :])
            below = unnormed if below is None else below + unnormed
            result = term if result is None else result + term
        below = jnp.sum(below, axis=1, keepdims=True)
        os[f, here, :] = (result / below).astype(jnp.bfloat16)

    @pl.when(f == FINE - 1)
    def _():
        swap = swap_matrix(FINE, batch, CAP)

        @pl.loop(0, sources // batch)
        def _(g):
            block = os[:, pl.ds(pl.multiple_of(g * unit, unit), unit), :].reshape(256, width)
            turned = matmul(swap, block).astype(jnp.bfloat16)
            out_ref[pl.ds(g * batch, batch)] = turned.reshape(batch, CHUNK, width)


def unplace_kernel(slot_ref, in_ref, out_ref, by_head):
    step = pl.program_id(0)
    rows = slot_ref.shape[0]
    width = in_ref.shape[3]
    group = 256 // HALF
    swap = swap_matrix(HALF, group, 1)
    lane = iota(slot_ref.shape, 1)
    for h in range(HALF):
        slot = jnp.sum(
            jnp.where(lane == step * HALF + h, slot_ref[...], 0), axis=1, keepdims=True
        )
        pick = one_hot(iota((rows, SLOTS), 1) == slot)
        by_head[h] = matmul(pick, in_ref[:, h].reshape(SLOTS, width)).astype(jnp.bfloat16)
    for g in range(rows // group):
        block = by_head[:, g * group : (g + 1) * group, :].reshape(256, width)
        out_ref[g * group : (g + 1) * group] = (
            matmul(swap, block).astype(jnp.bfloat16).reshape(group, HALF, width)
        )


def shards(queries, key_rows, value_rows, key_scale, value_scale, cluster_label):
    rows, heads, width = queries.shape
    devices = lax.axis_size("outer") * lax.axis_size("inner")
    labels = cluster_label.reshape(heads, rows)
    bf16, f32 = jnp.bfloat16, jnp.float32
    slots, scales = pl.pallas_call(
        slots_kernel,
        out_shape=(
            jax.ShapeDtypeStruct((heads, rows), jnp.int32),
            jax.ShapeDtypeStruct((COARSE * heads, 128), f32),
        ),
        cost_estimate=pl.CostEstimate(flops=10**8, bytes_accessed=10**6, transcendentals=0),
    )(labels, key_scale, value_scale)
    scales = lax.all_to_all(scales.reshape(devices, 1, 128), BOTH, 0, 0, tiled=True)
    scales = scales.reshape(devices, 128)

    tokens = pl.BlockSpec((rows, HALF, width), lambda i: (0, i, 0))
    message = pl.pallas_call(
        place_kernel,
        grid=(heads // HALF,),
        in_specs=[pl.BlockSpec((heads, rows), lambda i: (0, 0)), tokens, tokens, tokens],
        out_specs=pl.BlockSpec((COARSE, HALF, 3 * CHUNK, width), lambda i: (0, i, 0, 0)),
        out_shape=jax.ShapeDtypeStruct((COARSE, heads, 3 * CHUNK, width), bf16),
        scratch_shapes=[pltpu.VMEM((HALF, rows, 3 * width), bf16)],
        cost_estimate=pl.CostEstimate(
            flops=3 * 10**9, bytes_accessed=9 * 2**20, transcendentals=0
        ),
    )(slots, queries, key_rows, value_rows)
    message = message.reshape(devices, 3 * CHUNK, width)
    message = lax.all_to_all(message, BOTH, 0, 0, tiled=True)

    total = devices * CAP
    table = pltpu.VMEM((FINE, total, width), bf16)
    answer = pl.pallas_call(
        attend_kernel,
        grid=(FINE,),
        in_specs=[
            pl.BlockSpec((devices, 3 * CHUNK, width), lambda i: (0, 0, 0)),
            pl.BlockSpec((devices, 128), lambda i: (0, 0)),
        ],
        out_specs=pl.BlockSpec((devices, CHUNK, width), lambda i: (0, 0, 0)),
        out_shape=jax.ShapeDtypeStruct((devices, CHUNK, width), bf16),
        scratch_shapes=[table, table, table, table, pltpu.VMEM((2 * FINE, total), f32)],
        cost_estimate=pl.CostEstimate(
            flops=4 * 10**9, bytes_accessed=8 * 2**20, transcendentals=5 * 10**6
        ),
    )(message, scales)
    answer = lax.all_to_all(answer, BOTH, 0, 0, tiled=True)

    return pl.pallas_call(
        unplace_kernel,
        grid=(heads // HALF,),
        in_specs=[
            pl.BlockSpec((rows, heads), lambda i: (0, 0)),
            pl.BlockSpec((COARSE, HALF, CHUNK, width), lambda i: (0, i, 0, 0)),
        ],
        out_specs=pl.BlockSpec((rows, HALF, width), lambda i: (0, i, 0)),
        out_shape=jax.ShapeDtypeStruct((rows, heads, width), bf16),
        scratch_shapes=[pltpu.VMEM((HALF, rows, width), bf16)],
        cost_estimate=pl.CostEstimate(
            flops=10**9, bytes_accessed=3 * 2**20, transcendentals=0
        ),
    )(slots.T, answer.reshape(COARSE, heads, CHUNK, width))


def solution(mesh):
    placed = (
        P(BOTH, None, None),
        P(BOTH, None, None),
        P(BOTH, None, None),
        P(BOTH, None),
        P(BOTH, None),
        P(None, BOTH, None),
    )
    return jax.shard_map(
        shards,
        mesh=mesh,
        in_specs=placed,
        out_specs=P(BOTH, None, None),
        check_vma=False,
    )
```

time: 727 us -> 288 us (0.40)
  local copies, waits for them, and re-layouts: 263 us -> 6.25 us
  waiting for transfers between devices: 207 us -> 59.1 us
  Pallas kernels: 0 us -> 48.3 us
  starting transfers between devices: 67.5 us -> 20.8 us
  matrix products: 46 us -> 0 us
  blocking collectives: 117 us -> 153 us
  other arithmetic: 23.8 us -> 0 us
    gather x6 -> x0, local copies, waits for them, and re-layouts: 204 us -> none  [the longest x5 189 us: place(): picked = rows[source_row]]
    all_to_all x11 -> x2, waiting for transfers between devices: 207 us -> 59.1 us  [the longest x1 53.7 us: shards(): answer = lax.all_to_all(answer, BOTH, 0, 0, tiled=True)]
    pallas_call x0 -> x4, Pallas kernels: none -> 48.3 us  [the longest x1 32.5 us: shards(): pl.pallas_call(attend_kernel, grid=(FINE,), in_specs=[pl.BlockSpec((devic...]
    all_to_all x11 -> x2, starting transfers between devices: 67.5 us -> 20.8 us  [the longest x1 15.7 us: shards(): lax.all_to_all(scales.reshape(devices, 1, 128), BOTH, 0, 0, tiled=True)]
    dot_general x16 -> x0, matrix products: 46 us -> none  [the longest x8 29 us: attend(): jnp.dot(weights, value_block, preferred_element_type=jnp.float32)]
    all_to_all x3 -> x1, blocking collectives: 117 us -> 153 us  [shards(): message = lax.all_to_all(message, BOTH, 0, 0, tiled=True)]
    scatter x1 -> x0, local copies, waits for them, and re-layouts: 15.5 us -> none  [shards(): source = jnp.full((total,), -1, jnp.int32).at[flat].set(jnp.arange(tok_ro...]
    reduce_sum x9 -> x0, other arithmetic: 15 us -> none  [the longest x8 13.6 us: attend(): denominator = jnp.sum(unnormed, axis=1)]
  transfers between devices with their start and end apart: 11 -> 2, of which waited for: 10 -> 2; matrix products, arithmetic and copies ran while one was open for 17% -> 0% of each run, Pallas kernels for 0% -> 3%
where the time goes in v1:
time: 288 us; the launch traced here: 287 us
  blocking collectives  153 us (53%)
  waiting for transfers between devices  59.1 us (21%)
  Pallas kernels  48.3 us (17%)
  starting transfers between devices  20.8 us (7%)
  local copies, waits for them, and re-layouts  6.25 us (2%)
    all_to_all x1, blocking collectives, shards(): message = lax.all_to_all(message, BOTH, 0, 0, tiled=True)  153 us
    all_to_all x1, waiting for transfers between devices, shards(): answer = lax.all_to_all(answer, BOTH, 0, 0, tiled=True)  53.7 us
    pallas_call x1, Pallas kernels, shards(): pl.pallas_call(attend_kernel, grid=(FINE,), in_specs=[pl.BlockSpec((devic...  32.5 us
    all_to_all x1, starting transfers between devices, shards(): lax.all_to_all(scales.reshape(devices, 1, 128), BOTH, 0, 0, tiled=True)  15.7 us
    pallas_call x1, Pallas kernels, shards(): pl.pallas_call(place_kernel, grid=(heads // HALF,), in_specs=[pl.BlockSpe...  7.5 us
  transfers between devices with their start and end apart: 2, of which 2 were waited for; matrix products, arithmetic and copies ran while one was open for 0% of the time, Pallas kernels for 3%

profile of v1, /device:TPU:1, one launch (start us, length us, event | category | flops | bytes accessed | tf_op | source)
XLA Modules:
  0.0 287.4 jit_solution(30914381145091942)
XLA Ops:
  0.0 1.4 copy.10.key_scale_ref
  1.4 1.4 copy.11.value_scale_ref
  2.8 1.3 copy.16
  4.2 3.8 %shard_map.64 = (s32[16,256]{1,0:T(8,128)}, f32[256,128]{1,0:T(8,128)}) custom-call(s32[16,256]{1,0:T(8,128)} %bitcast.15, bf16[256,16]{1,0:T(8,128)(2,1)} %copy.10.key_scale_ref, bf16[256,16]{1,0:T(8,128)(2,1)} %copy.11.value_scale_ref), custom_call_target="tpu_custom_call" | custom-call | flops 100000000 | bytes 1000000 | tf_op jit(solution)/shard_map/pallas_call | solution.py:186
  8.0 15.7 %all-to-all-start.1 = ((f32[256,1,128]{2,1,0:T(1,128)}), f32[256,1,128]{2,1,0:T(1,128)S(1)}, u32[]{:S(2)}, u32[]{:S(2)}) async-start(f32[256,1,128]{2,1,0:T(1,128)} %bitcast.14), calls=%async_computation.1 | async-start | bytes 262144 | tf_op jit(solution)/shard_map/all_to_all | solution.py:194
  23.7 7.5 %shard_map.65 = bf16[16,16,96,128]{3,2,1,0:T(8,128)(2,1)} custom-call(s32[16,256]{1,0:T(8,128)} %get-tuple-element.7.slot_ref, bf16[256,16,128]{2,1,0:T(8,128)(2,1)} %q_ref.1, bf16[256,16,128]{2,1,0:T(8,128)(2,1)} %k_ref.1, bf16[256,16,128]{2,1,0:T(8,128)(2,1)} %v_ref.1), custom_call_target="tpu_custom_call" | custom-call | flops 3000000000 | bytes 9437184 | tf_op jit(solution)/shard_map/pallas_call | solution.py:198
  31.1 5.4 %all-to-all-done.1 = f32[256,1,128]{2,1,0:T(1,128)S(1)} async-done(((f32[256,1,128]{2,1,0:T(1,128)}), f32[256,1,128]{2,1,0:T(1,128)S(1)}, u32[]{:S(2)}, u32[]{:S(2)}) %all-to-all-start.1) | async-done | bytes 131104 | tf_op jit(solution)/shard_map/all_to_all | solution.py:194
  36.5 0.0 copy-start.1
  36.5 153.0 %all_to_all.15.message_ref = bf16[256,96,128]{2,1,0:T(8,128)(2,1)} all-to-all(bf16[256,96,128]{2,1,0:T(8,128)(2,1)} %bitcast.10), channel_id=1, replica_groups=mesh['outer'=16,'inner'=16] {'outer','inner'}, dimensions={0} | all-to-all | bytes 12582912 | tf_op jit(solution)/shard_map/all_to_all | solution.py:210
  189.5 0.0 copy-done.1
  189.5 0.0 copy-start.2
  189.5 32.5 %shard_map.66 = bf16[256,32,128]{2,1,0:T(8,128)(2,1)} custom-call(bf16[256,96,128]{2,1,0:T(8,128)(2,1)} %all_to_all.15.message_ref, f32[256,128]{1,0:T(8,128)} %bitcast.13), custom_call_target="tpu_custom_call" | custom-call | flops 4000000000 | bytes 8388608 | tf_op jit(solution)/shard_map/pallas_call | solution.py:214
  221.9 5.2 %all-to-all-start.2 = ((bf16[256,32,128]{2,1,0:T(8,128)(2,1)}), bf16[256,32,128]{2,1,0:T(8,128)(2,1)S(1)}, u32[]{:S(2)}, u32[]{:S(2)}) async-start(bf16[256,32,128]{2,1,0:T(8,128)(2,1)} %shard_map.66), calls=%async_computation.2 | async-start | bytes 4194304 | tf_op jit(solution)/shard_map/all_to_all | solution.py:228
  227.1 0.0 copy-done.2
  227.1 0.7 copy.12
  227.9 53.7 %all-to-all-done.2 = bf16[256,32,128]{2,1,0:T(8,128)(2,1)S(1)} async-done(((bf16[256,32,128]{2,1,0:T(8,128)(2,1)}), bf16[256,32,128]{2,1,0:T(8,128)(2,1)S(1)}, u32[]{:S(2)}, u32[]{:S(2)}) %all-to-all-start.2) | async-done | bytes 2097184 | tf_op jit(solution)/shard_map/all_to_all | solution.py:228
  281.6 0.0 copy-start
  281.6 1.3 copy-done
  282.9 4.5 %shard_map.67 = bf16[256,16,128]{2,1,0:T(8,128)(2,1)} custom-call(s32[256,16]{1,0:T(8,128)} %bitcast.12, bf16[16,16,32,128]{3,2,1,0:T(8,128)(2,1)} %bitcast.11), custom_call_target="tpu_custom_call" | custom-call | flops 1000000000 | bytes 3145728 | tf_op jit(solution)/shard_map/pallas_call | solution.py:230
Async XLA Ops:
  8.0 28.5 %all-to-all-start.1 = ((f32[256,1,128]{2,1,0:T(1,128)}), f32[256,1,128]{2,1,0:T(1,128)S(1)}, u32[]{:S(2)}, u32[]{:S(2)}) async-start(f32[256,1,128]{2,1,0:T(1,128)} %bitcast.14), calls=%async_computation.1 | async-start | bytes 262144 | tf_op jit(solution)/shard_map/all_to_all | solution.py:194
  36.5 153.0 %copy-start.1 = (f32[256,1,128]{2,1,0:T(1,128)}, f32[256,1,128]{2,1,0:T(1,128)S(1)}, u32[]{:S(2)}) copy-start(f32[256,1,128]{2,1,0:T(1,128)S(1)} %all-to-all-done.1) | copy-start | bytes 393220
  189.5 37.7 %copy-start.2 = (s32[16,256]{1,0:T(8,128)S(1)}, s32[16,256]{1,0:T(8,128)}, u32[]{:S(2)}) copy-start(s32[16,256]{1,0:T(8,128)} %get-tuple-element.7.slot_ref) | copy-start | bytes 49156
  221.9 59.6 %all-to-all-start.2 = ((bf16[256,32,128]{2,1,0:T(8,128)(2,1)}), bf16[256,32,128]{2,1,0:T(8,128)(2,1)S(1)}, u32[]{:S(2)}, u32[]{:S(2)}) async-start(bf16[256,32,128]{2,1,0:T(8,128)(2,1)} %shard_map.66), calls=%async_computation.2 | async-start | bytes 4194304 | tf_op jit(solution)/shard_map/all_to_all | solution.py:228
  281.6 1.3 copy-start

commit v2 on v1

v2 whole, which is shorter than its diff:
```python
import jax
import jax.numpy as jnp
from jax import lax
from jax.experimental import pallas as pl
from jax.experimental.pallas import tpu as pltpu
from jax.sharding import PartitionSpec as P

COARSE = 16
FINE = 8
CAP = 4
CLUSTERS = COARSE * FINE
SLOTS = CLUSTERS * CAP
CHUNK = FINE * CAP
META = 8
BOTH = ("outer", "inner")
NT = (((1,), (1,)), ((), ()))
NEG = -1e30
LOG2E = 1.4426950408889634
HALF = 8


def iota(shape, axis):
    return lax.broadcasted_iota(jnp.int32, shape, axis)


def one_hot(condition):
    return jnp.where(condition, 1.0, 0.0).astype(jnp.bfloat16)


def matmul(a, b):
    return jnp.dot(a, b, preferred_element_type=jnp.float32)


def matmul_nt(a, b):
    return lax.dot_general(a, b, NT, preferred_element_type=jnp.float32)


def swap_matrix(major, minor, unit):
    total = major * minor * unit
    row, column = iota((total, total), 0), iota((total, total), 1)
    b, a, u = row // (major * unit), (row // unit) % major, row % unit
    return one_hot(column == (a * minor + b) * unit + u)


def pack_kernel(label_ref, key_scale_ref, value_scale_ref, q_ref, slot_ref, out_ref):
    rows, heads, width = q_ref.shape
    before = one_hot(iota((rows, rows), 0) < iota((rows, rows), 1))
    for h in range(heads):
        label = label_ref[h]
        member = iota((CLUSTERS, rows), 0) == label
        count = matmul(one_hot(member), before)
        rank = jnp.sum(jnp.where(member, count, 0.0), axis=0, keepdims=True).astype(jnp.int32)
        slot = label * CAP + rank
        slot_ref[h : h + 1, :] = slot
        kinds = (
            (slot // CHUNK).astype(jnp.float32),
            (slot % CHUNK).astype(jnp.float32),
            key_scale_ref[h : h + 1, :].astype(jnp.float32),
            value_scale_ref[h : h + 1, :].astype(jnp.float32),
        )
        meta = jnp.concatenate(
            [kind[:, half : half + width] for kind in kinds for half in range(0, rows, width)],
            axis=0,
        )
        out_ref[h, rows : rows + META, :] = meta.astype(jnp.bfloat16)
    group = 256 // heads
    swap = swap_matrix(group, heads, 1)
    for g in range(rows // group):
        block = q_ref[g * group : (g + 1) * group].reshape(256, width)
        turned = matmul(swap, block).astype(jnp.bfloat16)
        out_ref[:, g * group : (g + 1) * group, :] = turned.reshape(heads, group, width)


def place_kernel(slot_ref, k_ref, v_ref, out_ref, by_head):
    step = pl.program_id(0)
    rows, _, width = k_ref.shape
    group = 256 // HALF
    swap = swap_matrix(group, HALF, 1)
    for g in range(rows // group):
        here = slice(g * group, (g + 1) * group)
        block = jnp.concatenate(
            [k_ref[here].reshape(256, width), v_ref[here].reshape(256, width)], axis=1
        )
        turned = matmul(swap, block).astype(jnp.bfloat16)
        by_head[:, here, :] = turned.reshape(HALF, group, 2 * width)
    for h in range(HALF):
        slot = slot_ref[pl.ds(step * HALF + h, 1), :]
        pick = one_hot(iota((SLOTS, rows), 0) == slot)
        placed = matmul(pick, by_head[h]).astype(jnp.bfloat16)
        out_ref[:, h] = placed.reshape(COARSE, CHUNK, 2 * width)


def sort_kernel(me_ref, in_ref, *refs):
    outs, (table, scales) = refs[:COARSE], refs[COARSE:]
    me = me_ref[0]
    blocks, rows, width = in_ref.shape
    rows = rows - META
    batch = 256 // CHUNK
    for s in range(blocks):
        meta = in_ref[s, rows : rows + META, :].astype(jnp.float32)
        coarse, here, key_scale, value_scale = (
            jnp.concatenate([meta[2 * n : 2 * n + 1], meta[2 * n + 1 : 2 * n + 2]], axis=1)
            for n in range(4)
        )
        owner = coarse.astype(jnp.int32) ^ me
        here = here.astype(jnp.int32)
        pick = one_hot(iota((SLOTS, rows), 0) == owner * CHUNK + here)
        placed = matmul(pick, in_ref[s, :rows, :]).astype(jnp.bfloat16)
        table[:, s] = placed.reshape(COARSE, CHUNK, width)
        mine = iota((CHUNK, rows), 0) == here
        both = jnp.concatenate(
            [
                jnp.where(mine, key_scale, 0.0),
                jnp.where(mine, value_scale, 0.0),
                jnp.zeros((width - 2 * CHUNK, rows), jnp.float32),
            ],
            axis=0,
        ).astype(jnp.bfloat16)
        scales[pl.ds(s, COARSE, stride=blocks), :] = matmul_nt(
            one_hot(iota((COARSE, rows), 0) == owner), both
        )
    swap = swap_matrix(batch, FINE, CAP)
    unit = batch * CAP
    for d, out_ref in enumerate(outs):
        block = jnp.concatenate(
            [
                table[d, b * batch : (b + 1) * batch].reshape(256, width)
                for b in range(blocks // batch)
            ],
            axis=1,
        )
        turned = matmul(swap, block).astype(jnp.bfloat16)
        for f in range(FINE):
            for b in range(blocks // batch):
                at = f * blocks * CAP + b * unit
                out_ref[at : at + unit, :] = turned[
                    f * unit : (f + 1) * unit, b * width : (b + 1) * width
                ]
        out_ref[FINE * blocks * CAP :, :] = scales[d * blocks : (d + 1) * blocks, :].astype(
            jnp.bfloat16
        )


def attend_kernel(me_ref, message_ref, *refs):
    parts, out_ref = refs[:COARSE], refs[COARSE]
    qs, kvs, os, scale_rows, scales = refs[COARSE + 1 :]
    f = pl.program_id(0)
    sources, _, width = message_ref.shape
    width = width // 2
    blocks = sources // COARSE
    total = sources * CAP
    batch = 256 // CHUNK
    unit = batch * CAP
    slab = blocks * CAP

    @pl.when(f == 0)
    def _():
        me = me_ref[0]
        for d, part in enumerate(parts):
            source = me ^ d
            qs[:, pl.ds(pl.multiple_of(source * slab, slab), slab), :] = part[
                : FINE * slab, :
            ].reshape(FINE, slab, width)
            scale_rows[pl.ds(pl.multiple_of(source * blocks, blocks), blocks), :] = part[
                FINE * slab :, :
            ]
        swap = swap_matrix(batch, FINE, CAP)

        def turn(g, carry):
            block = message_ref[pl.ds(g * batch, batch)].reshape(256, 2 * width)
            turned = matmul(swap, block).astype(jnp.bfloat16)
            kvs[:, pl.ds(pl.multiple_of(g * unit, unit), unit), :] = turned.reshape(
                FINE, unit, 2 * width
            )
            return carry

        lax.fori_loop(0, sources // batch, turn, 0, unroll=8)

        spread = one_hot(iota((total, sources), 0) // CAP == iota((total, sources), 1))
        table = matmul(spread, scale_rows[...])
        lane, row = iota((total, 128), 1), iota((total, 128), 0)
        table = jnp.where(lane % CAP == row % CAP, table, 0.0).astype(jnp.bfloat16)
        gather = one_hot(iota((2 * FINE, 128), 0) == iota((2 * FINE, 128), 1) // CAP)
        scales[...] = matmul_nt(gather, table)

    key_scale = scales[pl.ds(f, 1), :]
    value_scale = scales[pl.ds(FINE + f, 1), :]
    factor = key_scale * (width**-0.5 * LOG2E)
    bias = jnp.where(key_scale > 0.0, 0.0, NEG)
    tile = 256
    ahead = iota((tile, tile), 1) > iota((tile, tile), 0)
    for t in range(total // tile):
        here = slice(t * tile, (t + 1) * tile)
        query = qs[f, here, :]
        pieces = []
        for u in range(t + 1):
            there = slice(u * tile, (u + 1) * tile)
            score = matmul_nt(query, kvs[f, there, :width])
            score = score * factor[:, there] + bias[:, there]
            if u == t:
                score = jnp.where(ahead, NEG, score)
            pieces.append(score)
        highest = pieces[0]
        for piece in pieces[1:]:
            highest = jnp.maximum(highest, piece)
        highest = jnp.max(highest, axis=1, keepdims=True)
        below, result = None, None
        for u, piece in enumerate(pieces):
            there = slice(u * tile, (u + 1) * tile)
            unnormed = jnp.exp2(piece - highest)
            weights = (unnormed * value_scale[:, there]).astype(jnp.bfloat16)
            term = matmul(weights, kvs[f, there, width:])
            below = unnormed if below is None else below + unnormed
            result = term if result is None else result + term
        below = jnp.sum(below, axis=1, keepdims=True)
        os[f, here, :] = (result / below).astype(jnp.bfloat16)

    @pl.when(f == FINE - 1)
    def _():
        swap = swap_matrix(FINE, batch, CAP)

        def turn(g, carry):
            block = os[:, pl.ds(pl.multiple_of(g * unit, unit), unit), :].reshape(256, width)
            turned = matmul(swap, block).astype(jnp.bfloat16)
            out_ref[pl.ds(g * batch, batch)] = turned.reshape(batch, CHUNK, width)
            return carry

        lax.fori_loop(0, sources // batch, turn, 0, unroll=8)


def unplace_kernel(slot_ref, in_ref, out_ref, by_head):
    step = pl.program_id(0)
    rows = slot_ref.shape[0]
    width = in_ref.shape[3]
    group = 256 // HALF
    swap = swap_matrix(HALF, group, 1)
    lane = iota(slot_ref.shape, 1)
    for h in range(HALF):
        slot = jnp.sum(
            jnp.where(lane == step * HALF + h, slot_ref[...], 0), axis=1, keepdims=True
        )
        pick = one_hot(iota((rows, SLOTS), 1) == slot)
        by_head[h] = matmul(pick, in_ref[:, h].reshape(SLOTS, width)).astype(jnp.bfloat16)
    for g in range(rows // group):
        block = by_head[:, g * group : (g + 1) * group, :].reshape(256, width)
        out_ref[g * group : (g + 1) * group] = (
            matmul(swap, block).astype(jnp.bfloat16).reshape(group, HALF, width)
        )


def shards(queries, key_rows, value_rows, key_scale, value_scale, cluster_label):
    rows, heads, width = queries.shape
    outer, inner = lax.axis_size("outer"), lax.axis_size("inner")
    devices = outer * inner
    bf16, f32 = jnp.bfloat16, jnp.float32
    me = lax.axis_index("outer").astype(jnp.int32).reshape(1)
    scalar = pl.BlockSpec(memory_space=pltpu.SMEM)

    slots, packed = pl.pallas_call(
        pack_kernel,
        out_shape=(
            jax.ShapeDtypeStruct((heads, rows), jnp.int32),
            jax.ShapeDtypeStruct((heads, rows + META, width), bf16),
        ),
        cost_estimate=pl.CostEstimate(flops=10**9, bytes_accessed=2**21, transcendentals=0),
    )(jnp.swapaxes(cluster_label, 1, 2), key_scale.T, value_scale.T, queries)
    packed = lax.all_to_all(packed, "inner", 0, 0, tiled=True)

    tokens = pl.BlockSpec((rows, HALF, width), lambda i: (0, i, 0))
    message = pl.pallas_call(
        place_kernel,
        grid=(heads // HALF,),
        in_specs=[pl.BlockSpec((heads, rows), lambda i: (0, 0)), tokens, tokens],
        out_specs=pl.BlockSpec((COARSE, HALF, CHUNK, 2 * width), lambda i: (0, i, 0, 0)),
        out_shape=jax.ShapeDtypeStruct((COARSE, heads, CHUNK, 2 * width), bf16),
        scratch_shapes=[pltpu.VMEM((HALF, rows, 2 * width), bf16)],
        cost_estimate=pl.CostEstimate(
            flops=3 * 10**9, bytes_accessed=6 * 2**20, transcendentals=0
        ),
    )(slots, key_rows, value_rows)
    message = message.reshape(devices, CHUNK, 2 * width)
    message = lax.all_to_all(message, BOTH, 0, 0, tiled=True)

    part_rows = FINE * inner * CAP + inner
    parts = pl.pallas_call(
        sort_kernel,
        in_specs=[scalar, pl.BlockSpec(memory_space=pltpu.VMEM)],
        out_shape=[jax.ShapeDtypeStruct((part_rows, width), bf16)] * COARSE,
        scratch_shapes=[
            pltpu.VMEM((COARSE, inner, CHUNK, width), bf16),
            pltpu.VMEM((COARSE * inner, width), f32),
        ],
        cost_estimate=pl.CostEstimate(
            flops=2 * 10**9, bytes_accessed=3 * 2**20, transcendentals=0
        ),
    )(me, packed)
    parts = [parts[0]] + [
        lax.ppermute(parts[d], "outer", [(n, n ^ d) for n in range(outer)])
        for d in range(1, outer)
    ]

    total = devices * CAP
    answer = pl.pallas_call(
        attend_kernel,
        grid=(FINE,),
        in_specs=[scalar, pl.BlockSpec((devices, CHUNK, 2 * width), lambda i: (0, 0, 0))]
        + [pl.BlockSpec((part_rows, width), lambda i: (0, 0))] * COARSE,
        out_specs=pl.BlockSpec((devices, CHUNK, width), lambda i: (0, 0, 0)),
        out_shape=jax.ShapeDtypeStruct((devices, CHUNK, width), bf16),
        scratch_shapes=[
            pltpu.VMEM((FINE, total, width), bf16),
            pltpu.VMEM((FINE, total, 2 * width), bf16),
            pltpu.VMEM((FINE, total, width), bf16),
            pltpu.VMEM((devices, width), bf16),
            pltpu.VMEM((2 * FINE, total), f32),
        ],
        cost_estimate=pl.CostEstimate(
            flops=4 * 10**9, bytes_accessed=8 * 2**20, transcendentals=5 * 10**6
        ),
    )(me, message, *parts)
    answer = lax.all_to_all(answer, BOTH, 0, 0, tiled=True)

    return pl.pallas_call(
        unplace_kernel,
        grid=(heads // HALF,),
        in_specs=[
            pl.BlockSpec((rows, heads), lambda i: (0, 0)),
            pl.BlockSpec((COARSE, HALF, CHUNK, width), lambda i: (0, i, 0, 0)),
        ],
        out_specs=pl.BlockSpec((rows, HALF, width), lambda i: (0, i, 0)),
        out_shape=jax.ShapeDtypeStruct((rows, heads, width), bf16),
        scratch_shapes=[pltpu.VMEM((HALF, rows, width), bf16)],
        cost_estimate=pl.CostEstimate(
            flops=10**9, bytes_accessed=3 * 2**20, transcendentals=0
        ),
    )(slots.T, answer.reshape(COARSE, heads, CHUNK, width))


def solution(mesh):
    placed = (
        P(BOTH, None, None),
        P(BOTH, None, None),
        P(BOTH, None, None),
        P(BOTH, None),
        P(BOTH, None),
        P(None, BOTH, None),
    )
    return jax.shard_map(
        shards,
        mesh=mesh,
        in_specs=placed,
        out_specs=P(BOTH, None, None),
        check_vma=False,
    )
```

time: 288 us -> 241 us (0.84)
  blocking collectives: 153 us -> 0 us
  waiting for transfers between devices: 59.1 us -> 139 us
  starting transfers between devices: 20.8 us -> 58.4 us
  Pallas kernels: 48.3 us -> 39.8 us
  local copies, waits for them, and re-layouts: 6.25 us -> 3.16 us
    all_to_all x1 -> x0, blocking collectives: 153 us -> none  [shards(): message = lax.all_to_all(message, BOTH, 0, 0, tiled=True)]
    ppermute x0 -> x15, waiting for transfers between devices: none -> 48.3 us  [shards(): lax.ppermute(parts[d], 'outer', [(n, n ^ d) for n in range(outer)])]
    ppermute x0 -> x15, starting transfers between devices: none -> 32.9 us  [shards(): lax.ppermute(parts[d], 'outer', [(n, n ^ d) for n in range(outer)])]
    all_to_all x1 -> x2, waiting for transfers between devices: 5.36 us -> 37.3 us  [the longest x1 23.9 us: shards(): packed = lax.all_to_all(packed, 'inner', 0, 0, tiled=True)]
    pallas_call x2 -> x3, Pallas kernels: 36.3 us -> 30.5 us  [the longest x1 22.8 us: shards(): pl.pallas_call(attend_kernel, grid=(FINE,), in_specs=[scalar, pl.BlockSpe...]
    all_to_all x1 -> x2, starting transfers between devices: 15.7 us -> 20.2 us  [the longest x1 10.2 us: shards(): message = lax.all_to_all(message, BOTH, 0, 0, tiled=True)]
    unnamed x9 -> x36, local copies, waits for them, and re-layouts: 5.51 us -> 2.41 us
  transfers between devices with their start and end apart: 2 -> 18, of which waited for: 2 -> 12; matrix products, arithmetic and copies ran while one was open for 0% -> 0% of each run, Pallas kernels for 3% -> 4%
where the time goes in v2:
time: 241 us; the launch traced here: 240 us
  waiting for transfers between devices  139 us (58%)
  starting transfers between devices  58.4 us (24%)
  Pallas kernels  39.8 us (17%)
  local copies, waits for them, and re-layouts  3.16 us (1%)
    all_to_all x1, waiting for transfers between devices, shards(): answer = lax.all_to_all(answer, BOTH, 0, 0, tiled=True)  53.4 us
    ppermute x15, waiting for transfers between devices, shards(): lax.ppermute(parts[d], 'outer', [(n, n ^ d) for n in range(outer)])  48.3 us
    ppermute x15, starting transfers between devices, shards(): lax.ppermute(parts[d], 'outer', [(n, n ^ d) for n in range(outer)])  32.9 us
    all_to_all x1, waiting for transfers between devices, shards(): packed = lax.all_to_all(packed, 'inner', 0, 0, tiled=True)  23.9 us
    pallas_call x1, Pallas kernels, shards(): pl.pallas_call(attend_kernel, grid=(FINE,), in_specs=[scalar, pl.BlockSpe...  22.8 us
    all_to_all x1, waiting for transfers between devices, shards(): message = lax.all_to_all(message, BOTH, 0, 0, tiled=True)  13.5 us
    all_to_all x1, starting transfers between devices, shards(): message = lax.all_to_all(message, BOTH, 0, 0, tiled=True)  10.2 us
    all_to_all x1, starting transfers between devices, shards(): packed = lax.all_to_all(packed, 'inner', 0, 0, tiled=True)  9.98 us
  transfers between devices with their start and end apart: 18, of which 12 were waited for; matrix products, arithmetic and copies ran while one was open for 0% of the time, Pallas kernels for 4%

profile of v2, /device:TPU:1, one launch (start us, length us, event | category | flops | bytes accessed | tf_op | source)
XLA Modules:
  0.0 240.5 jit_solution(13653076957880966793)
XLA Ops:
  0.0 3.6 %shard_map.64 = (s32[16,256]{1,0:T(8,128)}, bf16[16,264,128]{2,1,0:T(8,128)(2,1)}) custom-call(s32[16,1,256]{2,1,0:T(1,128)} %bitcast.10, bf16[16,256]{1,0:T(8,128)(2,1)} %bitcast.11, bf16[16,256]{1,0:T(8,128)(2,1)} %bitcast.12, bf16[256,16,128]{2,1,0:T(8,128)(2,1)} %q_ref.1), custom_call_target="tpu_custom_call" | custom-call | flops 1000000000 | bytes 2097152 | tf_op jit(solution)/shard_map/pallas_call | solution.py:259
  3.6 10.0 %all-to-all-start.1 = ((bf16[16,264,128]{2,1,0:T(8,128)(2,1)}), bf16[16,264,128]{2,1,0:T(8,128)(2,1)S(1)}, u32[]{:S(2)}, u32[]{:S(2)}) async-start(bf16[16,264,128]{2,1,0:T(8,128)(2,1)} %get-tuple-element.24), calls=%async_computation.1 | async-start | bytes 2162688 | tf_op jit(solution)/shard_map/all_to_all | solution.py:267
  13.6 4.7 %shard_map.65 = bf16[16,16,32,256]{3,2,1,0:T(8,128)(2,1)} custom-call(s32[16,256]{1,0:T(8,128)} %get-tuple-element.23.slot_ref, bf16[256,16,128]{2,1,0:T(8,128)(2,1)} %k_ref.1, bf16[256,16,128]{2,1,0:T(8,128)(2,1)} %v_ref.1), custom_call_target="tpu_custom_call" | custom-call | flops 3000000000 | bytes 6291456 | tf_op jit(solution)/shard_map/pallas_call | solution.py:270
  18.3 23.9 %all-to-all-done.1.in_ref = bf16[16,264,128]{2,1,0:T(8,128)(2,1)S(1)} async-done(((bf16[16,264,128]{2,1,0:T(8,128)(2,1)}), bf16[16,264,128]{2,1,0:T(8,128)(2,1)S(1)}, u32[]{:S(2)}, u32[]{:S(2)}) %all-to-all-start.1) | async-done | bytes 1081376 | tf_op jit(solution)/shard_map/all_to_all | solution.py:267
  42.2 0.0 copy-start.1
  42.2 1.0 copy-done.1
  43.2 10.2 %all-to-all-start = ((bf16[256,32,256]{2,1,0:T(8,128)(2,1)}), bf16[256,32,256]{2,1,0:T(8,128)(2,1)}, u32[]{:S(2)}, u32[]{:S(2)}) async-start(bf16[256,32,256]{2,1,0:T(8,128)(2,1)} %bitcast.7), calls=%async_computation | async-start | bytes 8388608 | tf_op jit(solution)/shard_map/all_to_all | solution.py:282
  53.4 4.2 %shard_map.66 = (bf16[528,128]{1,0:T(8,128)(2,1)}, bf16[528,128]{1,0:T(8,128)(2,1)}, bf16[528,128]{1,0:T(8,128)(2,1)}, bf16[528,128]{1,0:T(8,128)(2,1)}, bf16[52...) custom-call(s32[1]{0:T(128)} %bitcast.4.me_ref, ...), custom_call_target="tpu_custom_call" | custom-call | flops 2000000000 | bytes 3145728 | tf_op jit(solution)/shard_map/pallas_call | solution.py:285
  57.6 1.4 collective-permute-start
  59.0 2.4 %collective-permute-start.1 = (bf16[528,128]{1,0:T(8,128)(2,1)}, bf16[528,128]{1,0:T(8,128)(2,1)S(1)}, u32[]{:S(2)}, u32[]{:S(2)}) collective-permute-start(bf16[528,128]{1,0:T(8,128)(2,1)} %get-tuple-element.27), channel_id=1, source_target_pairs={{0,32},{16,48},{32,0},{48,16},{64,96},{80,112},{96,64},{112,80},{1... | collective-permute-start | bytes 405512 | tf_op jit(solution)/shard_map/ppermute | solution.py:298
  61.4 0.0 collective-permute-start.2
  61.4 1.4 collective-permute-start.3
  62.8 0.0 collective-permute-start.4
  62.8 5.5 %collective-permute-done.refs_1_ = bf16[528,128]{1,0:T(8,128)(2,1)S(1)} collective-permute-done((bf16[528,128]{1,0:T(8,128)(2,1)}, bf16[528,128]{1,0:T(8,128)(2,1)S(1)}, u32[]{:S(2)}, u32[]{:S(2)}) %collective-permute-start) | collective-permute-done | bytes 135200 | tf_op jit(solution)/shard_map/ppermute | solution.py:298
  68.3 0.0 copy-start.3
  68.3 1.5 collective-permute-start.5
  69.8 16.0 %collective-permute-done.1.refs_2_ = bf16[528,128]{1,0:T(8,128)(2,1)S(1)} collective-permute-done((bf16[528,128]{1,0:T(8,128)(2,1)}, bf16[528,128]{1,0:T(8,128)(2,1)S(1)}, u32[]{:S(2)}, u32[]{:S(2)}) %collective-permute-start.1) | collective-permute-done | bytes 135200 | tf_op jit(solution)/shard_map/ppermute | solution.py:298
  85.8 0.0 copy-start.4
  85.8 0.0 collective-permute-start.6
  85.8 0.0 collective-permute-done.2.refs_3_
  85.8 0.0 copy-start.5
  85.8 1.8 collective-permute-start.7
  87.6 0.0 collective-permute-done.3.refs_4_
  87.6 0.5 collective-permute-start.8
  88.1 0.0 collective-permute-done.4.refs_5_
  88.1 5.7 %collective-permute-start.9 = (bf16[528,128]{1,0:T(8,128)(2,1)}, bf16[528,128]{1,0:T(8,128)(2,1)S(1)}, u32[]{:S(2)}, u32[]{:S(2)}) collective-permute-start(bf16[528,128]{1,0:T(8,128)(2,1)} %get-tuple-element.35), channel_id=1, source_target_pairs={{0,160},{16,176},{32,128},{48,144},{64,224},{80,240},{96,192},{112... | collective-permute-start | bytes 405512 | tf_op jit(solution)/shard_map/ppermute | solution.py:298
  93.7 0.0 collective-permute-done.5.refs_6_
  93.7 1.1 collective-permute-start.10
  94.9 0.8 collective-permute-done.6.refs_7_
  95.7 0.5 collective-permute-start.11
  96.1 2.4 collective-permute-done.7.refs_8_
  98.6 2.9 %collective-permute-start.12 = (bf16[528,128]{1,0:T(8,128)(2,1)}, bf16[528,128]{1,0:T(8,128)(2,1)S(1)}, u32[]{:S(2)}, u32[]{:S(2)}) collective-permute-start(bf16[528,128]{1,0:T(8,128)(2,1)} %get-tuple-element.38), channel_id=1, source_target_pairs={{0,208},{16,192},{32,240},{48,224},{64,144},{80,128},{96,176},{112... | collective-permute-start | bytes 405512 | tf_op jit(solution)/shard_map/ppermute | solution.py:298
  101.4 0.0 collective-permute-done.8.refs_9_
  101.5 7.4 %collective-permute-start.13 = (bf16[528,128]{1,0:T(8,128)(2,1)}, bf16[528,128]{1,0:T(8,128)(2,1)S(1)}, u32[]{:S(2)}, u32[]{:S(2)}) collective-permute-start(bf16[528,128]{1,0:T(8,128)(2,1)} %get-tuple-element.39), channel_id=1, source_target_pairs={{0,224},{16,240},{32,192},{48,208},{64,160},{80,176},{96,128},{112... | collective-permute-start | bytes 405512 | tf_op jit(solution)/shard_map/ppermute | solution.py:298
  108.9 0.0 collective-permute-done.9.refs_10_
  108.9 6.3 %collective-permute-start.14 = (bf16[528,128]{1,0:T(8,128)(2,1)}, bf16[528,128]{1,0:T(8,128)(2,1)S(1)}, u32[]{:S(2)}, u32[]{:S(2)}) collective-permute-start(bf16[528,128]{1,0:T(8,128)(2,1)} %get-tuple-element.40), channel_id=1, source_target_pairs={{0,240},{16,224},{32,208},{48,192},{64,176},{80,160},{96,144},{112... | collective-permute-start | bytes 405512 | tf_op jit(solution)/shard_map/ppermute | solution.py:298
  115.2 0.8 collective-permute-done.10.refs_11_
  116.0 4.6 %collective-permute-done.11.refs_12_ = bf16[528,128]{1,0:T(8,128)(2,1)S(1)} collective-permute-done((bf16[528,128]{1,0:T(8,128)(2,1)}, bf16[528,128]{1,0:T(8,128)(2,1)S(1)}, u32[]{:S(2)}, u32[]{:S(2)}) %collective-permute-start.11) | collective-permute-done | bytes 135200 | tf_op jit(solution)/shard_map/ppermute | solution.py:298
  120.5 3.5 %collective-permute-done.12.refs_13_ = bf16[528,128]{1,0:T(8,128)(2,1)S(1)} collective-permute-done((bf16[528,128]{1,0:T(8,128)(2,1)}, bf16[528,128]{1,0:T(8,128)(2,1)S(1)}, u32[]{:S(2)}, u32[]{:S(2)}) %collective-permute-start.12) | collective-permute-done | bytes 135200 | tf_op jit(solution)/shard_map/ppermute | solution.py:298
  124.0 6.4 %collective-permute-done.13.refs_14_ = bf16[528,128]{1,0:T(8,128)(2,1)S(1)} collective-permute-done((bf16[528,128]{1,0:T(8,128)(2,1)}, bf16[528,128]{1,0:T(8,128)(2,1)S(1)}, u32[]{:S(2)}, u32[]{:S(2)}) %collective-permute-start.13) | collective-permute-done | bytes 135200 | tf_op jit(solution)/shard_map/ppermute | solution.py:298
  130.4 8.3 %collective-permute-done.14.refs_15_ = bf16[528,128]{1,0:T(8,128)(2,1)S(1)} collective-permute-done((bf16[528,128]{1,0:T(8,128)(2,1)}, bf16[528,128]{1,0:T(8,128)(2,1)S(1)}, u32[]{:S(2)}, u32[]{:S(2)}) %collective-permute-start.14) | collective-permute-done | bytes 135200 | tf_op jit(solution)/shard_map/ppermute | solution.py:298
  138.8 13.5 %all-to-all-done.message_ref = bf16[256,32,256]{2,1,0:T(8,128)(2,1)} async-done(((bf16[256,32,256]{2,1,0:T(8,128)(2,1)}), bf16[256,32,256]{2,1,0:T(8,128)(2,1)}, u32[]{:S(2)}, u32[]{:S(2)}) %all-to-all-start) | async-done | bytes 4194336 | tf_op jit(solution)/shard_map/all_to_all | solution.py:282
  152.2 0.0 copy-done.3
  152.2 0.0 copy-done.4
  152.2 0.0 copy-done.5
  152.2 0.0 copy-done.6
  152.3 0.0 copy-done.7
  152.3 0.0 copy-done.8
  152.3 0.0 copy-done.9
  152.3 0.0 copy-done.10
  152.3 0.0 copy-done.11
  152.3 0.0 copy-done.12
  152.3 0.0 copy-done.13
  152.3 0.0 copy-done.14
  152.3 0.0 copy-done.15
  152.3 0.0 copy-done.16
  152.4 0.0 copy-done.17
  152.4 22.8 %shard_map.67 = bf16[256,32,128]{2,1,0:T(8,128)(2,1)} custom-call(s32[1]{0:T(128)} %bitcast.4.me_ref, bf16[256,32,256]{2,1,0:T(8,128)(2,1)} %all-to-all-done.message_ref, bf16[528,128]{1,0:T(8,128)(2,1)} %get-tuple-element.25.refs_0_, bf16[528,128]{1,0:T(8,128)(2,1)} %copy-done.3, bf16[528,128]{1,0:T(8,128)(2,1)} %copy-done.4, bf16[528,128]{1,0:T(8,128)(2,1)} %copy-done.5, ...), custom_call_target="tpu_custom_call" | custom-call | flops 4000000000 | bytes 8388608 | tf_op jit(solution)/shard_map/pallas_call | solution.py:303
  175.2 5.3 %all-to-all-start.2 = ((bf16[256,32,128]{2,1,0:T(8,128)(2,1)}), bf16[256,32,128]{2,1,0:T(8,128)(2,1)S(1)}, u32[]{:S(2)}, u32[]{:S(2)}) async-start(bf16[256,32,128]{2,1,0:T(8,128)(2,1)} %shard_map.67), calls=%async_computation.2 | async-start | bytes 4194304 | tf_op jit(solution)/shard_map/all_to_all | solution.py:321
  180.5 0.0 copy-done.2
  180.5 0.7 copy.7
  181.2 53.4 %all-to-all-done.2 = bf16[256,32,128]{2,1,0:T(8,128)(2,1)S(1)} async-done(((bf16[256,32,128]{2,1,0:T(8,128)(2,1)}), bf16[256,32,128]{2,1,0:T(8,128)(2,1)S(1)}, u32[]{:S(2)}, u32[]{:S(2)}) %all-to-all-start.2) | async-done | bytes 2097184 | tf_op jit(solution)/shard_map/all_to_all | solution.py:321
  234.6 1.4 copy-done
  236.0 4.5 %shard_map.68 = bf16[256,16,128]{2,1,0:T(8,128)(2,1)} custom-call(s32[256,16]{1,0:T(8,128)} %bitcast.9, bf16[16,16,32,128]{3,2,1,0:T(8,128)(2,1)} %bitcast.8), custom_call_target="tpu_custom_call" | custom-call | flops 1000000000 | bytes 3145728 | tf_op jit(solution)/shard_map/pallas_call | solution.py:323
  (14 shorter events, 0.0 us)
Async XLA Ops:
  3.6 38.6 %all-to-all-start.1 = ((bf16[16,264,128]{2,1,0:T(8,128)(2,1)}), bf16[16,264,128]{2,1,0:T(8,128)(2,1)S(1)}, u32[]{:S(2)}, u32[]{:S(2)}) async-start(bf16[16,264,128]{2,1,0:T(8,128)(2,1)} %get-tuple-element.24), calls=%async_computation.1 | async-start | bytes 2162688 | tf_op jit(solution)/shard_map/all_to_all | solution.py:267
  42.2 1.0 copy-start.1
  43.2 109.1 %all-to-all-start = ((bf16[256,32,256]{2,1,0:T(8,128)(2,1)}), bf16[256,32,256]{2,1,0:T(8,128)(2,1)}, u32[]{:S(2)}, u32[]{:S(2)}) async-start(bf16[256,32,256]{2,1,0:T(8,128)(2,1)} %bitcast.7), calls=%async_computation | async-start | bytes 8388608 | tf_op jit(solution)/shard_map/all_to_all | solution.py:282
  57.6 10.8 %collective-permute-start = (bf16[528,128]{1,0:T(8,128)(2,1)}, bf16[528,128]{1,0:T(8,128)(2,1)S(1)}, u32[]{:S(2)}, u32[]{:S(2)}) collective-permute-start(bf16[528,128]{1,0:T(8,128)(2,1)} %get-tuple-element.26), channel_id=1, source_target_pairs={{0,16},{16,0},{32,48},{48,32},{64,80},{80,64},{96,112},{112,96},{1... | collective-permute-start | bytes 405512 | tf_op jit(solution)/shard_map/ppermute | solution.py:298
  59.0 26.8 %collective-permute-start.1 = (bf16[528,128]{1,0:T(8,128)(2,1)}, bf16[528,128]{1,0:T(8,128)(2,1)S(1)}, u32[]{:S(2)}, u32[]{:S(2)}) collective-permute-start(bf16[528,128]{1,0:T(8,128)(2,1)} %get-tuple-element.27), channel_id=1, source_target_pairs={{0,32},{16,48},{32,0},{48,16},{64,96},{80,112},{96,64},{112,80},{1... | collective-permute-start | bytes 405512 | tf_op jit(solution)/shard_map/ppermute | solution.py:298
  61.4 24.4 %collective-permute-start.2 = (bf16[528,128]{1,0:T(8,128)(2,1)}, bf16[528,128]{1,0:T(8,128)(2,1)S(1)}, u32[]{:S(2)}, u32[]{:S(2)}) collective-permute-start(bf16[528,128]{1,0:T(8,128)(2,1)} %get-tuple-element.28), channel_id=1, source_target_pairs={{0,48},{16,32},{32,16},{48,0},{64,112},{80,96},{96,80},{112,64},{1... | collective-permute-start | bytes 405512 | tf_op jit(solution)/shard_map/ppermute | solution.py:298
  61.4 26.2 %collective-permute-start.3 = (bf16[528,128]{1,0:T(8,128)(2,1)}, bf16[528,128]{1,0:T(8,128)(2,1)S(1)}, u32[]{:S(2)}, u32[]{:S(2)}) collective-permute-start(bf16[528,128]{1,0:T(8,128)(2,1)} %get-tuple-element.29), channel_id=1, source_target_pairs={{0,64},{16,80},{32,96},{48,112},{64,0},{80,16},{96,32},{112,48},{1... | collective-permute-start | bytes 405512 | tf_op jit(solution)/shard_map/ppermute | solution.py:298
  62.8 25.3 %collective-permute-start.4 = (bf16[528,128]{1,0:T(8,128)(2,1)}, bf16[528,128]{1,0:T(8,128)(2,1)S(1)}, u32[]{:S(2)}, u32[]{:S(2)}) collective-permute-start(bf16[528,128]{1,0:T(8,128)(2,1)} %get-tuple-element.30), channel_id=1, source_target_pairs={{0,80},{16,64},{32,112},{48,96},{64,16},{80,0},{96,48},{112,32},{1... | collective-permute-start | bytes 405512 | tf_op jit(solution)/shard_map/ppermute | solution.py:298
  68.3 83.9 %copy-start.3 = (bf16[528,128]{1,0:T(8,128)(2,1)}, bf16[528,128]{1,0:T(8,128)(2,1)S(1)}, u32[]{:S(2)}) copy-start(bf16[528,128]{1,0:T(8,128)(2,1)S(1)} %collective-permute-done.refs_1_) | copy-start | bytes 405508
  68.3 25.4 %collective-permute-start.5 = (bf16[528,128]{1,0:T(8,128)(2,1)}, bf16[528,128]{1,0:T(8,128)(2,1)S(1)}, u32[]{:S(2)}, u32[]{:S(2)}) collective-permute-start(bf16[528,128]{1,0:T(8,128)(2,1)} %get-tuple-element.31), channel_id=1, source_target_pairs={{0,96},{16,112},{32,64},{48,80},{64,32},{80,48},{96,0},{112,16},{1... | collective-permute-start | bytes 405512 | tf_op jit(solution)/shard_map/ppermute | solution.py:298
  85.8 66.5 %copy-start.4 = (bf16[528,128]{1,0:T(8,128)(2,1)}, bf16[528,128]{1,0:T(8,128)(2,1)S(1)}, u32[]{:S(2)}) copy-start(bf16[528,128]{1,0:T(8,128)(2,1)S(1)} %collective-permute-done.1.refs_2_) | copy-start | bytes 405508
  85.8 9.9 %collective-permute-start.6 = (bf16[528,128]{1,0:T(8,128)(2,1)}, bf16[528,128]{1,0:T(8,128)(2,1)S(1)}, u32[]{:S(2)}, u32[]{:S(2)}) collective-permute-start(bf16[528,128]{1,0:T(8,128)(2,1)} %get-tuple-element.32), channel_id=1, source_target_pairs={{0,112},{16,96},{32,80},{48,64},{64,48},{80,32},{96,16},{112,0},{1... | collective-permute-start | bytes 405512 | tf_op jit(solution)/shard_map/ppermute | solution.py:298
  85.8 66.4 %copy-start.5 = (bf16[528,128]{1,0:T(8,128)(2,1)}, bf16[528,128]{1,0:T(8,128)(2,1)S(1)}, u32[]{:S(2)}) copy-start(bf16[528,128]{1,0:T(8,128)(2,1)S(1)} %collective-permute-done.2.refs_3_) | copy-start | bytes 405508
  85.8 12.7 %collective-permute-start.7 = (bf16[528,128]{1,0:T(8,128)(2,1)}, bf16[528,128]{1,0:T(8,128)(2,1)S(1)}, u32[]{:S(2)}, u32[]{:S(2)}) collective-permute-start(bf16[528,128]{1,0:T(8,128)(2,1)} %get-tuple-element.33), channel_id=1, source_target_pairs={{0,128},{16,144},{32,160},{48,176},{64,192},{80,208},{96,224},{112... | collective-permute-start | bytes 405512 | tf_op jit(solution)/shard_map/ppermute | solution.py:298
  87.6 64.6 %copy-start.6 = (bf16[528,128]{1,0:T(8,128)(2,1)}, bf16[528,128]{1,0:T(8,128)(2,1)S(1)}, u32[]{:S(2)}) copy-start(bf16[528,128]{1,0:T(8,128)(2,1)S(1)} %collective-permute-done.3.refs_4_) | copy-start | bytes 405508
  87.6 13.8 %collective-permute-start.8 = (bf16[528,128]{1,0:T(8,128)(2,1)}, bf16[528,128]{1,0:T(8,128)(2,1)S(1)}, u32[]{:S(2)}, u32[]{:S(2)}) collective-permute-start(bf16[528,128]{1,0:T(8,128)(2,1)} %get-tuple-element.34), channel_id=1, source_target_pairs={{0,144},{16,128},{32,176},{48,160},{64,208},{80,192},{96,240},{112... | collective-permute-start | bytes 405512 | tf_op jit(solution)/shard_map/ppermute | solution.py:298
  88.1 64.2 %copy-start.7 = (bf16[528,128]{1,0:T(8,128)(2,1)}, bf16[528,128]{1,0:T(8,128)(2,1)S(1)}, u32[]{:S(2)}) copy-start(bf16[528,128]{1,0:T(8,128)(2,1)S(1)} %collective-permute-done.4.refs_5_) | copy-start | bytes 405508
  88.1 20.8 %collective-permute-start.9 = (bf16[528,128]{1,0:T(8,128)(2,1)}, bf16[528,128]{1,0:T(8,128)(2,1)S(1)}, u32[]{:S(2)}, u32[]{:S(2)}) collective-permute-start(bf16[528,128]{1,0:T(8,128)(2,1)} %get-tuple-element.35), channel_id=1, source_target_pairs={{0,160},{16,176},{32,128},{48,144},{64,224},{80,240},{96,192},{112... | collective-permute-start | bytes 405512 | tf_op jit(solution)/shard_map/ppermute | solution.py:298
  93.7 58.5 %copy-start.8 = (bf16[528,128]{1,0:T(8,128)(2,1)}, bf16[528,128]{1,0:T(8,128)(2,1)S(1)}, u32[]{:S(2)}) copy-start(bf16[528,128]{1,0:T(8,128)(2,1)S(1)} %collective-permute-done.5.refs_6_) | copy-start | bytes 405508
  93.7 22.2 %collective-permute-start.10 = (bf16[528,128]{1,0:T(8,128)(2,1)}, bf16[528,128]{1,0:T(8,128)(2,1)S(1)}, u32[]{:S(2)}, u32[]{:S(2)}) collective-permute-start(bf16[528,128]{1,0:T(8,128)(2,1)} %get-tuple-element.36), channel_id=1, source_target_pairs={{0,176},{16,160},{32,144},{48,128},{64,240},{80,224},{96,208},{112... | collective-permute-start | bytes 405512 | tf_op jit(solution)/shard_map/ppermute | solution.py:298
  95.7 56.6 %copy-start.9 = (bf16[528,128]{1,0:T(8,128)(2,1)}, bf16[528,128]{1,0:T(8,128)(2,1)S(1)}, u32[]{:S(2)}) copy-start(bf16[528,128]{1,0:T(8,128)(2,1)S(1)} %collective-permute-done.6.refs_7_) | copy-start | bytes 405508
  95.7 24.9 %collective-permute-start.11 = (bf16[528,128]{1,0:T(8,128)(2,1)}, bf16[528,128]{1,0:T(8,128)(2,1)S(1)}, u32[]{:S(2)}, u32[]{:S(2)}) collective-permute-start(bf16[528,128]{1,0:T(8,128)(2,1)} %get-tuple-element.37), channel_id=1, source_target_pairs={{0,192},{16,208},{32,224},{48,240},{64,128},{80,144},{96,160},{112... | collective-permute-start | bytes 405512 | tf_op jit(solution)/shard_map/ppermute | solution.py:298
  98.5 53.7 %copy-start.10 = (bf16[528,128]{1,0:T(8,128)(2,1)}, bf16[528,128]{1,0:T(8,128)(2,1)S(1)}, u32[]{:S(2)}) copy-start(bf16[528,128]{1,0:T(8,128)(2,1)S(1)} %collective-permute-done.7.refs_8_) | copy-start | bytes 405508
  98.6 25.4 %collective-permute-start.12 = (bf16[528,128]{1,0:T(8,128)(2,1)}, bf16[528,128]{1,0:T(8,128)(2,1)S(1)}, u32[]{:S(2)}, u32[]{:S(2)}) collective-permute-start(bf16[528,128]{1,0:T(8,128)(2,1)} %get-tuple-element.38), channel_id=1, source_target_pairs={{0,208},{16,192},{32,240},{48,224},{64,144},{80,128},{96,176},{112... | collective-permute-start | bytes 405512 | tf_op jit(solution)/shard_map/ppermute | solution.py:298
  101.5 50.8 %copy-start.11 = (bf16[528,128]{1,0:T(8,128)(2,1)}, bf16[528,128]{1,0:T(8,128)(2,1)S(1)}, u32[]{:S(2)}) copy-start(bf16[528,128]{1,0:T(8,128)(2,1)S(1)} %collective-permute-done.8.refs_9_) | copy-start | bytes 405508
  101.5 29.0 %collective-permute-start.13 = (bf16[528,128]{1,0:T(8,128)(2,1)}, bf16[528,128]{1,0:T(8,128)(2,1)S(1)}, u32[]{:S(2)}, u32[]{:S(2)}) collective-permute-start(bf16[528,128]{1,0:T(8,128)(2,1)} %get-tuple-element.39), channel_id=1, source_target_pairs={{0,224},{16,240},{32,192},{48,208},{64,160},{80,176},{96,128},{112... | collective-permute-start | bytes 405512 | tf_op jit(solution)/shard_map/ppermute | solution.py:298
  108.9 43.4 %copy-start.12 = (bf16[528,128]{1,0:T(8,128)(2,1)}, bf16[528,128]{1,0:T(8,128)(2,1)S(1)}, u32[]{:S(2)}) copy-start(bf16[528,128]{1,0:T(8,128)(2,1)S(1)} %collective-permute-done.9.refs_10_) | copy-start | bytes 405508
  108.9 29.9 %collective-permute-start.14 = (bf16[528,128]{1,0:T(8,128)(2,1)}, bf16[528,128]{1,0:T(8,128)(2,1)S(1)}, u32[]{:S(2)}, u32[]{:S(2)}) collective-permute-start(bf16[528,128]{1,0:T(8,128)(2,1)} %get-tuple-element.40), channel_id=1, source_target_pairs={{0,240},{16,224},{32,208},{48,192},{64,176},{80,160},{96,144},{112... | collective-permute-start | bytes 405512 | tf_op jit(solution)/shard_map/ppermute | solution.py:298
  116.0 36.4 %copy-start.13 = (bf16[528,128]{1,0:T(8,128)(2,1)}, bf16[528,128]{1,0:T(8,128)(2,1)S(1)}, u32[]{:S(2)}) copy-start(bf16[528,128]{1,0:T(8,128)(2,1)S(1)} %collective-permute-done.10.refs_11_) | copy-start | bytes 405508
  120.5 31.8 %copy-start.14 = (bf16[528,128]{1,0:T(8,128)(2,1)}, bf16[528,128]{1,0:T(8,128)(2,1)S(1)}, u32[]{:S(2)}) copy-start(bf16[528,128]{1,0:T(8,128)(2,1)S(1)} %collective-permute-done.11.refs_12_) | copy-start | bytes 405508
  124.0 28.3 %copy-start.15 = (bf16[528,128]{1,0:T(8,128)(2,1)}, bf16[528,128]{1,0:T(8,128)(2,1)S(1)}, u32[]{:S(2)}) copy-start(bf16[528,128]{1,0:T(8,128)(2,1)S(1)} %collective-permute-done.12.refs_13_) | copy-start | bytes 405508
  130.4 21.9 %copy-start.16 = (bf16[528,128]{1,0:T(8,128)(2,1)}, bf16[528,128]{1,0:T(8,128)(2,1)S(1)}, u32[]{:S(2)}) copy-start(bf16[528,128]{1,0:T(8,128)(2,1)S(1)} %collective-permute-done.13.refs_14_) | copy-start | bytes 405508
  138.8 13.6 %copy-start.17 = (bf16[528,128]{1,0:T(8,128)(2,1)}, bf16[528,128]{1,0:T(8,128)(2,1)S(1)}, u32[]{:S(2)}) copy-start(bf16[528,128]{1,0:T(8,128)(2,1)S(1)} %collective-permute-done.14.refs_15_) | copy-start | bytes 405508
  175.2 5.3 %copy-start.2 = (s32[16,256]{1,0:T(8,128)S(1)}, s32[16,256]{1,0:T(8,128)}, u32[]{:S(2)}) copy-start(s32[16,256]{1,0:T(8,128)} %get-tuple-element.23.slot_ref) | copy-start | bytes 49156
  175.2 59.5 %all-to-all-start.2 = ((bf16[256,32,128]{2,1,0:T(8,128)(2,1)}), bf16[256,32,128]{2,1,0:T(8,128)(2,1)S(1)}, u32[]{:S(2)}, u32[]{:S(2)}) async-start(bf16[256,32,128]{2,1,0:T(8,128)(2,1)} %shard_map.67), calls=%async_computation.2 | async-start | bytes 4194304 | tf_op jit(solution)/shard_map/all_to_all | solution.py:321
  234.6 1.4 copy-start

commit v3 on v2

--- a/solution.py
+++ b/solution.py
@@ -42,24 +42,29 @@
     return one_hot(column == (a * minor + b) * unit + u)
 
 
-def pack_kernel(label_ref, key_scale_ref, value_scale_ref, q_ref, slot_ref, out_ref):
+def slot_of(label, before):
+    member = iota((CLUSTERS, label.shape[1]), 0) == label
+    count = matmul(one_hot(member), before)
+    rank = jnp.sum(jnp.where(member, count, 0.0), axis=0, keepdims=True)
+    return label * CAP + rank.astype(jnp.int32)
+
+
+def before_matrix(rows):
+    return one_hot(iota((rows, rows), 0) < iota((rows, rows), 1))
+
+
+def pack_kernel(label_ref, key_scale_ref, value_scale_ref, q_ref, out_ref):
     rows, heads, width = q_ref.shape
-    before = one_hot(iota((rows, rows), 0) < iota((rows, rows), 1))
+    halves = rows // width
     for h in range(heads):
-        label = label_ref[h]
-        member = iota((CLUSTERS, rows), 0) == label
-        count = matmul(one_hot(member), before)
-        rank = jnp.sum(jnp.where(member, count, 0.0), axis=0, keepdims=True).astype(jnp.int32)
-        slot = label * CAP + rank
-        slot_ref[h : h + 1, :] = slot
         kinds = (
-            (slot // CHUNK).astype(jnp.float32),
-            (slot % CHUNK).astype(jnp.float32),
+            label_ref[h].astype(jnp.float32),
             key_scale_ref[h : h + 1, :].astype(jnp.float32),
             value_scale_ref[h : h + 1, :].astype(jnp.float32),
         )
         meta = jnp.concatenate(
-            [kind[:, half : half + width] for kind in kinds for half in range(0, rows, width)],
+            [kind[:, n * width : (n + 1) * width] for kind in kinds for n in range(halves)]
+            + [jnp.zeros((META - 3 * halves, width), jnp.float32)],
             axis=0,
         )
         out_ref[h, rows : rows + META, :] = meta.astype(jnp.bfloat16)
@@ -71,8 +76,7 @@
         out_ref[:, g * group : (g + 1) * group, :] = turned.reshape(heads, group, width)
 
 
-def place_kernel(slot_ref, k_ref, v_ref, out_ref, by_head):
-    step = pl.program_id(0)
+def place_kernel(label_ref, k_ref, v_ref, slot_ref, out_ref, by_head):
     rows, _, width = k_ref.shape
     group = 256 // HALF
     swap = swap_matrix(group, HALF, 1)
@@ -83,27 +87,44 @@
         )
         turned = matmul(swap, block).astype(jnp.bfloat16)
         by_head[:, here, :] = turned.reshape(HALF, group, 2 * width)
+    before = before_matrix(rows)
     for h in range(HALF):
-        slot = slot_ref[pl.ds(step * HALF + h, 1), :]
+        slot = slot_of(label_ref[h], before)
+        slot_ref[h : h + 1, :] = slot
         pick = one_hot(iota((SLOTS, rows), 0) == slot)
         placed = matmul(pick, by_head[h]).astype(jnp.bfloat16)
         out_ref[:, h] = placed.reshape(COARSE, CHUNK, 2 * width)
 
 
-def sort_kernel(me_ref, in_ref, *refs):
-    outs, (table, scales) = refs[:COARSE], refs[COARSE:]
+def sort_kernel(me_ref, arrived_ref, *refs):
+    outs, (table, scales, in_ref, sems) = refs[:COARSE], refs[COARSE:]
     me = me_ref[0]
     blocks, rows, width = in_ref.shape
     rows = rows - META
     batch = 256 // CHUNK
+    quarter = blocks // 4
+    copies = [
+        pltpu.make_async_copy(
+            arrived_ref.at[pl.ds(n * quarter, quarter)],
+            in_ref.at[pl.ds(n * quarter, quarter)],
+            sems.at[n],
+        )
+        for n in range(4)
+    ]
+    for copy in copies:
+        copy.start()
+    before = before_matrix(rows)
     for s in range(blocks):
+        if s % quarter == 0:
+            copies[s // quarter].wait()
         meta = in_ref[s, rows : rows + META, :].astype(jnp.float32)
-        coarse, here, key_scale, value_scale = (
+        label, key_scale, value_scale = (
             jnp.concatenate([meta[2 * n : 2 * n + 1], meta[2 * n + 1 : 2 * n + 2]], axis=1)
-            for n in range(4)
-        )
-        owner = coarse.astype(jnp.int32) ^ me
-        here = here.astype(jnp.int32)
+            for n in range(3)
+        )
+        slot = slot_of(label.astype(jnp.int32), before)
+        owner = (slot // CHUNK) ^ me
+        here = slot % CHUNK
         pick = one_hot(iota((SLOTS, rows), 0) == owner * CHUNK + here)
         placed = matmul(pick, in_ref[s, :rows, :]).astype(jnp.bfloat16)
         table[:, s] = placed.reshape(COARSE, CHUNK, width)
@@ -141,47 +162,60 @@
         )
 
 
-def attend_kernel(me_ref, message_ref, *refs):
-    parts, out_ref = refs[:COARSE], refs[COARSE]
-    qs, kvs, os, scale_rows, scales = refs[COARSE + 1 :]
+def queries_kernel(me_ref, *refs):
+    parts, (qs, scales, scale_rows) = refs[:COARSE], refs[COARSE:]
+    me = me_ref[0]
+    total, width = qs.shape[1:]
+    sources = total // CAP
+    blocks = sources // COARSE
+    slab = blocks * CAP
+    for d, part in enumerate(parts):
+        source = me ^ d
+        qs[:, pl.ds(pl.multiple_of(source * slab, slab), slab), :] = part[
+            : FINE * slab, :
+        ].reshape(FINE, slab, width)
+        scale_rows[pl.ds(pl.multiple_of(source * blocks, blocks), blocks), :] = part[
+            FINE * slab :, :
+        ]
+    spread = one_hot(iota((total, sources), 0) // CAP == iota((total, sources), 1))
+    table = matmul(spread, scale_rows[...])
+    lane, row = iota((total, 128), 1), iota((total, 128), 0)
+    table = jnp.where(lane % CAP == row % CAP, table, 0.0).astype(jnp.bfloat16)
+    gather = one_hot(iota((2 * FINE, 128), 0) == iota((2 * FINE, 128), 1) // CAP)
+    scales[...] = matmul_nt(gather, table)
+
+
+PIECES = 4
+
+
+def attend_kernel(arrived_ref, qs, scales, out_ref, message, kvs, os, sems):
     f = pl.program_id(0)
-    sources, _, width = message_ref.shape
+    sources, _, width = message.shape
     width = width // 2
-    blocks = sources // COARSE
     total = sources * CAP
     batch = 256 // CHUNK
     unit = batch * CAP
-    slab = blocks * CAP
 
     @pl.when(f == 0)
     def _():
-        me = me_ref[0]
-        for d, part in enumerate(parts):
-            source = me ^ d
-            qs[:, pl.ds(pl.multiple_of(source * slab, slab), slab), :] = part[
-                : FINE * slab, :
-            ].reshape(FINE, slab, width)
-            scale_rows[pl.ds(pl.multiple_of(source * blocks, blocks), blocks), :] = part[
-                FINE * slab :, :
-            ]
+        piece = sources // PIECES
+        copies = [
+            pltpu.make_async_copy(
+                arrived_ref.at[pl.ds(n * piece, piece)],
+                message.at[pl.ds(n * piece, piece)],
+                sems.at[n],
+            )
+            for n in range(PIECES)
+        ]
+        for copy in copies:
+            copy.start()
         swap = swap_matrix(batch, FINE, CAP)
-
-        def turn(g, carry):
-            block = message_ref[pl.ds(g * batch, batch)].reshape(256, 2 * width)
-            turned = matmul(swap, block).astype(jnp.bfloat16)
-            kvs[:, pl.ds(pl.multiple_of(g * unit, unit), unit), :] = turned.reshape(
-                FINE, unit, 2 * width
-            )
-            return carry
-
-        lax.fori_loop(0, sources // batch, turn, 0, unroll=8)
-
-        spread = one_hot(iota((total, sources), 0) // CAP == iota((total, sources), 1))
-        table = matmul(spread, scale_rows[...])
-        lane, row = iota((total, 128), 1), iota((total, 128), 0)
-        table = jnp.where(lane % CAP == row % CAP, table, 0.0).astype(jnp.bfloat16)
-        gather = one_hot(iota((2 * FINE, 128), 0) == iota((2 * FINE, 128), 1) // CAP)
-        scales[...] = matmul_nt(gather, table)
+        for n in range(PIECES):
+            copies[n].wait()
+            for g in range(n * piece // batch, (n + 1) * piece // batch):
+                block = message[g * batch : (g + 1) * batch].reshape(256, 2 * width)
+                turned = matmul(swap, block).astype(jnp.bfloat16)
+                kvs[:, g * unit : (g + 1) * unit, :] = turned.reshape(FINE, unit, 2 * width)
 
     key_scale = scales[pl.ds(f, 1), :]
     value_scale = scales[pl.ds(FINE + f, 1), :]
@@ -191,7 +225,7 @@
     ahead = iota((tile, tile), 1) > iota((tile, tile), 0)
     for t in range(total // tile):
         here = slice(t * tile, (t + 1) * tile)
-        query = qs[f, here, :]
+        query = qs[0, here, :]
         pieces = []
         for u in range(t + 1):
             there = slice(u * tile, (u + 1) * tile)
@@ -228,10 +262,23 @@
         lax.fori_loop(0, sources // batch, turn, 0, unroll=8)
 
 
-def unplace_kernel(slot_ref, in_ref, out_ref, by_head):
+def unplace_kernel(slot_ref, arrived_ref, out_ref, by_head, answer, sems):
     step = pl.program_id(0)
     rows = slot_ref.shape[0]
-    width = in_ref.shape[3]
+    width = out_ref.shape[2]
+
+    def copy(n):
+        return pltpu.make_async_copy(
+            arrived_ref.at[:, pl.ds(n * HALF, HALF)], answer.at[n], sems.at[n]
+        )
+
+    @pl.when(step == 0)
+    def _():
+        for n in range(answer.shape[0]):
+            copy(n).start()
+
+    copy(step).wait()
+    in_ref = answer.at[step]
     group = 256 // HALF
     swap = swap_matrix(HALF, group, 1)
     lane = iota(slot_ref.shape, 1)
@@ -256,40 +303,48 @@
     me = lax.axis_index("outer").astype(jnp.int32).reshape(1)
     scalar = pl.BlockSpec(memory_space=pltpu.SMEM)
 
-    slots, packed = pl.pallas_call(
+    anywhere = pl.BlockSpec(memory_space=pl.ANY)
+    labels = jnp.swapaxes(cluster_label, 1, 2)
+    packed = pl.pallas_call(
         pack_kernel,
-        out_shape=(
-            jax.ShapeDtypeStruct((heads, rows), jnp.int32),
-            jax.ShapeDtypeStruct((heads, rows + META, width), bf16),
-        ),
+        out_shape=jax.ShapeDtypeStruct((heads, rows + META, width), bf16),
         cost_estimate=pl.CostEstimate(flops=10**9, bytes_accessed=2**21, transcendentals=0),
-    )(jnp.swapaxes(cluster_label, 1, 2), key_scale.T, value_scale.T, queries)
+    )(labels, key_scale.T, value_scale.T, queries)
     packed = lax.all_to_all(packed, "inner", 0, 0, tiled=True)
 
     tokens = pl.BlockSpec((rows, HALF, width), lambda i: (0, i, 0))
-    message = pl.pallas_call(
+    slots, message = pl.pallas_call(
         place_kernel,
         grid=(heads // HALF,),
-        in_specs=[pl.BlockSpec((heads, rows), lambda i: (0, 0)), tokens, tokens],
-        out_specs=pl.BlockSpec((COARSE, HALF, CHUNK, 2 * width), lambda i: (0, i, 0, 0)),
-        out_shape=jax.ShapeDtypeStruct((COARSE, heads, CHUNK, 2 * width), bf16),
+        in_specs=[pl.BlockSpec((HALF, 1, rows), lambda i: (i, 0, 0)), tokens, tokens],
+        out_specs=[
+            pl.BlockSpec((HALF, rows), lambda i: (i, 0)),
+            pl.BlockSpec((COARSE, HALF, CHUNK, 2 * width), lambda i: (0, i, 0, 0)),
+        ],
+        out_shape=[
+            jax.ShapeDtypeStruct((heads, rows), jnp.int32),
+            jax.ShapeDtypeStruct((COARSE, heads, CHUNK, 2 * width), bf16),
+        ],
         scratch_shapes=[pltpu.VMEM((HALF, rows, 2 * width), bf16)],
         cost_estimate=pl.CostEstimate(
             flops=3 * 10**9, bytes_accessed=6 * 2**20, transcendentals=0
         ),
-    )(slots, key_rows, value_rows)
+    )(labels, key_rows, value_rows)
     message = message.reshape(devices, CHUNK, 2 * width)
     message = lax.all_to_all(message, BOTH, 0, 0, tiled=True)
 
     part_rows = FINE * inner * CAP + inner
     parts = pl.pallas_call(
         sort_kernel,
-        in_specs=[scalar, pl.BlockSpec(memory_space=pltpu.VMEM)],
+        in_specs=[scalar, anywhere],
         out_shape=[jax.ShapeDtypeStruct((part_rows, width), bf16)] * COARSE,
         scratch_shapes=[
             pltpu.VMEM((COARSE, inner, CHUNK, width), bf16),
             pltpu.VMEM((COARSE * inner, width), f32),
-        ],
+            pltpu.VMEM((inner, rows + META, width), bf16),
+            pltpu.SemaphoreType.DMA((4,)),
+        ],
+        compiler_params=pltpu.CompilerParams(vmem_limit_bytes=24 * 2**20),
         cost_estimate=pl.CostEstimate(
             flops=2 * 10**9, bytes_accessed=3 * 2**20, transcendentals=0
         ),
@@ -300,24 +355,38 @@
     ]
 
     total = devices * CAP
+    by_cluster, scales = pl.pallas_call(
+        queries_kernel,
+        in_specs=[scalar] + [pl.BlockSpec(memory_space=pltpu.VMEM)] * COARSE,
+        out_shape=[
+            jax.ShapeDtypeStruct((FINE, total, width), bf16),
+            jax.ShapeDtypeStruct((2 * FINE, total), f32),
+        ],
+        scratch_shapes=[pltpu.VMEM((devices, width), bf16)],
+        cost_estimate=pl.CostEstimate(
+            flops=10**9, bytes_accessed=4 * 2**20, transcendentals=0
+        ),
+    )(me, *parts)
     answer = pl.pallas_call(
         attend_kernel,
         grid=(FINE,),
-        in_specs=[scalar, pl.BlockSpec((devices, CHUNK, 2 * width), lambda i: (0, 0, 0))]
-        + [pl.BlockSpec((part_rows, width), lambda i: (0, 0))] * COARSE,
+        in_specs=[
+            anywhere,
+            pl.BlockSpec((1, total, width), lambda i: (i, 0, 0)),
+            pl.BlockSpec((2 * FINE, total), lambda i: (0, 0)),
+        ],
         out_specs=pl.BlockSpec((devices, CHUNK, width), lambda i: (0, 0, 0)),
         out_shape=jax.ShapeDtypeStruct((devices, CHUNK, width), bf16),
         scratch_shapes=[
-            pltpu.VMEM((FINE, total, width), bf16),
+            pltpu.VMEM((devices, CHUNK, 2 * width), bf16),
             pltpu.VMEM((FINE, total, 2 * width), bf16),
             pltpu.VMEM((FINE, total, width), bf16),
-            pltpu.VMEM((devices, width), bf16),
-            pltpu.VMEM((2 * FINE, total), f32),
+            pltpu.SemaphoreType.DMA((PIECES,)),
         ],
         cost_estimate=pl.CostEstimate(
             flops=4 * 10**9, bytes_accessed=8 * 2**20, transcendentals=5 * 10**6
         ),
-    )(me, message, *parts)
+    )(message, by_cluster, scales)
     answer = lax.all_to_all(answer, BOTH, 0, 0, tiled=True)
 
     return pl.pallas_call(
@@ -325,11 +394,16 @@
         grid=(heads // HALF,),
         in_specs=[
             pl.BlockSpec((rows, heads), lambda i: (0, 0)),
-            pl.BlockSpec((COARSE, HALF, CHUNK, width), lambda i: (0, i, 0, 0)),
+            anywhere,
         ],
         out_specs=pl.BlockSpec((rows, HALF, width), lambda i: (0, i, 0)),
         out_shape=jax.ShapeDtypeStruct((rows, heads, width), bf16),
-        scratch_shapes=[pltpu.VMEM((HALF, rows, width), bf16)],
+        scratch_shapes=[
+            pltpu.VMEM((HALF, rows, width), bf16),
+            pltpu.VMEM((heads // HALF, COARSE, HALF, CHUNK, width), bf16),
+            pltpu.SemaphoreType.DMA((heads // HALF,)),
+        ],
+        compiler_params=pltpu.CompilerParams(vmem_limit_bytes=24 * 2**20),
         cost_estimate=pl.CostEstimate(
             flops=10**9, bytes_accessed=3 * 2**20, transcendentals=0
         ),

time: 241 us -> 235 us (0.975)
  starting transfers between devices: 58.4 us -> 52.5 us
  Pallas kernels: 39.8 us -> 42.5 us
    ppermute x15, starting transfers between devices: 32.9 us -> 27.1 us  [shards(): lax.ppermute(parts[d], 'outer', [(n, n ^ d) for n in range(outer)])]
    all_to_all x1, waiting for transfers between devices: 13.5 us -> 9.28 us  [shards(): message = lax.all_to_all(message, BOTH, 0, 0, tiled=True)]
    ppermute x15, waiting for transfers between devices: 48.3 us -> 52.2 us  [shards(): lax.ppermute(parts[d], 'outer', [(n, n ^ d) for n in range(outer)])]
    pallas_call x3 -> x4, Pallas kernels: 30.5 us -> 33.1 us  [the longest x1 21.3 us: shards(): pl.pallas_call(attend_kernel, grid=(FINE,), in_specs=[anywhere, pl.BlockS...]
  transfers between devices with their start and end apart: 18 -> 18, of which waited for: 12 -> 13; matrix products, arithmetic and copies ran while one was open for 0% -> 0% of each run, Pallas kernels for 4% -> 6%
where the time goes in v3:
time: 235 us
  waiting for transfers between devices  138 us (59%)
  starting transfers between devices  52.5 us (22%)
  Pallas kernels  42.5 us (18%)
    all_to_all x1, waiting for transfers between devices, shards(): answer = lax.all_to_all(answer, BOTH, 0, 0, tiled=True)  54.1 us
    ppermute x15, waiting for transfers between devices, shards(): lax.ppermute(parts[d], 'outer', [(n, n ^ d) for n in range(outer)])  52.2 us
    ppermute x15, starting transfers between devices, shards(): lax.ppermute(parts[d], 'outer', [(n, n ^ d) for n in range(outer)])  27.1 us
    all_to_all x1, waiting for transfers between devices, shards(): packed = lax.all_to_all(packed, 'inner', 0, 0, tiled=True)  22.6 us
    pallas_call x1, Pallas kernels, shards(): pl.pallas_call(attend_kernel, grid=(FINE,), in_specs=[anywhere, pl.BlockS...  21.3 us
    all_to_all x1, starting transfers between devices, shards(): message = lax.all_to_all(message, BOTH, 0, 0, tiled=True)  10.2 us
    all_to_all x1, starting transfers between devices, shards(): packed = lax.all_to_all(packed, 'inner', 0, 0, tiled=True)  9.98 us
    all_to_all x1, waiting for transfers between devices, shards(): message = lax.all_to_all(message, BOTH, 0, 0, tiled=True)  9.28 us
  transfers between devices with their start and end apart: 18, of which 13 were waited for; matrix products, arithmetic and copies ran while one was open for 0% of the time, Pallas kernels for 6%

profile of v3, /device:TPU:1, one launch (start us, length us, event | category | flops | bytes accessed | tf_op | source)
XLA Modules:
  0.0 235.0 jit_solution(2865298784258432744)
XLA Ops:
  0.0 3.0 %shard_map.65 = bf16[16,264,128]{2,1,0:T(8,128)(2,1)} custom-call(s32[16,1,256]{2,1,0:T(1,128)} %bitcast.10, bf16[16,256]{1,0:T(8,128)(2,1)} %bitcast.12, bf16[16,256]{1,0:T(8,128)(2,1)} %bitcast.13, bf16[256,16,128]{2,1,0:T(8,128)(2,1)} %q_ref.1), custom_call_target="tpu_custom_call" | custom-call | flops 1000000000 | bytes 2097152 | tf_op jit(solution)/shard_map/pallas_call | solution.py:308
  3.0 10.0 %all-to-all-start.1 = ((bf16[16,264,128]{2,1,0:T(8,128)(2,1)}), bf16[16,264,128]{2,1,0:T(8,128)(2,1)S(1)}, u32[]{:S(2)}, u32[]{:S(2)}) async-start(bf16[16,264,128]{2,1,0:T(8,128)(2,1)} %shard_map.65), calls=%async_computation.1 | async-start | bytes 2162688 | tf_op jit(solution)/shard_map/all_to_all | solution.py:313
  13.0 6.0 %shard_map.64 = (s32[16,256]{1,0:T(8,128)}, bf16[16,16,32,256]{3,2,1,0:T(8,128)(2,1)}) custom-call(s32[16,1,256]{2,1,0:T(1,128)} %bitcast.11, bf16[256,16,128]{2,1,0:T(8,128)(2,1)} %k_ref.1, bf16[256,16,128]{2,1,0:T(8,128)(2,1)} %v_ref.1), custom_call_target="tpu_custom_call" | custom-call | flops 3000000000 | bytes 6291456 | tf_op jit(solution)/shard_map/pallas_call | solution.py:316
  18.9 22.6 %all-to-all-done.1.arrived_ref = bf16[16,264,128]{2,1,0:T(8,128)(2,1)S(1)} async-done(((bf16[16,264,128]{2,1,0:T(8,128)(2,1)}), bf16[16,264,128]{2,1,0:T(8,128)(2,1)S(1)}, u32[]{:S(2)}, u32[]{:S(2)}) %all-to-all-start.1) | async-done | bytes 1081376 | tf_op jit(solution)/shard_map/all_to_all | solution.py:313
  41.6 10.2 %all-to-all-start = ((bf16[256,32,256]{2,1,0:T(8,128)(2,1)}), bf16[256,32,256]{2,1,0:T(8,128)(2,1)}, u32[]{:S(2)}, u32[]{:S(2)}) async-start(bf16[256,32,256]{2,1,0:T(8,128)(2,1)} %bitcast.9), calls=%async_computation | async-start | bytes 8388608 | tf_op jit(solution)/shard_map/all_to_all | solution.py:334
  51.8 5.3 %shard_map.66 = (bf16[528,128]{1,0:T(8,128)(2,1)S(1)}, bf16[528,128]{1,0:T(8,128)(2,1)S(1)}, bf16[528,128]{1,0:T(8,128)(2,1)S(1)}, bf16[528,128]{1,0:T(8,128)(2,...) custom-call(s32[1]{0:T(128)} %bitcast.3.me_ref, ...), custom_call_target="tpu_custom_call" | custom-call | flops 2000000000 | bytes 3145728 | tf_op jit(solution)/shard_map/pallas_call | solution.py:337
  57.1 0.0 copy-start
  57.2 0.6 copy-done
  57.8 1.4 collective-permute-start
  59.2 2.4 %collective-permute-start.1 = (bf16[528,128]{1,0:T(8,128)(2,1)S(1)}, bf16[528,128]{1,0:T(8,128)(2,1)S(1)}, u32[]{:S(2)}, u32[]{:S(2)}) collective-permute-start(bf16[528,128]{1,0:T(8,128)(2,1)S(1)} %get-tuple-element.29), channel_id=1, source_target_pairs={{0,32},{16,48},{32,0},{48,16},{64,96},{80,112},{96,64},{112,80},{1... | collective-permute-start | bytes 405512 | tf_op jit(solution)/shard_map/ppermute | solution.py:353
  61.6 0.0 collective-permute-start.2
  61.7 1.4 collective-permute-start.3
  63.0 0.0 collective-permute-start.4
  63.1 3.0 %collective-permute-done.refs_1_ = bf16[528,128]{1,0:T(8,128)(2,1)S(1)} collective-permute-done((bf16[528,128]{1,0:T(8,128)(2,1)S(1)}, bf16[528,128]{1,0:T(8,128)(2,1)S(1)}, u32[]{:S(2)}, u32[]{:S(2)}) %collective-permute-start) | collective-permute-done | bytes 135200 | tf_op jit(solution)/shard_map/ppermute | solution.py:353
  66.0 4.6 %collective-permute-start.5 = (bf16[528,128]{1,0:T(8,128)(2,1)S(1)}, bf16[528,128]{1,0:T(8,128)(2,1)S(1)}, u32[]{:S(2)}, u32[]{:S(2)}) collective-permute-start(bf16[528,128]{1,0:T(8,128)(2,1)S(1)} %get-tuple-element.33), channel_id=1, source_target_pairs={{0,96},{16,112},{32,64},{48,80},{64,32},{80,48},{96,0},{112,16},{1... | collective-permute-start | bytes 405512 | tf_op jit(solution)/shard_map/ppermute | solution.py:353
  70.6 13.3 %collective-permute-done.1.refs_2_ = bf16[528,128]{1,0:T(8,128)(2,1)S(1)} collective-permute-done((bf16[528,128]{1,0:T(8,128)(2,1)S(1)}, bf16[528,128]{1,0:T(8,128)(2,1)S(1)}, u32[]{:S(2)}, u32[]{:S(2)}) %collective-permute-start.1) | collective-permute-done | bytes 135200 | tf_op jit(solution)/shard_map/ppermute | solution.py:353
  83.9 0.0 copy-start.3
  84.0 2.7 %collective-permute-start.6 = (bf16[528,128]{1,0:T(8,128)(2,1)S(1)}, bf16[528,128]{1,0:T(8,128)(2,1)S(1)}, u32[]{:S(2)}, u32[]{:S(2)}) collective-permute-start(bf16[528,128]{1,0:T(8,128)(2,1)S(1)} %get-tuple-element.34), channel_id=1, source_target_pairs={{0,112},{16,96},{32,80},{48,64},{64,48},{80,32},{96,16},{112,0},{1... | collective-permute-start | bytes 405512 | tf_op jit(solution)/shard_map/ppermute | solution.py:353
  86.6 0.0 collective-permute-done.2.refs_3_
  86.6 1.9 collective-permute-start.7
  88.5 0.0 collective-permute-done.3.refs_4_
  88.5 0.0 collective-permute-start.8
  88.6 0.0 collective-permute-done.4.refs_5_
  88.6 0.0 copy-start.6
  88.6 4.3 %collective-permute-start.9 = (bf16[528,128]{1,0:T(8,128)(2,1)S(1)}, bf16[528,128]{1,0:T(8,128)(2,1)S(1)}, u32[]{:S(2)}, u32[]{:S(2)}) collective-permute-start(bf16[528,128]{1,0:T(8,128)(2,1)S(1)} %get-tuple-element.37), channel_id=1, source_target_pairs={{0,160},{16,176},{32,128},{48,144},{64,224},{80,240},{96,192},{112... | collective-permute-start | bytes 405512 | tf_op jit(solution)/shard_map/ppermute | solution.py:353
  92.8 0.0 collective-permute-done.5.refs_6_
  92.8 2.8 %collective-permute-start.10 = (bf16[528,128]{1,0:T(8,128)(2,1)S(1)}, bf16[528,128]{1,0:T(8,128)(2,1)S(1)}, u32[]{:S(2)}, u32[]{:S(2)}) collective-permute-start(bf16[528,128]{1,0:T(8,128)(2,1)S(1)} %get-tuple-element.38), channel_id=1, source_target_pairs={{0,176},{16,160},{32,144},{48,128},{64,240},{80,224},{96,208},{112... | collective-permute-start | bytes 405512 | tf_op jit(solution)/shard_map/ppermute | solution.py:353
  95.6 0.0 collective-permute-done.6.refs_7_
  95.6 0.5 collective-permute-start.11
  96.1 2.6 %collective-permute-done.7.refs_8_ = bf16[528,128]{1,0:T(8,128)(2,1)S(1)} collective-permute-done((bf16[528,128]{1,0:T(8,128)(2,1)S(1)}, bf16[528,128]{1,0:T(8,128)(2,1)S(1)}, u32[]{:S(2)}, u32[]{:S(2)}) %collective-permute-start.7) | collective-permute-done | bytes 135200 | tf_op jit(solution)/shard_map/ppermute | solution.py:353
  98.8 1.2 collective-permute-start.12
  99.9 4.6 %collective-permute-done.8.refs_9_ = bf16[528,128]{1,0:T(8,128)(2,1)S(1)} collective-permute-done((bf16[528,128]{1,0:T(8,128)(2,1)S(1)}, bf16[528,128]{1,0:T(8,128)(2,1)S(1)}, u32[]{:S(2)}, u32[]{:S(2)}) %collective-permute-start.8) | collective-permute-done | bytes 135200 | tf_op jit(solution)/shard_map/ppermute | solution.py:353
  104.5 1.7 collective-permute-start.13
  106.3 5.4 %collective-permute-done.9.refs_10_ = bf16[528,128]{1,0:T(8,128)(2,1)S(1)} collective-permute-done((bf16[528,128]{1,0:T(8,128)(2,1)S(1)}, bf16[528,128]{1,0:T(8,128)(2,1)S(1)}, u32[]{:S(2)}, u32[]{:S(2)}) %collective-permute-start.9) | collective-permute-done | bytes 135200 | tf_op jit(solution)/shard_map/ppermute | solution.py:353
  111.6 2.2 collective-permute-start.14
  113.8 1.6 collective-permute-done.10.refs_11_
  115.4 5.1 %collective-permute-done.11.refs_12_ = bf16[528,128]{1,0:T(8,128)(2,1)S(1)} collective-permute-done((bf16[528,128]{1,0:T(8,128)(2,1)S(1)}, bf16[528,128]{1,0:T(8,128)(2,1)S(1)}, u32[]{:S(2)}, u32[]{:S(2)}) %collective-permute-start.11) | collective-permute-done | bytes 135200 | tf_op jit(solution)/shard_map/ppermute | solution.py:353
  120.5 5.3 %collective-permute-done.12.refs_13_ = bf16[528,128]{1,0:T(8,128)(2,1)S(1)} collective-permute-done((bf16[528,128]{1,0:T(8,128)(2,1)S(1)}, bf16[528,128]{1,0:T(8,128)(2,1)S(1)}, u32[]{:S(2)}, u32[]{:S(2)}) %collective-permute-start.12) | collective-permute-done | bytes 135200 | tf_op jit(solution)/shard_map/ppermute | solution.py:353
  125.8 7.2 %collective-permute-done.13.refs_14_ = bf16[528,128]{1,0:T(8,128)(2,1)S(1)} collective-permute-done((bf16[528,128]{1,0:T(8,128)(2,1)S(1)}, bf16[528,128]{1,0:T(8,128)(2,1)S(1)}, u32[]{:S(2)}, u32[]{:S(2)}) %collective-permute-start.13) | collective-permute-done | bytes 135200 | tf_op jit(solution)/shard_map/ppermute | solution.py:353
  133.0 4.1 %collective-permute-done.14.refs_15_ = bf16[528,128]{1,0:T(8,128)(2,1)S(1)} collective-permute-done((bf16[528,128]{1,0:T(8,128)(2,1)S(1)}, bf16[528,128]{1,0:T(8,128)(2,1)S(1)}, u32[]{:S(2)}, u32[]{:S(2)}) %collective-permute-start.14) | collective-permute-done | bytes 135200 | tf_op jit(solution)/shard_map/ppermute | solution.py:353
  137.2 0.0 copy-done.2
  137.2 0.0 copy-done.3
  137.2 0.0 copy-done.4
  137.2 0.0 copy-done.5
  137.2 0.0 copy-done.6
  137.2 0.0 copy-done.7
  137.2 0.0 copy-done.8
  137.2 0.0 copy-done.9
  137.2 0.0 copy-done.10
  137.2 0.0 copy-done.11
  137.2 0.0 copy-done.12
  137.3 0.0 copy-done.13
  137.3 0.0 copy-done.14
  137.3 0.0 copy-done.15
  137.3 0.5 copy-done.16
  137.8 3.5 %shard_map.67 = (bf16[8,1024,128]{2,1,0:T(8,128)(2,1)}, f32[16,1024]{1,0:T(8,128)}) custom-call(s32[1]{0:T(128)} %bitcast.3.me_ref, bf16[528,128]{1,0:T(8,128)(2,1)} %copy-done, bf16[528,128]{1,0:T(8,128)(2,1)} %copy-done.2, bf16[528,128]{1,0:T(8,128)(2,1)} %copy-done.3, bf16[528,128]{1,0:T(8,128)(2,1)} %copy-done.4, bf16[528,128]{1,0:T(8,128)(2,1)} %copy-done.5, ...), custom_call_target="tpu_custom_call" | custom-call | flops 1000000000 | bytes 4194304 | tf_op jit(solution)/shard_map/pallas_call | solution.py:358
  141.4 9.3 %all-to-all-done.arrived_ref = bf16[256,32,256]{2,1,0:T(8,128)(2,1)} async-done(((bf16[256,32,256]{2,1,0:T(8,128)(2,1)}), bf16[256,32,256]{2,1,0:T(8,128)(2,1)}, u32[]{:S(2)}, u32[]{:S(2)}) %all-to-all-start) | async-done | bytes 4194336 | tf_op jit(solution)/shard_map/all_to_all | solution.py:334
  150.7 21.3 %shard_map.68 = bf16[256,32,128]{2,1,0:T(8,128)(2,1)} custom-call(bf16[256,32,256]{2,1,0:T(8,128)(2,1)} %all-to-all-done.arrived_ref, bf16[8,1024,128]{2,1,0:T(8,128)(2,1)} %get-tuple-element.43.qs, f32[16,1024]{1,0:T(8,128)} %get-tuple-element.44.scales), custom_call_target="tpu_custom_call" | custom-call | flops 4000000000 | bytes 8388608 | tf_op jit(solution)/shard_map/pallas_call | solution.py:370
  171.9 0.0 copy-start.1
  171.9 5.2 %all-to-all-start.2 = ((bf16[256,32,128]{2,1,0:T(8,128)(2,1)}), bf16[256,32,128]{2,1,0:T(8,128)(2,1)S(1)}, u32[]{:S(2)}, u32[]{:S(2)}) async-start(bf16[256,32,128]{2,1,0:T(8,128)(2,1)} %shard_map.68), calls=%async_computation.2 | async-start | bytes 4194304 | tf_op jit(solution)/shard_map/all_to_all | solution.py:390
  177.2 0.0 copy-done.1
  177.2 0.1 copy.7
  177.3 54.1 %all-to-all-done.2 = bf16[256,32,128]{2,1,0:T(8,128)(2,1)S(1)} async-done(((bf16[256,32,128]{2,1,0:T(8,128)(2,1)}), bf16[256,32,128]{2,1,0:T(8,128)(2,1)S(1)}, u32[]{:S(2)}, u32[]{:S(2)}) %all-to-all-start.2) | async-done | bytes 2097184 | tf_op jit(solution)/shard_map/all_to_all | solution.py:390
  231.4 3.5 %shard_map.69 = bf16[256,16,128]{2,1,0:T(8,128)(2,1)} custom-call(s32[256,16]{1,0:T(8,128)S(1)} %bitcast.8, bf16[16,16,32,128]{3,2,1,0:T(8,128)(2,1)S(1)} %bitcast.7), custom_call_target="tpu_custom_call" | custom-call | flops 1000000000 | bytes 3145728 | tf_op jit(solution)/shard_map/pallas_call | solution.py:392
  (13 shorter events, 0.0 us)
Async XLA Ops:
  3.0 38.6 %all-to-all-start.1 = ((bf16[16,264,128]{2,1,0:T(8,128)(2,1)}), bf16[16,264,128]{2,1,0:T(8,128)(2,1)S(1)}, u32[]{:S(2)}, u32[]{:S(2)}) async-start(bf16[16,264,128]{2,1,0:T(8,128)(2,1)} %shard_map.65), calls=%async_computation.1 | async-start | bytes 2162688 | tf_op jit(solution)/shard_map/all_to_all | solution.py:313
  41.6 109.1 %all-to-all-start = ((bf16[256,32,256]{2,1,0:T(8,128)(2,1)}), bf16[256,32,256]{2,1,0:T(8,128)(2,1)}, u32[]{:S(2)}, u32[]{:S(2)}) async-start(bf16[256,32,256]{2,1,0:T(8,128)(2,1)} %bitcast.9), calls=%async_computation | async-start | bytes 8388608 | tf_op jit(solution)/shard_map/all_to_all | solution.py:334
  57.1 0.7 copy-start
  57.8 8.2 %collective-permute-start = (bf16[528,128]{1,0:T(8,128)(2,1)S(1)}, bf16[528,128]{1,0:T(8,128)(2,1)S(1)}, u32[]{:S(2)}, u32[]{:S(2)}) collective-permute-start(bf16[528,128]{1,0:T(8,128)(2,1)S(1)} %get-tuple-element.28), channel_id=1, source_target_pairs={{0,16},{16,0},{32,48},{48,32},{64,80},{80,64},{96,112},{112,96},{1... | collective-permute-start | bytes 405512 | tf_op jit(solution)/shard_map/ppermute | solution.py:353
  59.2 24.8 %collective-permute-start.1 = (bf16[528,128]{1,0:T(8,128)(2,1)S(1)}, bf16[528,128]{1,0:T(8,128)(2,1)S(1)}, u32[]{:S(2)}, u32[]{:S(2)}) collective-permute-start(bf16[528,128]{1,0:T(8,128)(2,1)S(1)} %get-tuple-element.29), channel_id=1, source_target_pairs={{0,32},{16,48},{32,0},{48,16},{64,96},{80,112},{96,64},{112,80},{1... | collective-permute-start | bytes 405512 | tf_op jit(solution)/shard_map/ppermute | solution.py:353
  61.6 25.0 %collective-permute-start.2 = (bf16[528,128]{1,0:T(8,128)(2,1)S(1)}, bf16[528,128]{1,0:T(8,128)(2,1)S(1)}, u32[]{:S(2)}, u32[]{:S(2)}) collective-permute-start(bf16[528,128]{1,0:T(8,128)(2,1)S(1)} %get-tuple-element.30), channel_id=1, source_target_pairs={{0,48},{16,32},{32,16},{48,0},{64,112},{80,96},{96,80},{112,64},{1... | collective-permute-start | bytes 405512 | tf_op jit(solution)/shard_map/ppermute | solution.py:353
  61.7 26.9 %collective-permute-start.3 = (bf16[528,128]{1,0:T(8,128)(2,1)S(1)}, bf16[528,128]{1,0:T(8,128)(2,1)S(1)}, u32[]{:S(2)}, u32[]{:S(2)}) collective-permute-start(bf16[528,128]{1,0:T(8,128)(2,1)S(1)} %get-tuple-element.31), channel_id=1, source_target_pairs={{0,64},{16,80},{32,96},{48,112},{64,0},{80,16},{96,32},{112,48},{1... | collective-permute-start | bytes 405512 | tf_op jit(solution)/shard_map/ppermute | solution.py:353
  63.0 25.5 %collective-permute-start.4 = (bf16[528,128]{1,0:T(8,128)(2,1)S(1)}, bf16[528,128]{1,0:T(8,128)(2,1)S(1)}, u32[]{:S(2)}, u32[]{:S(2)}) collective-permute-start(bf16[528,128]{1,0:T(8,128)(2,1)S(1)} %get-tuple-element.32), channel_id=1, source_target_pairs={{0,80},{16,64},{32,112},{48,96},{64,16},{80,0},{96,48},{112,32},{1... | collective-permute-start | bytes 405512 | tf_op jit(solution)/shard_map/ppermute | solution.py:353
  66.0 71.1 %copy-start.2 = (bf16[528,128]{1,0:T(8,128)(2,1)}, bf16[528,128]{1,0:T(8,128)(2,1)S(1)}, u32[]{:S(2)}) copy-start(bf16[528,128]{1,0:T(8,128)(2,1)S(1)} %collective-permute-done.refs_1_) | copy-start | bytes 405508
  66.0 26.8 %collective-permute-start.5 = (bf16[528,128]{1,0:T(8,128)(2,1)S(1)}, bf16[528,128]{1,0:T(8,128)(2,1)S(1)}, u32[]{:S(2)}, u32[]{:S(2)}) collective-permute-start(bf16[528,128]{1,0:T(8,128)(2,1)S(1)} %get-tuple-element.33), channel_id=1, source_target_pairs={{0,96},{16,112},{32,64},{48,80},{64,32},{80,48},{96,0},{112,16},{1... | collective-permute-start | bytes 405512 | tf_op jit(solution)/shard_map/ppermute | solution.py:353
  83.9 53.2 %copy-start.3 = (bf16[528,128]{1,0:T(8,128)(2,1)}, bf16[528,128]{1,0:T(8,128)(2,1)S(1)}, u32[]{:S(2)}) copy-start(bf16[528,128]{1,0:T(8,128)(2,1)S(1)} %collective-permute-done.1.refs_2_) | copy-start | bytes 405508
  84.0 11.7 %collective-permute-start.6 = (bf16[528,128]{1,0:T(8,128)(2,1)S(1)}, bf16[528,128]{1,0:T(8,128)(2,1)S(1)}, u32[]{:S(2)}, u32[]{:S(2)}) collective-permute-start(bf16[528,128]{1,0:T(8,128)(2,1)S(1)} %get-tuple-element.34), channel_id=1, source_target_pairs={{0,112},{16,96},{32,80},{48,64},{64,48},{80,32},{96,16},{112,0},{1... | collective-permute-start | bytes 405512 | tf_op jit(solution)/shard_map/ppermute | solution.py:353
  86.6 50.5 %copy-start.4 = (bf16[528,128]{1,0:T(8,128)(2,1)}, bf16[528,128]{1,0:T(8,128)(2,1)S(1)}, u32[]{:S(2)}) copy-start(bf16[528,128]{1,0:T(8,128)(2,1)S(1)} %collective-permute-done.2.refs_3_) | copy-start | bytes 405508
  86.6 12.1 %collective-permute-start.7 = (bf16[528,128]{1,0:T(8,128)(2,1)S(1)}, bf16[528,128]{1,0:T(8,128)(2,1)S(1)}, u32[]{:S(2)}, u32[]{:S(2)}) collective-permute-start(bf16[528,128]{1,0:T(8,128)(2,1)S(1)} %get-tuple-element.35), channel_id=1, source_target_pairs={{0,128},{16,144},{32,160},{48,176},{64,192},{80,208},{96,224},{112... | collective-permute-start | bytes 405512 | tf_op jit(solution)/shard_map/ppermute | solution.py:353
  88.5 48.6 %copy-start.5 = (bf16[528,128]{1,0:T(8,128)(2,1)}, bf16[528,128]{1,0:T(8,128)(2,1)S(1)}, u32[]{:S(2)}) copy-start(bf16[528,128]{1,0:T(8,128)(2,1)S(1)} %collective-permute-done.3.refs_4_) | copy-start | bytes 405508
  88.5 16.0 %collective-permute-start.8 = (bf16[528,128]{1,0:T(8,128)(2,1)S(1)}, bf16[528,128]{1,0:T(8,128)(2,1)S(1)}, u32[]{:S(2)}, u32[]{:S(2)}) collective-permute-start(bf16[528,128]{1,0:T(8,128)(2,1)S(1)} %get-tuple-element.36), channel_id=1, source_target_pairs={{0,144},{16,128},{32,176},{48,160},{64,208},{80,192},{96,240},{112... | collective-permute-start | bytes 405512 | tf_op jit(solution)/shard_map/ppermute | solution.py:353
  88.6 48.6 %copy-start.6 = (bf16[528,128]{1,0:T(8,128)(2,1)}, bf16[528,128]{1,0:T(8,128)(2,1)S(1)}, u32[]{:S(2)}) copy-start(bf16[528,128]{1,0:T(8,128)(2,1)S(1)} %collective-permute-done.4.refs_5_) | copy-start | bytes 405508
  88.6 23.0 %collective-permute-start.9 = (bf16[528,128]{1,0:T(8,128)(2,1)S(1)}, bf16[528,128]{1,0:T(8,128)(2,1)S(1)}, u32[]{:S(2)}, u32[]{:S(2)}) collective-permute-start(bf16[528,128]{1,0:T(8,128)(2,1)S(1)} %get-tuple-element.37), channel_id=1, source_target_pairs={{0,160},{16,176},{32,128},{48,144},{64,224},{80,240},{96,192},{112... | collective-permute-start | bytes 405512 | tf_op jit(solution)/shard_map/ppermute | solution.py:353
  92.8 44.4 %copy-start.7 = (bf16[528,128]{1,0:T(8,128)(2,1)}, bf16[528,128]{1,0:T(8,128)(2,1)S(1)}, u32[]{:S(2)}) copy-start(bf16[528,128]{1,0:T(8,128)(2,1)S(1)} %collective-permute-done.5.refs_6_) | copy-start | bytes 405508
  92.8 22.5 %collective-permute-start.10 = (bf16[528,128]{1,0:T(8,128)(2,1)S(1)}, bf16[528,128]{1,0:T(8,128)(2,1)S(1)}, u32[]{:S(2)}, u32[]{:S(2)}) collective-permute-start(bf16[528,128]{1,0:T(8,128)(2,1)S(1)} %get-tuple-element.38), channel_id=1, source_target_pairs={{0,176},{16,160},{32,144},{48,128},{64,240},{80,224},{96,208},{112... | collective-permute-start | bytes 405512 | tf_op jit(solution)/shard_map/ppermute | solution.py:353
  95.6 41.6 %copy-start.8 = (bf16[528,128]{1,0:T(8,128)(2,1)}, bf16[528,128]{1,0:T(8,128)(2,1)S(1)}, u32[]{:S(2)}) copy-start(bf16[528,128]{1,0:T(8,128)(2,1)S(1)} %collective-permute-done.6.refs_7_) | copy-start | bytes 405508
  95.6 24.9 %collective-permute-start.11 = (bf16[528,128]{1,0:T(8,128)(2,1)S(1)}, bf16[528,128]{1,0:T(8,128)(2,1)S(1)}, u32[]{:S(2)}, u32[]{:S(2)}) collective-permute-start(bf16[528,128]{1,0:T(8,128)(2,1)S(1)} %get-tuple-element.39), channel_id=1, source_target_pairs={{0,192},{16,208},{32,224},{48,240},{64,128},{80,144},{96,160},{112... | collective-permute-start | bytes 405512 | tf_op jit(solution)/shard_map/ppermute | solution.py:353
  98.8 38.5 %copy-start.9 = (bf16[528,128]{1,0:T(8,128)(2,1)}, bf16[528,128]{1,0:T(8,128)(2,1)S(1)}, u32[]{:S(2)}) copy-start(bf16[528,128]{1,0:T(8,128)(2,1)S(1)} %collective-permute-done.7.refs_8_) | copy-start | bytes 405508
  98.8 27.1 %collective-permute-start.12 = (bf16[528,128]{1,0:T(8,128)(2,1)S(1)}, bf16[528,128]{1,0:T(8,128)(2,1)S(1)}, u32[]{:S(2)}, u32[]{:S(2)}) collective-permute-start(bf16[528,128]{1,0:T(8,128)(2,1)S(1)} %get-tuple-element.40), channel_id=1, source_target_pairs={{0,208},{16,192},{32,240},{48,224},{64,144},{80,128},{96,176},{112... | collective-permute-start | bytes 405512 | tf_op jit(solution)/shard_map/ppermute | solution.py:353
  104.5 32.7 %copy-start.10 = (bf16[528,128]{1,0:T(8,128)(2,1)}, bf16[528,128]{1,0:T(8,128)(2,1)S(1)}, u32[]{:S(2)}) copy-start(bf16[528,128]{1,0:T(8,128)(2,1)S(1)} %collective-permute-done.8.refs_9_) | copy-start | bytes 405508
  104.5 28.5 %collective-permute-start.13 = (bf16[528,128]{1,0:T(8,128)(2,1)S(1)}, bf16[528,128]{1,0:T(8,128)(2,1)S(1)}, u32[]{:S(2)}, u32[]{:S(2)}) collective-permute-start(bf16[528,128]{1,0:T(8,128)(2,1)S(1)} %get-tuple-element.41), channel_id=1, source_target_pairs={{0,224},{16,240},{32,192},{48,208},{64,160},{80,176},{96,128},{112... | collective-permute-start | bytes 405512 | tf_op jit(solution)/shard_map/ppermute | solution.py:353
  111.6 25.6 %copy-start.11 = (bf16[528,128]{1,0:T(8,128)(2,1)}, bf16[528,128]{1,0:T(8,128)(2,1)S(1)}, u32[]{:S(2)}) copy-start(bf16[528,128]{1,0:T(8,128)(2,1)S(1)} %collective-permute-done.9.refs_10_) | copy-start | bytes 405508
  111.6 25.5 %collective-permute-start.14 = (bf16[528,128]{1,0:T(8,128)(2,1)S(1)}, bf16[528,128]{1,0:T(8,128)(2,1)S(1)}, u32[]{:S(2)}, u32[]{:S(2)}) collective-permute-start(bf16[528,128]{1,0:T(8,128)(2,1)S(1)} %get-tuple-element.42), channel_id=1, source_target_pairs={{0,240},{16,224},{32,208},{48,192},{64,176},{80,160},{96,144},{112... | collective-permute-start | bytes 405512 | tf_op jit(solution)/shard_map/ppermute | solution.py:353
  115.4 21.9 %copy-start.12 = (bf16[528,128]{1,0:T(8,128)(2,1)}, bf16[528,128]{1,0:T(8,128)(2,1)S(1)}, u32[]{:S(2)}) copy-start(bf16[528,128]{1,0:T(8,128)(2,1)S(1)} %collective-permute-done.10.refs_11_) | copy-start | bytes 405508
  120.5 16.8 %copy-start.13 = (bf16[528,128]{1,0:T(8,128)(2,1)}, bf16[528,128]{1,0:T(8,128)(2,1)S(1)}, u32[]{:S(2)}) copy-start(bf16[528,128]{1,0:T(8,128)(2,1)S(1)} %collective-permute-done.11.refs_12_) | copy-start | bytes 405508
  125.8 11.4 %copy-start.14 = (bf16[528,128]{1,0:T(8,128)(2,1)}, bf16[528,128]{1,0:T(8,128)(2,1)S(1)}, u32[]{:S(2)}) copy-start(bf16[528,128]{1,0:T(8,128)(2,1)S(1)} %collective-permute-done.12.refs_13_) | copy-start | bytes 405508
  133.0 4.3 %copy-start.15 = (bf16[528,128]{1,0:T(8,128)(2,1)}, bf16[528,128]{1,0:T(8,128)(2,1)S(1)}, u32[]{:S(2)}) copy-start(bf16[528,128]{1,0:T(8,128)(2,1)S(1)} %collective-permute-done.13.refs_14_) | copy-start | bytes 405508
  137.2 0.7 copy-start.16
  171.9 5.2 %copy-start.1 = (s32[16,256]{1,0:T(8,128)S(1)}, s32[16,256]{1,0:T(8,128)}, u32[]{:S(2)}) copy-start(s32[16,256]{1,0:T(8,128)} %get-tuple-element.25) | copy-start | bytes 49156
  171.9 59.5 %all-to-all-start.2 = ((bf16[256,32,128]{2,1,0:T(8,128)(2,1)}), bf16[256,32,128]{2,1,0:T(8,128)(2,1)S(1)}, u32[]{:S(2)}, u32[]{:S(2)}) async-start(bf16[256,32,128]{2,1,0:T(8,128)(2,1)} %shard_map.68), calls=%async_computation.2 | async-start | bytes 4194304 | tf_op jit(solution)/shard_map/all_to_all | solution.py:390

commit v4 on v3

--- a/solution.py
+++ b/solution.py
@@ -17,6 +17,7 @@
 NEG = -1e30
 LOG2E = 1.4426950408889634
 HALF = 8
+PIECES = 4
 
 
 def iota(shape, axis):
@@ -33,12 +34,20 @@
 
 def matmul_nt(a, b):
     return lax.dot_general(a, b, NT, preferred_element_type=jnp.float32)
+
+
+def over(x, size):
+    return x >> (size.bit_length() - 1)
+
+
+def rest(x, size):
+    return x & (size - 1)
 
 
 def swap_matrix(major, minor, unit):
     total = major * minor * unit
     row, column = iota((total, total), 0), iota((total, total), 1)
-    b, a, u = row // (major * unit), (row // unit) % major, row % unit
+    b, a, u = over(row, major * unit), rest(over(row, unit), major), rest(row, unit)
     return one_hot(column == (a * minor + b) * unit + u)
 
 
@@ -55,19 +64,15 @@
 
 def pack_kernel(label_ref, key_scale_ref, value_scale_ref, q_ref, out_ref):
     rows, heads, width = q_ref.shape
-    halves = rows // width
-    for h in range(heads):
-        kinds = (
-            label_ref[h].astype(jnp.float32),
-            key_scale_ref[h : h + 1, :].astype(jnp.float32),
-            value_scale_ref[h : h + 1, :].astype(jnp.float32),
-        )
-        meta = jnp.concatenate(
-            [kind[:, n * width : (n + 1) * width] for kind in kinds for n in range(halves)]
-            + [jnp.zeros((META - 3 * halves, width), jnp.float32)],
-            axis=0,
-        )
-        out_ref[h, rows : rows + META, :] = meta.astype(jnp.bfloat16)
+    kinds = (label_ref[:, 0, :].astype(jnp.float32), key_scale_ref[...], value_scale_ref[...])
+    meta = [
+        kind[:, n * width : (n + 1) * width].astype(jnp.bfloat16)
+        for kind in kinds
+        for n in range(rows // width)
+    ]
+    meta.append(jnp.zeros(((META - len(meta)) * heads, width), jnp.bfloat16))
+    turned = matmul(swap_matrix(META, heads, 1), jnp.concatenate(meta, axis=0))
+    out_ref[:, rows : rows + META, :] = turned.astype(jnp.bfloat16).reshape(heads, META, width)
     group = 256 // heads
     swap = swap_matrix(group, heads, 1)
     for g in range(rows // group):
@@ -123,8 +128,8 @@
             for n in range(3)
         )
         slot = slot_of(label.astype(jnp.int32), before)
-        owner = (slot // CHUNK) ^ me
-        here = slot % CHUNK
+        owner = over(slot, CHUNK) ^ me
+        here = rest(slot, CHUNK)
         pick = one_hot(iota((SLOTS, rows), 0) == owner * CHUNK + here)
         placed = matmul(pick, in_ref[s, :rows, :]).astype(jnp.bfloat16)
         table[:, s] = placed.reshape(COARSE, CHUNK, width)
@@ -177,122 +182,125 @@
         scale_rows[pl.ds(pl.multiple_of(source * blocks, blocks), blocks), :] = part[
             FINE * slab :, :
         ]
-    spread = one_hot(iota((total, sources), 0) // CAP == iota((total, sources), 1))
+    spread = one_hot(over(iota((total, sources), 0), CAP) == iota((total, sources), 1))
     table = matmul(spread, scale_rows[...])
     lane, row = iota((total, 128), 1), iota((total, 128), 0)
-    table = jnp.where(lane % CAP == row % CAP, table, 0.0).astype(jnp.bfloat16)
-    gather = one_hot(iota((2 * FINE, 128), 0) == iota((2 * FINE, 128), 1) // CAP)
+    table = jnp.where(rest(lane, CAP) == rest(row, CAP), table, 0.0).astype(jnp.bfloat16)
+    gather = one_hot(iota((2 * FINE, 128), 0) == over(iota((2 * FINE, 128), 1), CAP))
     scales[...] = matmul_nt(gather, table)
 
 
-PIECES = 4
-
-
-def attend_kernel(arrived_ref, qs, scales, out_ref, message, kvs, os, sems):
-    f = pl.program_id(0)
+def attend_kernel(arrived_ref, q_ref, scales, out_ref, message, qs, kvs, os, result, sems):
     sources, _, width = message.shape
     width = width // 2
-    total = sources * CAP
+    piece = sources // PIECES
+    tile = piece * CAP
     batch = 256 // CHUNK
     unit = batch * CAP
 
-    @pl.when(f == 0)
-    def _():
-        piece = sources // PIECES
-        copies = [
-            pltpu.make_async_copy(
-                arrived_ref.at[pl.ds(n * piece, piece)],
-                message.at[pl.ds(n * piece, piece)],
-                sems.at[n],
-            )
-            for n in range(PIECES)
-        ]
-        for copy in copies:
-            copy.start()
-        swap = swap_matrix(batch, FINE, CAP)
-        for n in range(PIECES):
-            copies[n].wait()
-            for g in range(n * piece // batch, (n + 1) * piece // batch):
-                block = message[g * batch : (g + 1) * batch].reshape(256, 2 * width)
-                turned = matmul(swap, block).astype(jnp.bfloat16)
-                kvs[:, g * unit : (g + 1) * unit, :] = turned.reshape(FINE, unit, 2 * width)
-
-    key_scale = scales[pl.ds(f, 1), :]
-    value_scale = scales[pl.ds(FINE + f, 1), :]
-    factor = key_scale * (width**-0.5 * LOG2E)
-    bias = jnp.where(key_scale > 0.0, 0.0, NEG)
-    tile = 256
+    def rows(n, size):
+        return slice(n * size, (n + 1) * size)
+
+    def message_in(n):
+        here = pl.ds(n * piece, piece)
+        return pltpu.make_async_copy(arrived_ref.at[here], message.at[here], sems.at[0, n])
+
+    def queries_in(n):
+        here = pl.ds(n * tile, tile)
+        return pltpu.make_async_copy(q_ref.at[:, here], qs.at[:, here], sems.at[1, n])
+
+    def result_out(n):
+        here = pl.ds(n * piece, piece)
+        return pltpu.make_async_copy(result.at[here], out_ref.at[here], sems.at[2, n])
+
+    for n in range(PIECES):
+        message_in(n).start()
+        queries_in(n).start()
+    turn_in = swap_matrix(batch, FINE, CAP)
+    turn_out = swap_matrix(FINE, batch, CAP)
     ahead = iota((tile, tile), 1) > iota((tile, tile), 0)
-    for t in range(total // tile):
-        here = slice(t * tile, (t + 1) * tile)
-        query = qs[0, here, :]
-        pieces = []
-        for u in range(t + 1):
-            there = slice(u * tile, (u + 1) * tile)
-            score = matmul_nt(query, kvs[f, there, :width])
-            score = score * factor[:, there] + bias[:, there]
-            if u == t:
-                score = jnp.where(ahead, NEG, score)
-            pieces.append(score)
-        highest = pieces[0]
-        for piece in pieces[1:]:
-            highest = jnp.maximum(highest, piece)
-        highest = jnp.max(highest, axis=1, keepdims=True)
-        below, result = None, None
-        for u, piece in enumerate(pieces):
-            there = slice(u * tile, (u + 1) * tile)
-            unnormed = jnp.exp2(piece - highest)
-            weights = (unnormed * value_scale[:, there]).astype(jnp.bfloat16)
-            term = matmul(weights, kvs[f, there, width:])
-            below = unnormed if below is None else below + unnormed
-            result = term if result is None else result + term
-        below = jnp.sum(below, axis=1, keepdims=True)
-        os[f, here, :] = (result / below).astype(jnp.bfloat16)
-
-    @pl.when(f == FINE - 1)
-    def _():
-        swap = swap_matrix(FINE, batch, CAP)
-
-        def turn(g, carry):
-            block = os[:, pl.ds(pl.multiple_of(g * unit, unit), unit), :].reshape(256, width)
-            turned = matmul(swap, block).astype(jnp.bfloat16)
-            out_ref[pl.ds(g * batch, batch)] = turned.reshape(batch, CHUNK, width)
+    for t in range(PIECES):
+        message_in(t).wait()
+        for g in range(t * piece // batch, (t + 1) * piece // batch):
+            block = message[rows(g, batch)].reshape(256, 2 * width)
+            turned = matmul(turn_in, block).astype(jnp.bfloat16)
+            kvs[:, rows(g, unit), :] = turned.reshape(FINE, unit, 2 * width)
+        queries_in(t).wait()
+
+        def one(f, carry):
+            key_scale = scales[pl.ds(f, 1), :]
+            value_scale = scales[pl.ds(FINE + f, 1), :]
+            factor = key_scale * (width**-0.5 * LOG2E)
+            bias = jnp.where(key_scale > 0.0, 0.0, NEG)
+            query = qs[f, rows(t, tile), :]
+            pieces = []
+            for u in range(t + 1):
+                there = rows(u, tile)
+                score = matmul_nt(query, kvs[f, there, :width])
+                score = score * factor[:, there] + bias[:, there]
+                if u == t:
+                    score = jnp.where(ahead, NEG, score)
+                pieces.append(score)
+            highest = pieces[0]
+            for score in pieces[1:]:
+                highest = jnp.maximum(highest, score)
+            highest = jnp.max(highest, axis=1, keepdims=True)
+            below, total = None, None
+            for u, score in enumerate(pieces):
+                there = rows(u, tile)
+                unnormed = jnp.exp2(score - highest)
+                weights = (unnormed * value_scale[:, there]).astype(jnp.bfloat16)
+                term = matmul(weights, kvs[f, there, width:])
+                below = unnormed if below is None else below + unnormed
+                total = term if total is None else total + term
+            below = jnp.sum(below, axis=1, keepdims=True)
+            os[f] = (total / below).astype(jnp.bfloat16)
             return carry
 
-        lax.fori_loop(0, sources // batch, turn, 0, unroll=8)
-
-
-def unplace_kernel(slot_ref, arrived_ref, out_ref, by_head, answer, sems):
-    step = pl.program_id(0)
-    rows = slot_ref.shape[0]
-    width = out_ref.shape[2]
-
-    def copy(n):
+        lax.fori_loop(0, FINE, one, 0, unroll=FINE)
+        for g in range(piece // batch):
+            block = os[:, rows(g, unit), :].reshape(256, width)
+            turned = matmul(turn_out, block).astype(jnp.bfloat16)
+            result[rows(t * (piece // batch) + g, batch)] = turned.reshape(batch, CHUNK, width)
+        result_out(t).start()
+    for n in range(PIECES):
+        result_out(n).wait()
+
+
+def unplace_kernel(slot_ref, arrived_ref, out_ref, answer, by_head, result, sems):
+    rows, heads, width = result.shape
+    some = heads // PIECES
+    piece = rows // PIECES
+    group = 256 // heads
+
+    def answer_in(n):
+        here = pl.ds(n * some, some)
         return pltpu.make_async_copy(
-            arrived_ref.at[:, pl.ds(n * HALF, HALF)], answer.at[n], sems.at[n]
-        )
-
-    @pl.when(step == 0)
-    def _():
-        for n in range(answer.shape[0]):
-            copy(n).start()
-
-    copy(step).wait()
-    in_ref = answer.at[step]
-    group = 256 // HALF
-    swap = swap_matrix(HALF, group, 1)
-    lane = iota(slot_ref.shape, 1)
-    for h in range(HALF):
-        slot = jnp.sum(
-            jnp.where(lane == step * HALF + h, slot_ref[...], 0), axis=1, keepdims=True
-        )
-        pick = one_hot(iota((rows, SLOTS), 1) == slot)
-        by_head[h] = matmul(pick, in_ref[:, h].reshape(SLOTS, width)).astype(jnp.bfloat16)
-    for g in range(rows // group):
-        block = by_head[:, g * group : (g + 1) * group, :].reshape(256, width)
-        out_ref[g * group : (g + 1) * group] = (
-            matmul(swap, block).astype(jnp.bfloat16).reshape(group, HALF, width)
-        )
+            arrived_ref.at[:, here], answer.at[:, here], sems.at[0, n]
+        )
+
+    def result_out(n):
+        here = pl.ds(n * piece, piece)
+        return pltpu.make_async_copy(result.at[here], out_ref.at[here], sems.at[1, n])
+
+    for n in range(PIECES):
+        answer_in(n).start()
+    place = iota((rows, SLOTS), 1)
+    swap = swap_matrix(heads, group, 1)
+    for h in range(heads):
+        if h % some == 0:
+            answer_in(h // some).wait()
+        pick = one_hot(place == slot_ref[:, h : h + 1])
+        block = answer[:, h].reshape(SLOTS, width)
+        by_head[h] = matmul(pick, block).astype(jnp.bfloat16)
+    for n in range(PIECES):
+        for g in range(n * piece // group, (n + 1) * piece // group):
+            here = slice(g * group, (g + 1) * group)
+            block = by_head[:, here, :].reshape(256, width)
+            result[here] = matmul(swap, block).astype(jnp.bfloat16).reshape(group, heads, width)
+        result_out(n).start()
+    for n in range(PIECES):
+        result_out(n).wait()
 
 
 def shards(queries, key_rows, value_rows, key_scale, value_scale, cluster_label):
@@ -369,19 +377,16 @@
     )(me, *parts)
     answer = pl.pallas_call(
         attend_kernel,
-        grid=(FINE,),
-        in_specs=[
-            anywhere,
-            pl.BlockSpec((1, total, width), lambda i: (i, 0, 0)),
-            pl.BlockSpec((2 * FINE, total), lambda i: (0, 0)),
-        ],
-        out_specs=pl.BlockSpec((devices, CHUNK, width), lambda i: (0, 0, 0)),
+        in_specs=[anywhere, anywhere, pl.BlockSpec(memory_space=pltpu.VMEM)],
+        out_specs=anywhere,
         out_shape=jax.ShapeDtypeStruct((devices, CHUNK, width), bf16),
         scratch_shapes=[
             pltpu.VMEM((devices, CHUNK, 2 * width), bf16),
+            pltpu.VMEM((FINE, total, width), bf16),
             pltpu.VMEM((FINE, total, 2 * width), bf16),
-            pltpu.VMEM((FINE, total, width), bf16),
-            pltpu.SemaphoreType.DMA((PIECES,)),
+            pltpu.VMEM((FINE, total // PIECES, width), bf16),
+            pltpu.VMEM((devices, CHUNK, width), bf16),
+            pltpu.SemaphoreType.DMA((3, PIECES)),
         ],
         cost_estimate=pl.CostEstimate(
             flops=4 * 10**9, bytes_accessed=8 * 2**20, transcendentals=5 * 10**6
@@ -391,17 +396,14 @@
 
     return pl.pallas_call(
         unplace_kernel,
-        grid=(heads // HALF,),
-        in_specs=[
-            pl.BlockSpec((rows, heads), lambda i: (0, 0)),
-            anywhere,
-        ],
-        out_specs=pl.BlockSpec((rows, HALF, width), lambda i: (0, i, 0)),
+        in_specs=[pl.BlockSpec(memory_space=pltpu.VMEM), anywhere],
+        out_specs=anywhere,
         out_shape=jax.ShapeDtypeStruct((rows, heads, width), bf16),
         scratch_shapes=[
-            pltpu.VMEM((HALF, rows, width), bf16),
-            pltpu.VMEM((heads // HALF, COARSE, HALF, CHUNK, width), bf16),
-            pltpu.SemaphoreType.DMA((heads // HALF,)),
+            pltpu.VMEM((COARSE, heads, CHUNK, width), bf16),
+            pltpu.VMEM((heads, rows, width), bf16),
+            pltpu.VMEM((rows, heads, width), bf16),
+            pltpu.SemaphoreType.DMA((2, PIECES)),
         ],
         compiler_params=pltpu.CompilerParams(vmem_limit_bytes=24 * 2**20),
         cost_estimate=pl.CostEstimate(

time: 235 us -> 232 us (0.987)
  starting transfers between devices: 52.5 us -> 60.5 us
  waiting for transfers between devices: 138 us -> 130 us
  Pallas kernels: 42.5 us -> 38.8 us
    ppermute x15, waiting for transfers between devices: 52.2 us -> 44.2 us  [shards(): lax.ppermute(parts[d], 'outer', [(n, n ^ d) for n in range(outer)])]
    ppermute x15, starting transfers between devices: 27.1 us -> 35.1 us  [shards(): lax.ppermute(parts[d], 'outer', [(n, n ^ d) for n in range(outer)])]
    pallas_call x2, Pallas kernels: 24.7 us -> 21.1 us  [the longest x1 17.5 us: shards(): pl.pallas_call(attend_kernel, in_specs=[anywhere, anywhere, pl.BlockSpec(...]
where the time goes in v4:
time: 232 us; the launch traced here: 231 us
  waiting for transfers between devices  130 us (56%)
  starting transfers between devices  60.5 us (26%)
  Pallas kernels  38.8 us (17%)
    all_to_all x1, waiting for transfers between devices, shards(): answer = lax.all_to_all(answer, BOTH, 0, 0, tiled=True)  54.1 us
    ppermute x15, waiting for transfers between devices, shards(): lax.ppermute(parts[d], 'outer', [(n, n ^ d) for n in range(outer)])  44.2 us
    ppermute x15, starting transfers between devices, shards(): lax.ppermute(parts[d], 'outer', [(n, n ^ d) for n in range(outer)])  35.1 us
    all_to_all x1, waiting for transfers between devices, shards(): packed = lax.all_to_all(packed, 'inner', 0, 0, tiled=True)  22.6 us
    pallas_call x1, Pallas kernels, shards(): pl.pallas_call(attend_kernel, in_specs=[anywhere, anywhere, pl.BlockSpec(...  17.5 us
    all_to_all x1, starting transfers between devices, shards(): message = lax.all_to_all(message, BOTH, 0, 0, tiled=True)  10.2 us
    all_to_all x1, starting transfers between devices, shards(): packed = lax.all_to_all(packed, 'inner', 0, 0, tiled=True)  9.98 us
    all_to_all x1, waiting for transfers between devices, shards(): message = lax.all_to_all(message, BOTH, 0, 0, tiled=True)  9.47 us
  transfers between devices with their start and end apart: 18, of which 13 were waited for; matrix products, arithmetic and copies ran while one was open for 0% of the time, Pallas kernels for 6%

profile of v4, /device:TPU:1, one launch (start us, length us, event | category | flops | bytes accessed | tf_op | source)
XLA Modules:
  0.0 231.5 jit_solution(15678232320409856041)
XLA Ops:
  0.0 3.0 %shard_map.65 = bf16[16,264,128]{2,1,0:T(8,128)(2,1)} custom-call(s32[16,1,256]{2,1,0:T(1,128)} %bitcast.10, bf16[16,256]{1,0:T(8,128)(2,1)} %bitcast.12, bf16[16,256]{1,0:T(8,128)(2,1)} %bitcast.13, bf16[256,16,128]{2,1,0:T(8,128)(2,1)} %q_ref.1), custom_call_target="tpu_custom_call" | custom-call | flops 1000000000 | bytes 2097152 | tf_op jit(solution)/shard_map/pallas_call | solution.py:316
  3.0 10.0 %all-to-all-start.1 = ((bf16[16,264,128]{2,1,0:T(8,128)(2,1)}), bf16[16,264,128]{2,1,0:T(8,128)(2,1)S(1)}, u32[]{:S(2)}, u32[]{:S(2)}) async-start(bf16[16,264,128]{2,1,0:T(8,128)(2,1)} %shard_map.65), calls=%async_computation.1 | async-start | bytes 2162688 | tf_op jit(solution)/shard_map/all_to_all | solution.py:321
  13.0 6.0 %shard_map.64 = (s32[16,256]{1,0:T(8,128)}, bf16[16,16,32,256]{3,2,1,0:T(8,128)(2,1)}) custom-call(s32[16,1,256]{2,1,0:T(1,128)} %bitcast.11, bf16[256,16,128]{2,1,0:T(8,128)(2,1)} %k_ref.1, bf16[256,16,128]{2,1,0:T(8,128)(2,1)} %v_ref.1), custom_call_target="tpu_custom_call" | custom-call | flops 3000000000 | bytes 6291456 | tf_op jit(solution)/shard_map/pallas_call | solution.py:324
  19.0 22.6 %all-to-all-done.1.arrived_ref = bf16[16,264,128]{2,1,0:T(8,128)(2,1)S(1)} async-done(((bf16[16,264,128]{2,1,0:T(8,128)(2,1)}), bf16[16,264,128]{2,1,0:T(8,128)(2,1)S(1)}, u32[]{:S(2)}, u32[]{:S(2)}) %all-to-all-start.1) | async-done | bytes 1081376 | tf_op jit(solution)/shard_map/all_to_all | solution.py:321
  41.6 10.2 %all-to-all-start = ((bf16[256,32,256]{2,1,0:T(8,128)(2,1)}), bf16[256,32,256]{2,1,0:T(8,128)(2,1)}, u32[]{:S(2)}, u32[]{:S(2)}) async-start(bf16[256,32,256]{2,1,0:T(8,128)(2,1)} %bitcast.9), calls=%async_computation | async-start | bytes 8388608 | tf_op jit(solution)/shard_map/all_to_all | solution.py:342
  51.9 5.2 %shard_map.66 = (bf16[528,128]{1,0:T(8,128)(2,1)S(1)}, bf16[528,128]{1,0:T(8,128)(2,1)S(1)}, bf16[528,128]{1,0:T(8,128)(2,1)S(1)}, bf16[528,128]{1,0:T(8,128)(2,...) custom-call(s32[1]{0:T(128)} %bitcast.3.me_ref, ...), custom_call_target="tpu_custom_call" | custom-call | flops 2000000000 | bytes 3145728 | tf_op jit(solution)/shard_map/pallas_call | solution.py:345
  57.1 0.0 copy-start
  57.1 0.6 copy-done
  57.7 1.4 collective-permute-start
  59.1 2.4 %collective-permute-start.1 = (bf16[528,128]{1,0:T(8,128)(2,1)S(1)}, bf16[528,128]{1,0:T(8,128)(2,1)S(1)}, u32[]{:S(2)}, u32[]{:S(2)}) collective-permute-start(bf16[528,128]{1,0:T(8,128)(2,1)S(1)} %get-tuple-element.29), channel_id=1, source_target_pairs={{0,32},{16,48},{32,0},{48,16},{64,96},{80,112},{96,64},{112,80},{1... | collective-permute-start | bytes 405512 | tf_op jit(solution)/shard_map/ppermute | solution.py:361
  61.6 0.0 collective-permute-start.2
  61.6 1.4 collective-permute-start.3
  63.0 0.0 collective-permute-start.4
  63.0 3.2 %collective-permute-done.refs_1_ = bf16[528,128]{1,0:T(8,128)(2,1)S(1)} collective-permute-done((bf16[528,128]{1,0:T(8,128)(2,1)S(1)}, bf16[528,128]{1,0:T(8,128)(2,1)S(1)}, u32[]{:S(2)}, u32[]{:S(2)}) %collective-permute-start) | collective-permute-done | bytes 135200 | tf_op jit(solution)/shard_map/ppermute | solution.py:361
  66.2 0.0 copy-start.2
  66.2 4.5 %collective-permute-start.5 = (bf16[528,128]{1,0:T(8,128)(2,1)S(1)}, bf16[528,128]{1,0:T(8,128)(2,1)S(1)}, u32[]{:S(2)}, u32[]{:S(2)}) collective-permute-start(bf16[528,128]{1,0:T(8,128)(2,1)S(1)} %get-tuple-element.33), channel_id=1, source_target_pairs={{0,96},{16,112},{32,64},{48,80},{64,32},{80,48},{96,0},{112,16},{1... | collective-permute-start | bytes 405512 | tf_op jit(solution)/shard_map/ppermute | solution.py:361
  70.7 13.4 %collective-permute-done.1.refs_2_ = bf16[528,128]{1,0:T(8,128)(2,1)S(1)} collective-permute-done((bf16[528,128]{1,0:T(8,128)(2,1)S(1)}, bf16[528,128]{1,0:T(8,128)(2,1)S(1)}, u32[]{:S(2)}, u32[]{:S(2)}) %collective-permute-start.1) | collective-permute-done | bytes 135200 | tf_op jit(solution)/shard_map/ppermute | solution.py:361
  84.1 2.5 %collective-permute-start.6 = (bf16[528,128]{1,0:T(8,128)(2,1)S(1)}, bf16[528,128]{1,0:T(8,128)(2,1)S(1)}, u32[]{:S(2)}, u32[]{:S(2)}) collective-permute-start(bf16[528,128]{1,0:T(8,128)(2,1)S(1)} %get-tuple-element.34), channel_id=1, source_target_pairs={{0,112},{16,96},{32,80},{48,64},{64,48},{80,32},{96,16},{112,0},{1... | collective-permute-start | bytes 405512 | tf_op jit(solution)/shard_map/ppermute | solution.py:361
  86.6 0.0 collective-permute-done.2.refs_3_
  86.6 1.6 collective-permute-start.7
  88.3 0.0 collective-permute-done.3.refs_4_
  88.3 0.0 collective-permute-start.8
  88.3 0.0 collective-permute-done.4.refs_5_
  88.3 0.0 copy-start.6
  88.3 4.6 %collective-permute-start.9 = (bf16[528,128]{1,0:T(8,128)(2,1)S(1)}, bf16[528,128]{1,0:T(8,128)(2,1)S(1)}, u32[]{:S(2)}, u32[]{:S(2)}) collective-permute-start(bf16[528,128]{1,0:T(8,128)(2,1)S(1)} %get-tuple-element.37), channel_id=1, source_target_pairs={{0,160},{16,176},{32,128},{48,144},{64,224},{80,240},{96,192},{112... | collective-permute-start | bytes 405512 | tf_op jit(solution)/shard_map/ppermute | solution.py:361
  92.9 0.0 collective-permute-done.5.refs_6_
  93.0 2.7 %collective-permute-start.10 = (bf16[528,128]{1,0:T(8,128)(2,1)S(1)}, bf16[528,128]{1,0:T(8,128)(2,1)S(1)}, u32[]{:S(2)}, u32[]{:S(2)}) collective-permute-start(bf16[528,128]{1,0:T(8,128)(2,1)S(1)} %get-tuple-element.38), channel_id=1, source_target_pairs={{0,176},{16,160},{32,144},{48,128},{64,240},{80,224},{96,208},{112... | collective-permute-start | bytes 405512 | tf_op jit(solution)/shard_map/ppermute | solution.py:361
  95.6 0.0 collective-permute-done.6.refs_7_
  95.6 0.5 collective-permute-start.11
  96.1 2.6 %collective-permute-done.7.refs_8_ = bf16[528,128]{1,0:T(8,128)(2,1)S(1)} collective-permute-done((bf16[528,128]{1,0:T(8,128)(2,1)S(1)}, bf16[528,128]{1,0:T(8,128)(2,1)S(1)}, u32[]{:S(2)}, u32[]{:S(2)}) %collective-permute-start.7) | collective-permute-done | bytes 135200 | tf_op jit(solution)/shard_map/ppermute | solution.py:361
  98.7 1.3 collective-permute-start.12
  100.1 0.8 collective-permute-done.8.refs_9_
  100.8 5.7 %collective-permute-start.13 = (bf16[528,128]{1,0:T(8,128)(2,1)S(1)}, bf16[528,128]{1,0:T(8,128)(2,1)S(1)}, u32[]{:S(2)}, u32[]{:S(2)}) collective-permute-start(bf16[528,128]{1,0:T(8,128)(2,1)S(1)} %get-tuple-element.41), channel_id=1, source_target_pairs={{0,224},{16,240},{32,192},{48,208},{64,160},{80,176},{96,128},{112... | collective-permute-start | bytes 405512 | tf_op jit(solution)/shard_map/ppermute | solution.py:361
  106.6 1.0 collective-permute-done.9.refs_10_
  107.5 6.3 %collective-permute-start.14 = (bf16[528,128]{1,0:T(8,128)(2,1)S(1)}, bf16[528,128]{1,0:T(8,128)(2,1)S(1)}, u32[]{:S(2)}, u32[]{:S(2)}) collective-permute-start(bf16[528,128]{1,0:T(8,128)(2,1)S(1)} %get-tuple-element.42), channel_id=1, source_target_pairs={{0,240},{16,224},{32,208},{48,192},{64,176},{80,160},{96,144},{112... | collective-permute-start | bytes 405512 | tf_op jit(solution)/shard_map/ppermute | solution.py:361
  113.8 0.9 collective-permute-done.10.refs_11_
  114.8 5.6 %collective-permute-done.11.refs_12_ = bf16[528,128]{1,0:T(8,128)(2,1)S(1)} collective-permute-done((bf16[528,128]{1,0:T(8,128)(2,1)S(1)}, bf16[528,128]{1,0:T(8,128)(2,1)S(1)}, u32[]{:S(2)}, u32[]{:S(2)}) %collective-permute-start.11) | collective-permute-done | bytes 135200 | tf_op jit(solution)/shard_map/ppermute | solution.py:361
  120.4 2.4 %collective-permute-done.12.refs_13_ = bf16[528,128]{1,0:T(8,128)(2,1)S(1)} collective-permute-done((bf16[528,128]{1,0:T(8,128)(2,1)S(1)}, bf16[528,128]{1,0:T(8,128)(2,1)S(1)}, u32[]{:S(2)}, u32[]{:S(2)}) %collective-permute-start.12) | collective-permute-done | bytes 135200 | tf_op jit(solution)/shard_map/ppermute | solution.py:361
  122.7 8.7 %collective-permute-done.13.refs_14_ = bf16[528,128]{1,0:T(8,128)(2,1)S(1)} collective-permute-done((bf16[528,128]{1,0:T(8,128)(2,1)S(1)}, bf16[528,128]{1,0:T(8,128)(2,1)S(1)}, u32[]{:S(2)}, u32[]{:S(2)}) %collective-permute-start.13) | collective-permute-done | bytes 135200 | tf_op jit(solution)/shard_map/ppermute | solution.py:361
  131.4 5.6 %collective-permute-done.14.refs_15_ = bf16[528,128]{1,0:T(8,128)(2,1)S(1)} collective-permute-done((bf16[528,128]{1,0:T(8,128)(2,1)S(1)}, bf16[528,128]{1,0:T(8,128)(2,1)S(1)}, u32[]{:S(2)}, u32[]{:S(2)}) %collective-permute-start.14) | collective-permute-done | bytes 135200 | tf_op jit(solution)/shard_map/ppermute | solution.py:361
  137.0 0.0 copy-done.2
  137.0 0.0 copy-done.3
  137.0 0.0 copy-done.4
  137.0 0.0 copy-done.5
  137.0 0.0 copy-done.6
  137.0 0.0 copy-done.7
  137.1 0.0 copy-done.8
  137.1 0.0 copy-done.9
  137.1 0.0 copy-done.10
  137.1 0.0 copy-done.11
  137.1 0.0 copy-done.12
  137.1 0.0 copy-done.13
  137.1 0.0 copy-done.14
  137.1 0.0 copy-done.15
  137.1 0.5 copy-done.16
  137.7 3.5 %shard_map.67 = (bf16[8,1024,128]{2,1,0:T(8,128)(2,1)}, f32[16,1024]{1,0:T(8,128)}) custom-call(s32[1]{0:T(128)} %bitcast.3.me_ref, bf16[528,128]{1,0:T(8,128)(2,1)} %copy-done, bf16[528,128]{1,0:T(8,128)(2,1)} %copy-done.2, bf16[528,128]{1,0:T(8,128)(2,1)} %copy-done.3, bf16[528,128]{1,0:T(8,128)(2,1)} %copy-done.4, bf16[528,128]{1,0:T(8,128)(2,1)} %copy-done.5, ...), custom_call_target="tpu_custom_call" | custom-call | flops 1000000000 | bytes 4194304 | tf_op jit(solution)/shard_map/pallas_call | solution.py:366
  141.2 9.5 %all-to-all-done.arrived_ref = bf16[256,32,256]{2,1,0:T(8,128)(2,1)} async-done(((bf16[256,32,256]{2,1,0:T(8,128)(2,1)}), bf16[256,32,256]{2,1,0:T(8,128)(2,1)}, u32[]{:S(2)}, u32[]{:S(2)}) %all-to-all-start) | async-done | bytes 4194336 | tf_op jit(solution)/shard_map/all_to_all | solution.py:342
  150.7 17.5 %shard_map.68 = bf16[256,32,128]{2,1,0:T(8,128)(2,1)} custom-call(bf16[256,32,256]{2,1,0:T(8,128)(2,1)} %all-to-all-done.arrived_ref, bf16[8,1024,128]{2,1,0:T(8,128)(2,1)} %get-tuple-element.43.q_ref, f32[16,1024]{1,0:T(8,128)} %get-tuple-element.44.scales), custom_call_target="tpu_custom_call" | custom-call | flops 4000000000 | bytes 8388608 | tf_op jit(solution)/shard_map/pallas_call | solution.py:378
  168.2 0.0 copy-start.1
  168.3 5.2 %all-to-all-start.2 = ((bf16[256,32,128]{2,1,0:T(8,128)(2,1)}), bf16[256,32,128]{2,1,0:T(8,128)(2,1)S(1)}, u32[]{:S(2)}, u32[]{:S(2)}) async-start(bf16[256,32,128]{2,1,0:T(8,128)(2,1)} %shard_map.68), calls=%async_computation.2 | async-start | bytes 4194304 | tf_op jit(solution)/shard_map/all_to_all | solution.py:395
  173.5 0.0 copy-done.1
  173.5 0.1 copy.7
  173.6 54.1 %all-to-all-done.2 = bf16[256,32,128]{2,1,0:T(8,128)(2,1)S(1)} async-done(((bf16[256,32,128]{2,1,0:T(8,128)(2,1)}), bf16[256,32,128]{2,1,0:T(8,128)(2,1)S(1)}, u32[]{:S(2)}, u32[]{:S(2)}) %all-to-all-start.2) | async-done | bytes 2097184 | tf_op jit(solution)/shard_map/all_to_all | solution.py:395
  227.7 3.5 %shard_map.69 = bf16[256,16,128]{2,1,0:T(8,128)(2,1)} custom-call(s32[256,16]{1,0:T(8,128)S(1)} %bitcast.8, bf16[16,16,32,128]{3,2,1,0:T(8,128)(2,1)S(1)} %bitcast.7), custom_call_target="tpu_custom_call" | custom-call | flops 1000000000 | bytes 3145728 | tf_op jit(solution)/shard_map/pallas_call | solution.py:397
  (13 shorter events, 0.0 us)
Async XLA Ops:
  3.0 38.6 %all-to-all-start.1 = ((bf16[16,264,128]{2,1,0:T(8,128)(2,1)}), bf16[16,264,128]{2,1,0:T(8,128)(2,1)S(1)}, u32[]{:S(2)}, u32[]{:S(2)}) async-start(bf16[16,264,128]{2,1,0:T(8,128)(2,1)} %shard_map.65), calls=%async_computation.1 | async-start | bytes 2162688 | tf_op jit(solution)/shard_map/all_to_all | solution.py:321
  41.6 109.1 %all-to-all-start = ((bf16[256,32,256]{2,1,0:T(8,128)(2,1)}), bf16[256,32,256]{2,1,0:T(8,128)(2,1)}, u32[]{:S(2)}, u32[]{:S(2)}) async-start(bf16[256,32,256]{2,1,0:T(8,128)(2,1)} %bitcast.9), calls=%async_computation | async-start | bytes 8388608 | tf_op jit(solution)/shard_map/all_to_all | solution.py:342
  57.1 0.7 copy-start
  57.7 8.4 %collective-permute-start = (bf16[528,128]{1,0:T(8,128)(2,1)S(1)}, bf16[528,128]{1,0:T(8,128)(2,1)S(1)}, u32[]{:S(2)}, u32[]{:S(2)}) collective-permute-start(bf16[528,128]{1,0:T(8,128)(2,1)S(1)} %get-tuple-element.28), channel_id=1, source_target_pairs={{0,16},{16,0},{32,48},{48,32},{64,80},{80,64},{96,112},{112,96},{1... | collective-permute-start | bytes 405512 | tf_op jit(solution)/shard_map/ppermute | solution.py:361
  59.1 25.0 %collective-permute-start.1 = (bf16[528,128]{1,0:T(8,128)(2,1)S(1)}, bf16[528,128]{1,0:T(8,128)(2,1)S(1)}, u32[]{:S(2)}, u32[]{:S(2)}) collective-permute-start(bf16[528,128]{1,0:T(8,128)(2,1)S(1)} %get-tuple-element.29), channel_id=1, source_target_pairs={{0,32},{16,48},{32,0},{48,16},{64,96},{80,112},{96,64},{112,80},{1... | collective-permute-start | bytes 405512 | tf_op jit(solution)/shard_map/ppermute | solution.py:361
  61.6 25.1 %collective-permute-start.2 = (bf16[528,128]{1,0:T(8,128)(2,1)S(1)}, bf16[528,128]{1,0:T(8,128)(2,1)S(1)}, u32[]{:S(2)}, u32[]{:S(2)}) collective-permute-start(bf16[528,128]{1,0:T(8,128)(2,1)S(1)} %get-tuple-element.30), channel_id=1, source_target_pairs={{0,48},{16,32},{32,16},{48,0},{64,112},{80,96},{96,80},{112,64},{1... | collective-permute-start | bytes 405512 | tf_op jit(solution)/shard_map/ppermute | solution.py:361
  61.6 26.7 %collective-permute-start.3 = (bf16[528,128]{1,0:T(8,128)(2,1)S(1)}, bf16[528,128]{1,0:T(8,128)(2,1)S(1)}, u32[]{:S(2)}, u32[]{:S(2)}) collective-permute-start(bf16[528,128]{1,0:T(8,128)(2,1)S(1)} %get-tuple-element.31), channel_id=1, source_target_pairs={{0,64},{16,80},{32,96},{48,112},{64,0},{80,16},{96,32},{112,48},{1... | collective-permute-start | bytes 405512 | tf_op jit(solution)/shard_map/ppermute | solution.py:361
  63.0 25.3 %collective-permute-start.4 = (bf16[528,128]{1,0:T(8,128)(2,1)S(1)}, bf16[528,128]{1,0:T(8,128)(2,1)S(1)}, u32[]{:S(2)}, u32[]{:S(2)}) collective-permute-start(bf16[528,128]{1,0:T(8,128)(2,1)S(1)} %get-tuple-element.32), channel_id=1, source_target_pairs={{0,80},{16,64},{32,112},{48,96},{64,16},{80,0},{96,48},{112,32},{1... | collective-permute-start | bytes 405512 | tf_op jit(solution)/shard_map/ppermute | solution.py:361
  66.2 70.9 %copy-start.2 = (bf16[528,128]{1,0:T(8,128)(2,1)}, bf16[528,128]{1,0:T(8,128)(2,1)S(1)}, u32[]{:S(2)}) copy-start(bf16[528,128]{1,0:T(8,128)(2,1)S(1)} %collective-permute-done.refs_1_) | copy-start | bytes 405508
  66.2 26.8 %collective-permute-start.5 = (bf16[528,128]{1,0:T(8,128)(2,1)S(1)}, bf16[528,128]{1,0:T(8,128)(2,1)S(1)}, u32[]{:S(2)}, u32[]{:S(2)}) collective-permute-start(bf16[528,128]{1,0:T(8,128)(2,1)S(1)} %get-tuple-element.33), channel_id=1, source_target_pairs={{0,96},{16,112},{32,64},{48,80},{64,32},{80,48},{96,0},{112,16},{1... | collective-permute-start | bytes 405512 | tf_op jit(solution)/shard_map/ppermute | solution.py:361
  84.1 52.9 %copy-start.3 = (bf16[528,128]{1,0:T(8,128)(2,1)}, bf16[528,128]{1,0:T(8,128)(2,1)S(1)}, u32[]{:S(2)}) copy-start(bf16[528,128]{1,0:T(8,128)(2,1)S(1)} %collective-permute-done.1.refs_2_) | copy-start | bytes 405508
  84.1 11.5 %collective-permute-start.6 = (bf16[528,128]{1,0:T(8,128)(2,1)S(1)}, bf16[528,128]{1,0:T(8,128)(2,1)S(1)}, u32[]{:S(2)}, u32[]{:S(2)}) collective-permute-start(bf16[528,128]{1,0:T(8,128)(2,1)S(1)} %get-tuple-element.34), channel_id=1, source_target_pairs={{0,112},{16,96},{32,80},{48,64},{64,48},{80,32},{96,16},{112,0},{1... | collective-permute-start | bytes 405512 | tf_op jit(solution)/shard_map/ppermute | solution.py:361
  86.6 50.4 %copy-start.4 = (bf16[528,128]{1,0:T(8,128)(2,1)}, bf16[528,128]{1,0:T(8,128)(2,1)S(1)}, u32[]{:S(2)}) copy-start(bf16[528,128]{1,0:T(8,128)(2,1)S(1)} %collective-permute-done.2.refs_3_) | copy-start | bytes 405508
  86.6 12.1 %collective-permute-start.7 = (bf16[528,128]{1,0:T(8,128)(2,1)S(1)}, bf16[528,128]{1,0:T(8,128)(2,1)S(1)}, u32[]{:S(2)}, u32[]{:S(2)}) collective-permute-start(bf16[528,128]{1,0:T(8,128)(2,1)S(1)} %get-tuple-element.35), channel_id=1, source_target_pairs={{0,128},{16,144},{32,160},{48,176},{64,192},{80,208},{96,224},{112... | collective-permute-start | bytes 405512 | tf_op jit(solution)/shard_map/ppermute | solution.py:361
  88.3 48.7 %copy-start.5 = (bf16[528,128]{1,0:T(8,128)(2,1)}, bf16[528,128]{1,0:T(8,128)(2,1)S(1)}, u32[]{:S(2)}) copy-start(bf16[528,128]{1,0:T(8,128)(2,1)S(1)} %collective-permute-done.3.refs_4_) | copy-start | bytes 405508
  88.3 12.6 %collective-permute-start.8 = (bf16[528,128]{1,0:T(8,128)(2,1)S(1)}, bf16[528,128]{1,0:T(8,128)(2,1)S(1)}, u32[]{:S(2)}, u32[]{:S(2)}) collective-permute-start(bf16[528,128]{1,0:T(8,128)(2,1)S(1)} %get-tuple-element.36), channel_id=1, source_target_pairs={{0,144},{16,128},{32,176},{48,160},{64,208},{80,192},{96,240},{112... | collective-permute-start | bytes 405512 | tf_op jit(solution)/shard_map/ppermute | solution.py:361
  88.3 48.7 %copy-start.6 = (bf16[528,128]{1,0:T(8,128)(2,1)}, bf16[528,128]{1,0:T(8,128)(2,1)S(1)}, u32[]{:S(2)}) copy-start(bf16[528,128]{1,0:T(8,128)(2,1)S(1)} %collective-permute-done.4.refs_5_) | copy-start | bytes 405508
  88.3 19.2 %collective-permute-start.9 = (bf16[528,128]{1,0:T(8,128)(2,1)S(1)}, bf16[528,128]{1,0:T(8,128)(2,1)S(1)}, u32[]{:S(2)}, u32[]{:S(2)}) collective-permute-start(bf16[528,128]{1,0:T(8,128)(2,1)S(1)} %get-tuple-element.37), channel_id=1, source_target_pairs={{0,160},{16,176},{32,128},{48,144},{64,224},{80,240},{96,192},{112... | collective-permute-start | bytes 405512 | tf_op jit(solution)/shard_map/ppermute | solution.py:361
  93.0 44.1 %copy-start.7 = (bf16[528,128]{1,0:T(8,128)(2,1)}, bf16[528,128]{1,0:T(8,128)(2,1)S(1)}, u32[]{:S(2)}) copy-start(bf16[528,128]{1,0:T(8,128)(2,1)S(1)} %collective-permute-done.5.refs_6_) | copy-start | bytes 405508
  93.0 21.8 %collective-permute-start.10 = (bf16[528,128]{1,0:T(8,128)(2,1)S(1)}, bf16[528,128]{1,0:T(8,128)(2,1)S(1)}, u32[]{:S(2)}, u32[]{:S(2)}) collective-permute-start(bf16[528,128]{1,0:T(8,128)(2,1)S(1)} %get-tuple-element.38), channel_id=1, source_target_pairs={{0,176},{16,160},{32,144},{48,128},{64,240},{80,224},{96,208},{112... | collective-permute-start | bytes 405512 | tf_op jit(solution)/shard_map/ppermute | solution.py:361
  95.6 41.4 %copy-start.8 = (bf16[528,128]{1,0:T(8,128)(2,1)}, bf16[528,128]{1,0:T(8,128)(2,1)S(1)}, u32[]{:S(2)}) copy-start(bf16[528,128]{1,0:T(8,128)(2,1)S(1)} %collective-permute-done.6.refs_7_) | copy-start | bytes 405508
  95.6 24.7 %collective-permute-start.11 = (bf16[528,128]{1,0:T(8,128)(2,1)S(1)}, bf16[528,128]{1,0:T(8,128)(2,1)S(1)}, u32[]{:S(2)}, u32[]{:S(2)}) collective-permute-start(bf16[528,128]{1,0:T(8,128)(2,1)S(1)} %get-tuple-element.39), channel_id=1, source_target_pairs={{0,192},{16,208},{32,224},{48,240},{64,128},{80,144},{96,160},{112... | collective-permute-start | bytes 405512 | tf_op jit(solution)/shard_map/ppermute | solution.py:361
  98.7 38.3 %copy-start.9 = (bf16[528,128]{1,0:T(8,128)(2,1)}, bf16[528,128]{1,0:T(8,128)(2,1)S(1)}, u32[]{:S(2)}) copy-start(bf16[528,128]{1,0:T(8,128)(2,1)S(1)} %collective-permute-done.7.refs_8_) | copy-start | bytes 405508
  98.7 24.0 %collective-permute-start.12 = (bf16[528,128]{1,0:T(8,128)(2,1)S(1)}, bf16[528,128]{1,0:T(8,128)(2,1)S(1)}, u32[]{:S(2)}, u32[]{:S(2)}) collective-permute-start(bf16[528,128]{1,0:T(8,128)(2,1)S(1)} %get-tuple-element.40), channel_id=1, source_target_pairs={{0,208},{16,192},{32,240},{48,224},{64,144},{80,128},{96,176},{112... | collective-permute-start | bytes 405512 | tf_op jit(solution)/shard_map/ppermute | solution.py:361
  100.8 36.2 %copy-start.10 = (bf16[528,128]{1,0:T(8,128)(2,1)}, bf16[528,128]{1,0:T(8,128)(2,1)S(1)}, u32[]{:S(2)}) copy-start(bf16[528,128]{1,0:T(8,128)(2,1)S(1)} %collective-permute-done.8.refs_9_) | copy-start | bytes 405508
  100.8 30.6 %collective-permute-start.13 = (bf16[528,128]{1,0:T(8,128)(2,1)S(1)}, bf16[528,128]{1,0:T(8,128)(2,1)S(1)}, u32[]{:S(2)}, u32[]{:S(2)}) collective-permute-start(bf16[528,128]{1,0:T(8,128)(2,1)S(1)} %get-tuple-element.41), channel_id=1, source_target_pairs={{0,224},{16,240},{32,192},{48,208},{64,160},{80,176},{96,128},{112... | collective-permute-start | bytes 405512 | tf_op jit(solution)/shard_map/ppermute | solution.py:361
  107.5 29.6 %copy-start.11 = (bf16[528,128]{1,0:T(8,128)(2,1)}, bf16[528,128]{1,0:T(8,128)(2,1)S(1)}, u32[]{:S(2)}) copy-start(bf16[528,128]{1,0:T(8,128)(2,1)S(1)} %collective-permute-done.9.refs_10_) | copy-start | bytes 405508
  107.5 29.5 %collective-permute-start.14 = (bf16[528,128]{1,0:T(8,128)(2,1)S(1)}, bf16[528,128]{1,0:T(8,128)(2,1)S(1)}, u32[]{:S(2)}, u32[]{:S(2)}) collective-permute-start(bf16[528,128]{1,0:T(8,128)(2,1)S(1)} %get-tuple-element.42), channel_id=1, source_target_pairs={{0,240},{16,224},{32,208},{48,192},{64,176},{80,160},{96,144},{112... | collective-permute-start | bytes 405512 | tf_op jit(solution)/shard_map/ppermute | solution.py:361
  114.8 22.3 %copy-start.12 = (bf16[528,128]{1,0:T(8,128)(2,1)}, bf16[528,128]{1,0:T(8,128)(2,1)S(1)}, u32[]{:S(2)}) copy-start(bf16[528,128]{1,0:T(8,128)(2,1)S(1)} %collective-permute-done.10.refs_11_) | copy-start | bytes 405508
  120.4 16.7 %copy-start.13 = (bf16[528,128]{1,0:T(8,128)(2,1)}, bf16[528,128]{1,0:T(8,128)(2,1)S(1)}, u32[]{:S(2)}) copy-start(bf16[528,128]{1,0:T(8,128)(2,1)S(1)} %collective-permute-done.11.refs_12_) | copy-start | bytes 405508
  122.7 14.4 %copy-start.14 = (bf16[528,128]{1,0:T(8,128)(2,1)}, bf16[528,128]{1,0:T(8,128)(2,1)S(1)}, u32[]{:S(2)}) copy-start(bf16[528,128]{1,0:T(8,128)(2,1)S(1)} %collective-permute-done.12.refs_13_) | copy-start | bytes 405508
  131.4 5.7 %copy-start.15 = (bf16[528,128]{1,0:T(8,128)(2,1)}, bf16[528,128]{1,0:T(8,128)(2,1)S(1)}, u32[]{:S(2)}) copy-start(bf16[528,128]{1,0:T(8,128)(2,1)S(1)} %collective-permute-done.13.refs_14_) | copy-start | bytes 405508
  137.0 0.7 copy-start.16
  168.2 5.2 %copy-start.1 = (s32[16,256]{1,0:T(8,128)S(1)}, s32[16,256]{1,0:T(8,128)}, u32[]{:S(2)}) copy-start(s32[16,256]{1,0:T(8,128)} %get-tuple-element.25) | copy-start | bytes 49156
  168.3 59.5 %all-to-all-start.2 = ((bf16[256,32,128]{2,1,0:T(8,128)(2,1)}), bf16[256,32,128]{2,1,0:T(8,128)(2,1)S(1)}, u32[]{:S(2)}, u32[]{:S(2)}) async-start(bf16[256,32,128]{2,1,0:T(8,128)(2,1)} %shard_map.68), calls=%async_computation.2 | async-start | bytes 4194304 | tf_op jit(solution)/shard_map/all_to_all | solution.py:395

commit v5 on v4

--- a/solution.py
+++ b/solution.py
@@ -227,9 +227,8 @@
             kvs[:, rows(g, unit), :] = turned.reshape(FINE, unit, 2 * width)
         queries_in(t).wait()
 
-        def one(f, carry):
-            key_scale = scales[pl.ds(f, 1), :]
-            value_scale = scales[pl.ds(FINE + f, 1), :]
+        def scores_of(f):
+            key_scale = scales[f : f + 1, :]
             factor = key_scale * (width**-0.5 * LOG2E)
             bias = jnp.where(key_scale > 0.0, 0.0, NEG)
             query = qs[f, rows(t, tile), :]
@@ -241,28 +240,86 @@
                 if u == t:
                     score = jnp.where(ahead, NEG, score)
                 pieces.append(score)
+            return pieces
+
+        def finish(f, pieces):
+            value_scale = scales[FINE + f : FINE + f + 1, :]
             highest = pieces[0]
             for score in pieces[1:]:
                 highest = jnp.maximum(highest, score)
             highest = jnp.max(highest, axis=1, keepdims=True)
-            below, total = None, None
+            below, weights = None, []
             for u, score in enumerate(pieces):
                 there = rows(u, tile)
                 unnormed = jnp.exp2(score - highest)
-                weights = (unnormed * value_scale[:, there]).astype(jnp.bfloat16)
-                term = matmul(weights, kvs[f, there, width:])
+                weights.append((unnormed * value_scale[:, there]).astype(jnp.bfloat16))
                 below = unnormed if below is None else below + unnormed
-                total = term if total is None else total + term
+            total = matmul(jnp.concatenate(weights, axis=1), kvs[f, : (t + 1) * tile, width:])
             below = jnp.sum(below, axis=1, keepdims=True)
             os[f] = (total / below).astype(jnp.bfloat16)
-            return carry
-
-        lax.fori_loop(0, FINE, one, 0, unroll=FINE)
+
+        upcoming = scores_of(0)
+        for f in range(FINE):
+            current = upcoming
+            if f + 1 < FINE:
+                upcoming = scores_of(f + 1)
+            finish(f, current)
         for g in range(piece // batch):
             block = os[:, rows(g, unit), :].reshape(256, width)
             turned = matmul(turn_out, block).astype(jnp.bfloat16)
             result[rows(t * (piece // batch) + g, batch)] = turned.reshape(batch, CHUNK, width)
         result_out(t).start()
+    for n in range(PIECES):
+        result_out(n).wait()
+
+
+def unplace_kernel(slot_ref, arrived_ref, out_ref, answer, by_head, result, sems):
+    rows, heads, width = result.shape
+    some = heads // PIECES
+    piece = rows // PIECES
+    group = 256 // heads
+
+    def answer_in(n):
+        here = pl.ds(n * some, some)
+        return pltpu.make_async_copy(
+            arrived_ref.at[:, here], answer.at[:, here], sems.at[0, n]
+        )
+
+    def result_out(n):
+        here = pl.ds(n * piece, piece)
+        return pltpu.make_async_copy(result.at[here], out_ref.at[here], sems.at[1, n])
+
+    for n in range(PIECES):
+        answer_in(n).start()
+    place = iota((rows, SLOTS), 1)
+    swap = swap_matrix(heads, group, 1)
+    def pick_of(h):
+        return one_hot(place == slot_ref[:, h : h + 1])
+
+    upcoming = pick_of(0)
+    for h in range(heads):
+        if h % some == 0:
+            answer_in(h // some).wait()
+        pick = upcoming
+        if h + 1 < heads:
+            upcoming = pick_of(h + 1)
+        by_head[h] = matmul(pick, answer[:, h].reshape(SLOTS, width)).astype(jnp.bfloat16)
+
+    def turned(g):
+        block = by_head[:, g * group : (g + 1) * group, :].reshape(256, width)
+        return matmul(swap, block)
+
+    groups = piece // group
+    upcoming = turned(0)
+    for g in range(rows // group):
+        current = upcoming
+        if (g + 1) * group < rows:
+            upcoming = turned(g + 1)
+        result[g * group : (g + 1) * group] = current.astype(jnp.bfloat16).reshape(
+            group, heads, width
+        )
+        if (g + 1) % groups == 0:
+            result_out(g // groups).start()
     for n in range(PIECES):
         result_out(n).wait()
 

time: 232 us -> 229 us (0.987)
  Pallas kernels: 38.8 us -> 35.6 us
    pallas_call x1, Pallas kernels: 17.5 us -> 14.3 us  [shards(): pl.pallas_call(attend_kernel, in_specs=[anywhere, anywhere, pl.BlockSpec(...]
where the time goes in v5:
time: 229 us; the launch traced here: 228 us
  waiting for transfers between devices  130 us (57%)
  starting transfers between devices  60.8 us (27%)
  Pallas kernels  35.6 us (16%)
    all_to_all x1, waiting for transfers between devices, shards(): answer = lax.all_to_all(answer, BOTH, 0, 0, tiled=True)  53.9 us
    ppermute x15, waiting for transfers between devices, shards(): lax.ppermute(parts[d], 'outer', [(n, n ^ d) for n in range(outer)])  44.2 us
    ppermute x15, starting transfers between devices, shards(): lax.ppermute(parts[d], 'outer', [(n, n ^ d) for n in range(outer)])  35.1 us
    all_to_all x1, waiting for transfers between devices, shards(): packed = lax.all_to_all(packed, 'inner', 0, 0, tiled=True)  22.6 us
    pallas_call x1, Pallas kernels, shards(): pl.pallas_call(attend_kernel, in_specs=[anywhere, anywhere, pl.BlockSpec(...  14.3 us
    all_to_all x1, starting transfers between devices, shards(): message = lax.all_to_all(message, BOTH, 0, 0, tiled=True)  10.2 us
    all_to_all x1, starting transfers between devices, shards(): packed = lax.all_to_all(packed, 'inner', 0, 0, tiled=True)  9.98 us
    all_to_all x1, waiting for transfers between devices, shards(): message = lax.all_to_all(message, BOTH, 0, 0, tiled=True)  9.47 us
  transfers between devices with their start and end apart: 18, of which 13 were waited for; matrix products, arithmetic and copies ran while one was open for 0% of the time, Pallas kernels for 6%

profile of v5, /device:TPU:1, one launch (start us, length us, event | category | flops | bytes accessed | tf_op | source)
XLA Modules:
  0.0 228.2 jit_solution(17365860026669138571)
XLA Ops:
  0.0 3.0 %shard_map.65 = bf16[16,264,128]{2,1,0:T(8,128)(2,1)} custom-call(s32[16,1,256]{2,1,0:T(1,128)} %bitcast.10, bf16[16,256]{1,0:T(8,128)(2,1)} %bitcast.12, bf16[16,256]{1,0:T(8,128)(2,1)} %bitcast.13, bf16[256,16,128]{2,1,0:T(8,128)(2,1)} %q_ref.1), custom_call_target="tpu_custom_call" | custom-call | flops 1000000000 | bytes 2097152 | tf_op jit(solution)/shard_map/pallas_call | solution.py:373
  3.0 10.0 %all-to-all-start.1 = ((bf16[16,264,128]{2,1,0:T(8,128)(2,1)}), bf16[16,264,128]{2,1,0:T(8,128)(2,1)S(1)}, u32[]{:S(2)}, u32[]{:S(2)}) async-start(bf16[16,264,128]{2,1,0:T(8,128)(2,1)} %shard_map.65), calls=%async_computation.1 | async-start | bytes 2162688 | tf_op jit(solution)/shard_map/all_to_all | solution.py:378
  13.0 6.0 %shard_map.64 = (s32[16,256]{1,0:T(8,128)}, bf16[16,16,32,256]{3,2,1,0:T(8,128)(2,1)}) custom-call(s32[16,1,256]{2,1,0:T(1,128)} %bitcast.11, bf16[256,16,128]{2,1,0:T(8,128)(2,1)} %k_ref.1, bf16[256,16,128]{2,1,0:T(8,128)(2,1)} %v_ref.1), custom_call_target="tpu_custom_call" | custom-call | flops 3000000000 | bytes 6291456 | tf_op jit(solution)/shard_map/pallas_call | solution.py:381
  19.0 22.6 %all-to-all-done.1.arrived_ref = bf16[16,264,128]{2,1,0:T(8,128)(2,1)S(1)} async-done(((bf16[16,264,128]{2,1,0:T(8,128)(2,1)}), bf16[16,264,128]{2,1,0:T(8,128)(2,1)S(1)}, u32[]{:S(2)}, u32[]{:S(2)}) %all-to-all-start.1) | async-done | bytes 1081376 | tf_op jit(solution)/shard_map/all_to_all | solution.py:378
  41.6 10.2 %all-to-all-start = ((bf16[256,32,256]{2,1,0:T(8,128)(2,1)}), bf16[256,32,256]{2,1,0:T(8,128)(2,1)}, u32[]{:S(2)}, u32[]{:S(2)}) async-start(bf16[256,32,256]{2,1,0:T(8,128)(2,1)} %bitcast.9), calls=%async_computation | async-start | bytes 8388608 | tf_op jit(solution)/shard_map/all_to_all | solution.py:399
  51.9 5.2 %shard_map.66 = (bf16[528,128]{1,0:T(8,128)(2,1)S(1)}, bf16[528,128]{1,0:T(8,128)(2,1)S(1)}, bf16[528,128]{1,0:T(8,128)(2,1)S(1)}, bf16[528,128]{1,0:T(8,128)(2,...) custom-call(s32[1]{0:T(128)} %bitcast.3.me_ref, ...), custom_call_target="tpu_custom_call" | custom-call | flops 2000000000 | bytes 3145728 | tf_op jit(solution)/shard_map/pallas_call | solution.py:402
  57.1 0.0 copy-start
  57.1 0.6 copy-done
  57.7 1.4 collective-permute-start
  59.1 2.4 %collective-permute-start.1 = (bf16[528,128]{1,0:T(8,128)(2,1)S(1)}, bf16[528,128]{1,0:T(8,128)(2,1)S(1)}, u32[]{:S(2)}, u32[]{:S(2)}) collective-permute-start(bf16[528,128]{1,0:T(8,128)(2,1)S(1)} %get-tuple-element.29), channel_id=1, source_target_pairs={{0,32},{16,48},{32,0},{48,16},{64,96},{80,112},{96,64},{112,80},{1... | collective-permute-start | bytes 405512 | tf_op jit(solution)/shard_map/ppermute | solution.py:418
  61.6 0.0 collective-permute-start.2
  61.6 1.4 collective-permute-start.3
  63.0 0.0 collective-permute-start.4
  63.0 3.2 %collective-permute-done.refs_1_ = bf16[528,128]{1,0:T(8,128)(2,1)S(1)} collective-permute-done((bf16[528,128]{1,0:T(8,128)(2,1)S(1)}, bf16[528,128]{1,0:T(8,128)(2,1)S(1)}, u32[]{:S(2)}, u32[]{:S(2)}) %collective-permute-start) | collective-permute-done | bytes 135200 | tf_op jit(solution)/shard_map/ppermute | solution.py:418
  66.2 0.0 copy-start.2
  66.2 4.5 %collective-permute-start.5 = (bf16[528,128]{1,0:T(8,128)(2,1)S(1)}, bf16[528,128]{1,0:T(8,128)(2,1)S(1)}, u32[]{:S(2)}, u32[]{:S(2)}) collective-permute-start(bf16[528,128]{1,0:T(8,128)(2,1)S(1)} %get-tuple-element.33), channel_id=1, source_target_pairs={{0,96},{16,112},{32,64},{48,80},{64,32},{80,48},{96,0},{112,16},{1... | collective-permute-start | bytes 405512 | tf_op jit(solution)/shard_map/ppermute | solution.py:418
  70.7 13.4 %collective-permute-done.1.refs_2_ = bf16[528,128]{1,0:T(8,128)(2,1)S(1)} collective-permute-done((bf16[528,128]{1,0:T(8,128)(2,1)S(1)}, bf16[528,128]{1,0:T(8,128)(2,1)S(1)}, u32[]{:S(2)}, u32[]{:S(2)}) %collective-permute-start.1) | collective-permute-done | bytes 135200 | tf_op jit(solution)/shard_map/ppermute | solution.py:418
  84.1 2.5 %collective-permute-start.6 = (bf16[528,128]{1,0:T(8,128)(2,1)S(1)}, bf16[528,128]{1,0:T(8,128)(2,1)S(1)}, u32[]{:S(2)}, u32[]{:S(2)}) collective-permute-start(bf16[528,128]{1,0:T(8,128)(2,1)S(1)} %get-tuple-element.34), channel_id=1, source_target_pairs={{0,112},{16,96},{32,80},{48,64},{64,48},{80,32},{96,16},{112,0},{1... | collective-permute-start | bytes 405512 | tf_op jit(solution)/shard_map/ppermute | solution.py:418
  86.6 0.0 collective-permute-done.2.refs_3_
  86.6 1.6 collective-permute-start.7
  88.3 0.0 collective-permute-done.3.refs_4_
  88.3 0.0 collective-permute-start.8
  88.3 0.0 collective-permute-done.4.refs_5_
  88.3 0.0 copy-start.6
  88.3 4.6 %collective-permute-start.9 = (bf16[528,128]{1,0:T(8,128)(2,1)S(1)}, bf16[528,128]{1,0:T(8,128)(2,1)S(1)}, u32[]{:S(2)}, u32[]{:S(2)}) collective-permute-start(bf16[528,128]{1,0:T(8,128)(2,1)S(1)} %get-tuple-element.37), channel_id=1, source_target_pairs={{0,160},{16,176},{32,128},{48,144},{64,224},{80,240},{96,192},{112... | collective-permute-start | bytes 405512 | tf_op jit(solution)/shard_map/ppermute | solution.py:418
  92.9 0.0 collective-permute-done.5.refs_6_
  93.0 2.7 %collective-permute-start.10 = (bf16[528,128]{1,0:T(8,128)(2,1)S(1)}, bf16[528,128]{1,0:T(8,128)(2,1)S(1)}, u32[]{:S(2)}, u32[]{:S(2)}) collective-permute-start(bf16[528,128]{1,0:T(8,128)(2,1)S(1)} %get-tuple-element.38), channel_id=1, source_target_pairs={{0,176},{16,160},{32,144},{48,128},{64,240},{80,224},{96,208},{112... | collective-permute-start | bytes 405512 | tf_op jit(solution)/shard_map/ppermute | solution.py:418
  95.6 0.0 collective-permute-done.6.refs_7_
  95.6 0.5 collective-permute-start.11
  96.1 2.6 %collective-permute-done.7.refs_8_ = bf16[528,128]{1,0:T(8,128)(2,1)S(1)} collective-permute-done((bf16[528,128]{1,0:T(8,128)(2,1)S(1)}, bf16[528,128]{1,0:T(8,128)(2,1)S(1)}, u32[]{:S(2)}, u32[]{:S(2)}) %collective-permute-start.7) | collective-permute-done | bytes 135200 | tf_op jit(solution)/shard_map/ppermute | solution.py:418
  98.7 1.3 collective-permute-start.12
  100.1 0.8 collective-permute-done.8.refs_9_
  100.8 5.7 %collective-permute-start.13 = (bf16[528,128]{1,0:T(8,128)(2,1)S(1)}, bf16[528,128]{1,0:T(8,128)(2,1)S(1)}, u32[]{:S(2)}, u32[]{:S(2)}) collective-permute-start(bf16[528,128]{1,0:T(8,128)(2,1)S(1)} %get-tuple-element.41), channel_id=1, source_target_pairs={{0,224},{16,240},{32,192},{48,208},{64,160},{80,176},{96,128},{112... | collective-permute-start | bytes 405512 | tf_op jit(solution)/shard_map/ppermute | solution.py:418
  106.6 1.0 collective-permute-done.9.refs_10_
  107.5 6.3 %collective-permute-start.14 = (bf16[528,128]{1,0:T(8,128)(2,1)S(1)}, bf16[528,128]{1,0:T(8,128)(2,1)S(1)}, u32[]{:S(2)}, u32[]{:S(2)}) collective-permute-start(bf16[528,128]{1,0:T(8,128)(2,1)S(1)} %get-tuple-element.42), channel_id=1, source_target_pairs={{0,240},{16,224},{32,208},{48,192},{64,176},{80,160},{96,144},{112... | collective-permute-start | bytes 405512 | tf_op jit(solution)/shard_map/ppermute | solution.py:418
  113.8 0.9 collective-permute-done.10.refs_11_
  114.8 5.6 %collective-permute-done.11.refs_12_ = bf16[528,128]{1,0:T(8,128)(2,1)S(1)} collective-permute-done((bf16[528,128]{1,0:T(8,128)(2,1)S(1)}, bf16[528,128]{1,0:T(8,128)(2,1)S(1)}, u32[]{:S(2)}, u32[]{:S(2)}) %collective-permute-start.11) | collective-permute-done | bytes 135200 | tf_op jit(solution)/shard_map/ppermute | solution.py:418
  120.4 2.4 %collective-permute-done.12.refs_13_ = bf16[528,128]{1,0:T(8,128)(2,1)S(1)} collective-permute-done((bf16[528,128]{1,0:T(8,128)(2,1)S(1)}, bf16[528,128]{1,0:T(8,128)(2,1)S(1)}, u32[]{:S(2)}, u32[]{:S(2)}) %collective-permute-start.12) | collective-permute-done | bytes 135200 | tf_op jit(solution)/shard_map/ppermute | solution.py:418
  122.7 8.7 %collective-permute-done.13.refs_14_ = bf16[528,128]{1,0:T(8,128)(2,1)S(1)} collective-permute-done((bf16[528,128]{1,0:T(8,128)(2,1)S(1)}, bf16[528,128]{1,0:T(8,128)(2,1)S(1)}, u32[]{:S(2)}, u32[]{:S(2)}) %collective-permute-start.13) | collective-permute-done | bytes 135200 | tf_op jit(solution)/shard_map/ppermute | solution.py:418
  131.4 5.6 %collective-permute-done.14.refs_15_ = bf16[528,128]{1,0:T(8,128)(2,1)S(1)} collective-permute-done((bf16[528,128]{1,0:T(8,128)(2,1)S(1)}, bf16[528,128]{1,0:T(8,128)(2,1)S(1)}, u32[]{:S(2)}, u32[]{:S(2)}) %collective-permute-start.14) | collective-permute-done | bytes 135200 | tf_op jit(solution)/shard_map/ppermute | solution.py:418
  137.0 0.0 copy-done.2
  137.0 0.0 copy-done.3
  137.0 0.0 copy-done.4
  137.0 0.0 copy-done.5
  137.0 0.0 copy-done.6
  137.0 0.0 copy-done.7
  137.1 0.0 copy-done.8
  137.1 0.0 copy-done.9
  137.1 0.0 copy-done.10
  137.1 0.0 copy-done.11
  137.1 0.0 copy-done.12
  137.1 0.0 copy-done.13
  137.1 0.0 copy-done.14
  137.1 0.0 copy-done.15
  137.1 0.5 copy-done.16
  137.7 3.5 %shard_map.67 = (bf16[8,1024,128]{2,1,0:T(8,128)(2,1)}, f32[16,1024]{1,0:T(8,128)}) custom-call(s32[1]{0:T(128)} %bitcast.3.me_ref, bf16[528,128]{1,0:T(8,128)(2,1)} %copy-done, bf16[528,128]{1,0:T(8,128)(2,1)} %copy-done.2, bf16[528,128]{1,0:T(8,128)(2,1)} %copy-done.3, bf16[528,128]{1,0:T(8,128)(2,1)} %copy-done.4, bf16[528,128]{1,0:T(8,128)(2,1)} %copy-done.5, ...), custom_call_target="tpu_custom_call" | custom-call | flops 1000000000 | bytes 4194304 | tf_op jit(solution)/shard_map/pallas_call | solution.py:423
  141.2 9.5 %all-to-all-done.arrived_ref = bf16[256,32,256]{2,1,0:T(8,128)(2,1)} async-done(((bf16[256,32,256]{2,1,0:T(8,128)(2,1)}), bf16[256,32,256]{2,1,0:T(8,128)(2,1)}, u32[]{:S(2)}, u32[]{:S(2)}) %all-to-all-start) | async-done | bytes 4194336 | tf_op jit(solution)/shard_map/all_to_all | solution.py:399
  150.7 14.3 %shard_map.68 = bf16[256,32,128]{2,1,0:T(8,128)(2,1)} custom-call(bf16[256,32,256]{2,1,0:T(8,128)(2,1)} %all-to-all-done.arrived_ref, bf16[8,1024,128]{2,1,0:T(8,128)(2,1)} %get-tuple-element.43.q_ref, f32[16,1024]{1,0:T(8,128)} %get-tuple-element.44.scales), custom_call_target="tpu_custom_call" | custom-call | flops 4000000000 | bytes 8388608 | tf_op jit(solution)/shard_map/pallas_call | solution.py:435
  165.0 0.0 copy-start.1
  165.0 5.5 %all-to-all-start.2 = ((bf16[256,32,128]{2,1,0:T(8,128)(2,1)}), bf16[256,32,128]{2,1,0:T(8,128)(2,1)S(1)}, u32[]{:S(2)}, u32[]{:S(2)}) async-start(bf16[256,32,128]{2,1,0:T(8,128)(2,1)} %shard_map.68), calls=%async_computation.2 | async-start | bytes 4194304 | tf_op jit(solution)/shard_map/all_to_all | solution.py:452
  170.5 0.0 copy-done.1
  170.5 0.1 copy.7
  170.6 53.9 %all-to-all-done.2 = bf16[256,32,128]{2,1,0:T(8,128)(2,1)S(1)} async-done(((bf16[256,32,128]{2,1,0:T(8,128)(2,1)}), bf16[256,32,128]{2,1,0:T(8,128)(2,1)S(1)}, u32[]{:S(2)}, u32[]{:S(2)}) %all-to-all-start.2) | async-done | bytes 2097184 | tf_op jit(solution)/shard_map/all_to_all | solution.py:452
  224.5 3.5 %shard_map.69 = bf16[256,16,128]{2,1,0:T(8,128)(2,1)} custom-call(s32[256,16]{1,0:T(8,128)S(1)} %bitcast.8, bf16[16,16,32,128]{3,2,1,0:T(8,128)(2,1)S(1)} %bitcast.7), custom_call_target="tpu_custom_call" | custom-call | flops 1000000000 | bytes 3145728 | tf_op jit(solution)/shard_map/pallas_call | solution.py:454
  (13 shorter events, 0.0 us)
Async XLA Ops:
  3.0 38.6 %all-to-all-start.1 = ((bf16[16,264,128]{2,1,0:T(8,128)(2,1)}), bf16[16,264,128]{2,1,0:T(8,128)(2,1)S(1)}, u32[]{:S(2)}, u32[]{:S(2)}) async-start(bf16[16,264,128]{2,1,0:T(8,128)(2,1)} %shard_map.65), calls=%async_computation.1 | async-start | bytes 2162688 | tf_op jit(solution)/shard_map/all_to_all | solution.py:378
  41.6 109.1 %all-to-all-start = ((bf16[256,32,256]{2,1,0:T(8,128)(2,1)}), bf16[256,32,256]{2,1,0:T(8,128)(2,1)}, u32[]{:S(2)}, u32[]{:S(2)}) async-start(bf16[256,32,256]{2,1,0:T(8,128)(2,1)} %bitcast.9), calls=%async_computation | async-start | bytes 8388608 | tf_op jit(solution)/shard_map/all_to_all | solution.py:399
  57.1 0.7 copy-start
  57.7 8.4 %collective-permute-start = (bf16[528,128]{1,0:T(8,128)(2,1)S(1)}, bf16[528,128]{1,0:T(8,128)(2,1)S(1)}, u32[]{:S(2)}, u32[]{:S(2)}) collective-permute-start(bf16[528,128]{1,0:T(8,128)(2,1)S(1)} %get-tuple-element.28), channel_id=1, source_target_pairs={{0,16},{16,0},{32,48},{48,32},{64,80},{80,64},{96,112},{112,96},{1... | collective-permute-start | bytes 405512 | tf_op jit(solution)/shard_map/ppermute | solution.py:418
  59.1 25.0 %collective-permute-start.1 = (bf16[528,128]{1,0:T(8,128)(2,1)S(1)}, bf16[528,128]{1,0:T(8,128)(2,1)S(1)}, u32[]{:S(2)}, u32[]{:S(2)}) collective-permute-start(bf16[528,128]{1,0:T(8,128)(2,1)S(1)} %get-tuple-element.29), channel_id=1, source_target_pairs={{0,32},{16,48},{32,0},{48,16},{64,96},{80,112},{96,64},{112,80},{1... | collective-permute-start | bytes 405512 | tf_op jit(solution)/shard_map/ppermute | solution.py:418
  61.6 25.1 %collective-permute-start.2 = (bf16[528,128]{1,0:T(8,128)(2,1)S(1)}, bf16[528,128]{1,0:T(8,128)(2,1)S(1)}, u32[]{:S(2)}, u32[]{:S(2)}) collective-permute-start(bf16[528,128]{1,0:T(8,128)(2,1)S(1)} %get-tuple-element.30), channel_id=1, source_target_pairs={{0,48},{16,32},{32,16},{48,0},{64,112},{80,96},{96,80},{112,64},{1... | collective-permute-start | bytes 405512 | tf_op jit(solution)/shard_map/ppermute | solution.py:418
  61.6 26.7 %collective-permute-start.3 = (bf16[528,128]{1,0:T(8,128)(2,1)S(1)}, bf16[528,128]{1,0:T(8,128)(2,1)S(1)}, u32[]{:S(2)}, u32[]{:S(2)}) collective-permute-start(bf16[528,128]{1,0:T(8,128)(2,1)S(1)} %get-tuple-element.31), channel_id=1, source_target_pairs={{0,64},{16,80},{32,96},{48,112},{64,0},{80,16},{96,32},{112,48},{1... | collective-permute-start | bytes 405512 | tf_op jit(solution)/shard_map/ppermute | solution.py:418
  63.0 25.3 %collective-permute-start.4 = (bf16[528,128]{1,0:T(8,128)(2,1)S(1)}, bf16[528,128]{1,0:T(8,128)(2,1)S(1)}, u32[]{:S(2)}, u32[]{:S(2)}) collective-permute-start(bf16[528,128]{1,0:T(8,128)(2,1)S(1)} %get-tuple-element.32), channel_id=1, source_target_pairs={{0,80},{16,64},{32,112},{48,96},{64,16},{80,0},{96,48},{112,32},{1... | collective-permute-start | bytes 405512 | tf_op jit(solution)/shard_map/ppermute | solution.py:418
  66.2 70.9 %copy-start.2 = (bf16[528,128]{1,0:T(8,128)(2,1)}, bf16[528,128]{1,0:T(8,128)(2,1)S(1)}, u32[]{:S(2)}) copy-start(bf16[528,128]{1,0:T(8,128)(2,1)S(1)} %collective-permute-done.refs_1_) | copy-start | bytes 405508
  66.2 26.8 %collective-permute-start.5 = (bf16[528,128]{1,0:T(8,128)(2,1)S(1)}, bf16[528,128]{1,0:T(8,128)(2,1)S(1)}, u32[]{:S(2)}, u32[]{:S(2)}) collective-permute-start(bf16[528,128]{1,0:T(8,128)(2,1)S(1)} %get-tuple-element.33), channel_id=1, source_target_pairs={{0,96},{16,112},{32,64},{48,80},{64,32},{80,48},{96,0},{112,16},{1... | collective-permute-start | bytes 405512 | tf_op jit(solution)/shard_map/ppermute | solution.py:418
  84.1 52.9 %copy-start.3 = (bf16[528,128]{1,0:T(8,128)(2,1)}, bf16[528,128]{1,0:T(8,128)(2,1)S(1)}, u32[]{:S(2)}) copy-start(bf16[528,128]{1,0:T(8,128)(2,1)S(1)} %collective-permute-done.1.refs_2_) | copy-start | bytes 405508
  84.1 11.5 %collective-permute-start.6 = (bf16[528,128]{1,0:T(8,128)(2,1)S(1)}, bf16[528,128]{1,0:T(8,128)(2,1)S(1)}, u32[]{:S(2)}, u32[]{:S(2)}) collective-permute-start(bf16[528,128]{1,0:T(8,128)(2,1)S(1)} %get-tuple-element.34), channel_id=1, source_target_pairs={{0,112},{16,96},{32,80},{48,64},{64,48},{80,32},{96,16},{112,0},{1... | collective-permute-start | bytes 405512 | tf_op jit(solution)/shard_map/ppermute | solution.py:418
  86.6 50.4 %copy-start.4 = (bf16[528,128]{1,0:T(8,128)(2,1)}, bf16[528,128]{1,0:T(8,128)(2,1)S(1)}, u32[]{:S(2)}) copy-start(bf16[528,128]{1,0:T(8,128)(2,1)S(1)} %collective-permute-done.2.refs_3_) | copy-start | bytes 405508
  86.6 12.1 %collective-permute-start.7 = (bf16[528,128]{1,0:T(8,128)(2,1)S(1)}, bf16[528,128]{1,0:T(8,128)(2,1)S(1)}, u32[]{:S(2)}, u32[]{:S(2)}) collective-permute-start(bf16[528,128]{1,0:T(8,128)(2,1)S(1)} %get-tuple-element.35), channel_id=1, source_target_pairs={{0,128},{16,144},{32,160},{48,176},{64,192},{80,208},{96,224},{112... | collective-permute-start | bytes 405512 | tf_op jit(solution)/shard_map/ppermute | solution.py:418
  88.3 48.7 %copy-start.5 = (bf16[528,128]{1,0:T(8,128)(2,1)}, bf16[528,128]{1,0:T(8,128)(2,1)S(1)}, u32[]{:S(2)}) copy-start(bf16[528,128]{1,0:T(8,128)(2,1)S(1)} %collective-permute-done.3.refs_4_) | copy-start | bytes 405508
  88.3 12.6 %collective-permute-start.8 = (bf16[528,128]{1,0:T(8,128)(2,1)S(1)}, bf16[528,128]{1,0:T(8,128)(2,1)S(1)}, u32[]{:S(2)}, u32[]{:S(2)}) collective-permute-start(bf16[528,128]{1,0:T(8,128)(2,1)S(1)} %get-tuple-element.36), channel_id=1, source_target_pairs={{0,144},{16,128},{32,176},{48,160},{64,208},{80,192},{96,240},{112... | collective-permute-start | bytes 405512 | tf_op jit(solution)/shard_map/ppermute | solution.py:418
  88.3 48.7 %copy-start.6 = (bf16[528,128]{1,0:T(8,128)(2,1)}, bf16[528,128]{1,0:T(8,128)(2,1)S(1)}, u32[]{:S(2)}) copy-start(bf16[528,128]{1,0:T(8,128)(2,1)S(1)} %collective-permute-done.4.refs_5_) | copy-start | bytes 405508
  88.3 19.2 %collective-permute-start.9 = (bf16[528,128]{1,0:T(8,128)(2,1)S(1)}, bf16[528,128]{1,0:T(8,128)(2,1)S(1)}, u32[]{:S(2)}, u32[]{:S(2)}) collective-permute-start(bf16[528,128]{1,0:T(8,128)(2,1)S(1)} %get-tuple-element.37), channel_id=1, source_target_pairs={{0,160},{16,176},{32,128},{48,144},{64,224},{80,240},{96,192},{112... | collective-permute-start | bytes 405512 | tf_op jit(solution)/shard_map/ppermute | solution.py:418
  93.0 44.1 %copy-start.7 = (bf16[528,128]{1,0:T(8,128)(2,1)}, bf16[528,128]{1,0:T(8,128)(2,1)S(1)}, u32[]{:S(2)}) copy-start(bf16[528,128]{1,0:T(8,128)(2,1)S(1)} %collective-permute-done.5.refs_6_) | copy-start | bytes 405508
  93.0 21.8 %collective-permute-start.10 = (bf16[528,128]{1,0:T(8,128)(2,1)S(1)}, bf16[528,128]{1,0:T(8,128)(2,1)S(1)}, u32[]{:S(2)}, u32[]{:S(2)}) collective-permute-start(bf16[528,128]{1,0:T(8,128)(2,1)S(1)} %get-tuple-element.38), channel_id=1, source_target_pairs={{0,176},{16,160},{32,144},{48,128},{64,240},{80,224},{96,208},{112... | collective-permute-start | bytes 405512 | tf_op jit(solution)/shard_map/ppermute | solution.py:418
  95.6 41.4 %copy-start.8 = (bf16[528,128]{1,0:T(8,128)(2,1)}, bf16[528,128]{1,0:T(8,128)(2,1)S(1)}, u32[]{:S(2)}) copy-start(bf16[528,128]{1,0:T(8,128)(2,1)S(1)} %collective-permute-done.6.refs_7_) | copy-start | bytes 405508
  95.6 24.7 %collective-permute-start.11 = (bf16[528,128]{1,0:T(8,128)(2,1)S(1)}, bf16[528,128]{1,0:T(8,128)(2,1)S(1)}, u32[]{:S(2)}, u32[]{:S(2)}) collective-permute-start(bf16[528,128]{1,0:T(8,128)(2,1)S(1)} %get-tuple-element.39), channel_id=1, source_target_pairs={{0,192},{16,208},{32,224},{48,240},{64,128},{80,144},{96,160},{112... | collective-permute-start | bytes 405512 | tf_op jit(solution)/shard_map/ppermute | solution.py:418
  98.7 38.3 %copy-start.9 = (bf16[528,128]{1,0:T(8,128)(2,1)}, bf16[528,128]{1,0:T(8,128)(2,1)S(1)}, u32[]{:S(2)}) copy-start(bf16[528,128]{1,0:T(8,128)(2,1)S(1)} %collective-permute-done.7.refs_8_) | copy-start | bytes 405508
  98.7 24.0 %collective-permute-start.12 = (bf16[528,128]{1,0:T(8,128)(2,1)S(1)}, bf16[528,128]{1,0:T(8,128)(2,1)S(1)}, u32[]{:S(2)}, u32[]{:S(2)}) collective-permute-start(bf16[528,128]{1,0:T(8,128)(2,1)S(1)} %get-tuple-element.40), channel_id=1, source_target_pairs={{0,208},{16,192},{32,240},{48,224},{64,144},{80,128},{96,176},{112... | collective-permute-start | bytes 405512 | tf_op jit(solution)/shard_map/ppermute | solution.py:418
  100.8 36.2 %copy-start.10 = (bf16[528,128]{1,0:T(8,128)(2,1)}, bf16[528,128]{1,0:T(8,128)(2,1)S(1)}, u32[]{:S(2)}) copy-start(bf16[528,128]{1,0:T(8,128)(2,1)S(1)} %collective-permute-done.8.refs_9_) | copy-start | bytes 405508
  100.8 30.6 %collective-permute-start.13 = (bf16[528,128]{1,0:T(8,128)(2,1)S(1)}, bf16[528,128]{1,0:T(8,128)(2,1)S(1)}, u32[]{:S(2)}, u32[]{:S(2)}) collective-permute-start(bf16[528,128]{1,0:T(8,128)(2,1)S(1)} %get-tuple-element.41), channel_id=1, source_target_pairs={{0,224},{16,240},{32,192},{48,208},{64,160},{80,176},{96,128},{112... | collective-permute-start | bytes 405512 | tf_op jit(solution)/shard_map/ppermute | solution.py:418
  107.5 29.6 %copy-start.11 = (bf16[528,128]{1,0:T(8,128)(2,1)}, bf16[528,128]{1,0:T(8,128)(2,1)S(1)}, u32[]{:S(2)}) copy-start(bf16[528,128]{1,0:T(8,128)(2,1)S(1)} %collective-permute-done.9.refs_10_) | copy-start | bytes 405508
  107.5 29.5 %collective-permute-start.14 = (bf16[528,128]{1,0:T(8,128)(2,1)S(1)}, bf16[528,128]{1,0:T(8,128)(2,1)S(1)}, u32[]{:S(2)}, u32[]{:S(2)}) collective-permute-start(bf16[528,128]{1,0:T(8,128)(2,1)S(1)} %get-tuple-element.42), channel_id=1, source_target_pairs={{0,240},{16,224},{32,208},{48,192},{64,176},{80,160},{96,144},{112... | collective-permute-start | bytes 405512 | tf_op jit(solution)/shard_map/ppermute | solution.py:418
  114.8 22.3 %copy-start.12 = (bf16[528,128]{1,0:T(8,128)(2,1)}, bf16[528,128]{1,0:T(8,128)(2,1)S(1)}, u32[]{:S(2)}) copy-start(bf16[528,128]{1,0:T(8,128)(2,1)S(1)} %collective-permute-done.10.refs_11_) | copy-start | bytes 405508
  120.4 16.7 %copy-start.13 = (bf16[528,128]{1,0:T(8,128)(2,1)}, bf16[528,128]{1,0:T(8,128)(2,1)S(1)}, u32[]{:S(2)}) copy-start(bf16[528,128]{1,0:T(8,128)(2,1)S(1)} %collective-permute-done.11.refs_12_) | copy-start | bytes 405508
  122.7 14.4 %copy-start.14 = (bf16[528,128]{1,0:T(8,128)(2,1)}, bf16[528,128]{1,0:T(8,128)(2,1)S(1)}, u32[]{:S(2)}) copy-start(bf16[528,128]{1,0:T(8,128)(2,1)S(1)} %collective-permute-done.12.refs_13_) | copy-start | bytes 405508
  131.4 5.7 %copy-start.15 = (bf16[528,128]{1,0:T(8,128)(2,1)}, bf16[528,128]{1,0:T(8,128)(2,1)S(1)}, u32[]{:S(2)}) copy-start(bf16[528,128]{1,0:T(8,128)(2,1)S(1)} %collective-permute-done.13.refs_14_) | copy-start | bytes 405508
  137.0 0.7 copy-start.16
  165.0 5.5 %copy-start.1 = (s32[16,256]{1,0:T(8,128)S(1)}, s32[16,256]{1,0:T(8,128)}, u32[]{:S(2)}) copy-start(s32[16,256]{1,0:T(8,128)} %get-tuple-element.25) | copy-start | bytes 49156
  165.0 59.5 %all-to-all-start.2 = ((bf16[256,32,128]{2,1,0:T(8,128)(2,1)}), bf16[256,32,128]{2,1,0:T(8,128)(2,1)S(1)}, u32[]{:S(2)}, u32[]{:S(2)}) async-start(bf16[256,32,128]{2,1,0:T(8,128)(2,1)} %shard_map.68), calls=%async_computation.2 | async-start | bytes 4194304 | tf_op jit(solution)/shard_map/all_to_all | solution.py:452

commit v6 on v5

--- a/solution.py
+++ b/solution.py
@@ -66,12 +66,13 @@
     rows, heads, width = q_ref.shape
     kinds = (label_ref[:, 0, :].astype(jnp.float32), key_scale_ref[...], value_scale_ref[...])
     meta = [
-        kind[:, n * width : (n + 1) * width].astype(jnp.bfloat16)
+        kind[:, n * width : (n + 1) * width].astype(jnp.float32)
         for kind in kinds
         for n in range(rows // width)
     ]
-    meta.append(jnp.zeros(((META - len(meta)) * heads, width), jnp.bfloat16))
-    turned = matmul(swap_matrix(META, heads, 1), jnp.concatenate(meta, axis=0))
+    meta.append(jnp.zeros(((META - len(meta)) * heads, width), jnp.float32))
+    meta = jnp.concatenate(meta, axis=0).astype(jnp.bfloat16)
+    turned = matmul(swap_matrix(META, heads, 1), meta)
     out_ref[:, rows : rows + META, :] = turned.astype(jnp.bfloat16).reshape(heads, META, width)
     group = 256 // heads
     swap = swap_matrix(group, heads, 1)
@@ -372,6 +373,14 @@
     labels = jnp.swapaxes(cluster_label, 1, 2)
     packed = pl.pallas_call(
         pack_kernel,
+        grid=(heads // HALF,),
+        in_specs=[
+            pl.BlockSpec((HALF, 1, rows), lambda i: (i, 0, 0)),
+            pl.BlockSpec((HALF, rows), lambda i: (i, 0)),
+            pl.BlockSpec((HALF, rows), lambda i: (i, 0)),
+            pl.BlockSpec((rows, HALF, width), lambda i: (0, i, 0)),
+        ],
+        out_specs=pl.BlockSpec((HALF, rows + META, width), lambda i: (i, 0, 0)),
         out_shape=jax.ShapeDtypeStruct((heads, rows + META, width), bf16),
         cost_estimate=pl.CostEstimate(flops=10**9, bytes_accessed=2**21, transcendentals=0),
     )(labels, key_scale.T, value_scale.T, queries)

time: 229 us -> 228 us (level)
  no operation moved by 1% of the time
where the time goes in v6:
time: 228 us
  waiting for transfers between devices  130 us (57%)
  starting transfers between devices  60.8 us (27%)
  Pallas kernels  35.4 us (16%)
    all_to_all x1, waiting for transfers between devices, shards(): answer = lax.all_to_all(answer, BOTH, 0, 0, tiled=True)  53.9 us
    ppermute x15, waiting for transfers between devices, shards(): lax.ppermute(parts[d], 'outer', [(n, n ^ d) for n in range(outer)])  44.1 us
    ppermute x15, starting transfers between devices, shards(): lax.ppermute(parts[d], 'outer', [(n, n ^ d) for n in range(outer)])  35.1 us
    all_to_all x1, waiting for transfers between devices, shards(): packed = lax.all_to_all(packed, 'inner', 0, 0, tiled=True)  22.6 us
    pallas_call x1, Pallas kernels, shards(): pl.pallas_call(attend_kernel, in_specs=[anywhere, anywhere, pl.BlockSpec(...  14.3 us
    all_to_all x1, starting transfers between devices, shards(): message = lax.all_to_all(message, BOTH, 0, 0, tiled=True)  10.2 us
    all_to_all x1, starting transfers between devices, shards(): packed = lax.all_to_all(packed, 'inner', 0, 0, tiled=True)  9.98 us
    all_to_all x1, waiting for transfers between devices, shards(): message = lax.all_to_all(message, BOTH, 0, 0, tiled=True)  9.47 us
  transfers between devices with their start and end apart: 18, of which 13 were waited for; matrix products, arithmetic and copies ran while one was open for 0% of the time, Pallas kernels for 6%

profile of v6, /device:TPU:1, one launch (start us, length us, event | category | flops | bytes accessed | tf_op | source)
XLA Modules:
  0.0 228.0 jit_solution(1621190138140408086)
XLA Ops:
  0.0 2.9 %shard_map.65 = bf16[16,264,128]{2,1,0:T(8,128)(2,1)} custom-call(s32[16,1,256]{2,1,0:T(1,128)} %bitcast.10, bf16[16,256]{1,0:T(8,128)(2,1)} %bitcast.12, bf16[16,256]{1,0:T(8,128)(2,1)} %bitcast.13, bf16[256,16,128]{2,1,0:T(8,128)(2,1)} %q_ref.1), custom_call_target="tpu_custom_call" | custom-call | flops 1000000000 | bytes 2097152 | tf_op jit(solution)/shard_map/pallas_call | solution.py:374
  2.9 10.0 %all-to-all-start.1 = ((bf16[16,264,128]{2,1,0:T(8,128)(2,1)}), bf16[16,264,128]{2,1,0:T(8,128)(2,1)S(1)}, u32[]{:S(2)}, u32[]{:S(2)}) async-start(bf16[16,264,128]{2,1,0:T(8,128)(2,1)} %shard_map.65), calls=%async_computation.1 | async-start | bytes 2162688 | tf_op jit(solution)/shard_map/all_to_all | solution.py:387
  12.8 5.9 %shard_map.64 = (s32[16,256]{1,0:T(8,128)}, bf16[16,16,32,256]{3,2,1,0:T(8,128)(2,1)}) custom-call(s32[16,1,256]{2,1,0:T(1,128)} %bitcast.11, bf16[256,16,128]{2,1,0:T(8,128)(2,1)} %k_ref.1, bf16[256,16,128]{2,1,0:T(8,128)(2,1)} %v_ref.1), custom_call_target="tpu_custom_call" | custom-call | flops 3000000000 | bytes 6291456 | tf_op jit(solution)/shard_map/pallas_call | solution.py:390
  18.8 22.6 %all-to-all-done.1.arrived_ref = bf16[16,264,128]{2,1,0:T(8,128)(2,1)S(1)} async-done(((bf16[16,264,128]{2,1,0:T(8,128)(2,1)}), bf16[16,264,128]{2,1,0:T(8,128)(2,1)S(1)}, u32[]{:S(2)}, u32[]{:S(2)}) %all-to-all-start.1) | async-done | bytes 1081376 | tf_op jit(solution)/shard_map/all_to_all | solution.py:387
  41.4 10.2 %all-to-all-start = ((bf16[256,32,256]{2,1,0:T(8,128)(2,1)}), bf16[256,32,256]{2,1,0:T(8,128)(2,1)}, u32[]{:S(2)}, u32[]{:S(2)}) async-start(bf16[256,32,256]{2,1,0:T(8,128)(2,1)} %bitcast.9), calls=%async_computation | async-start | bytes 8388608 | tf_op jit(solution)/shard_map/all_to_all | solution.py:408
  51.7 5.2 %shard_map.66 = (bf16[528,128]{1,0:T(8,128)(2,1)S(1)}, bf16[528,128]{1,0:T(8,128)(2,1)S(1)}, bf16[528,128]{1,0:T(8,128)(2,1)S(1)}, bf16[528,128]{1,0:T(8,128)(2,...) custom-call(s32[1]{0:T(128)} %bitcast.3.me_ref, ...), custom_call_target="tpu_custom_call" | custom-call | flops 2000000000 | bytes 3145728 | tf_op jit(solution)/shard_map/pallas_call | solution.py:411
  56.9 0.0 copy-start
  56.9 0.6 copy-done
  57.5 1.4 collective-permute-start
  58.9 2.4 %collective-permute-start.1 = (bf16[528,128]{1,0:T(8,128)(2,1)S(1)}, bf16[528,128]{1,0:T(8,128)(2,1)S(1)}, u32[]{:S(2)}, u32[]{:S(2)}) collective-permute-start(bf16[528,128]{1,0:T(8,128)(2,1)S(1)} %get-tuple-element.29), channel_id=1, source_target_pairs={{0,32},{16,48},{32,0},{48,16},{64,96},{80,112},{96,64},{112,80},{1... | collective-permute-start | bytes 405512 | tf_op jit(solution)/shard_map/ppermute | solution.py:427
  61.4 0.0 collective-permute-start.2
  61.4 1.4 collective-permute-start.3
  62.8 0.0 collective-permute-start.4
  62.8 3.2 %collective-permute-done.refs_1_ = bf16[528,128]{1,0:T(8,128)(2,1)S(1)} collective-permute-done((bf16[528,128]{1,0:T(8,128)(2,1)S(1)}, bf16[528,128]{1,0:T(8,128)(2,1)S(1)}, u32[]{:S(2)}, u32[]{:S(2)}) %collective-permute-start) | collective-permute-done | bytes 135200 | tf_op jit(solution)/shard_map/ppermute | solution.py:427
  66.0 0.0 copy-start.2
  66.0 4.5 %collective-permute-start.5 = (bf16[528,128]{1,0:T(8,128)(2,1)S(1)}, bf16[528,128]{1,0:T(8,128)(2,1)S(1)}, u32[]{:S(2)}, u32[]{:S(2)}) collective-permute-start(bf16[528,128]{1,0:T(8,128)(2,1)S(1)} %get-tuple-element.33), channel_id=1, source_target_pairs={{0,96},{16,112},{32,64},{48,80},{64,32},{80,48},{96,0},{112,16},{1... | collective-permute-start | bytes 405512 | tf_op jit(solution)/shard_map/ppermute | solution.py:427
  70.5 13.4 %collective-permute-done.1.refs_2_ = bf16[528,128]{1,0:T(8,128)(2,1)S(1)} collective-permute-done((bf16[528,128]{1,0:T(8,128)(2,1)S(1)}, bf16[528,128]{1,0:T(8,128)(2,1)S(1)}, u32[]{:S(2)}, u32[]{:S(2)}) %collective-permute-start.1) | collective-permute-done | bytes 135200 | tf_op jit(solution)/shard_map/ppermute | solution.py:427
  83.9 2.5 %collective-permute-start.6 = (bf16[528,128]{1,0:T(8,128)(2,1)S(1)}, bf16[528,128]{1,0:T(8,128)(2,1)S(1)}, u32[]{:S(2)}, u32[]{:S(2)}) collective-permute-start(bf16[528,128]{1,0:T(8,128)(2,1)S(1)} %get-tuple-element.34), channel_id=1, source_target_pairs={{0,112},{16,96},{32,80},{48,64},{64,48},{80,32},{96,16},{112,0},{1... | collective-permute-start | bytes 405512 | tf_op jit(solution)/shard_map/ppermute | solution.py:427
  86.5 0.0 collective-permute-done.2.refs_3_
  86.5 1.6 collective-permute-start.7
  88.1 0.0 collective-permute-done.3.refs_4_
  88.1 0.0 collective-permute-start.8
  88.1 0.0 collective-permute-done.4.refs_5_
  88.1 0.0 copy-start.6
  88.1 4.7 %collective-permute-start.9 = (bf16[528,128]{1,0:T(8,128)(2,1)S(1)}, bf16[528,128]{1,0:T(8,128)(2,1)S(1)}, u32[]{:S(2)}, u32[]{:S(2)}) collective-permute-start(bf16[528,128]{1,0:T(8,128)(2,1)S(1)} %get-tuple-element.37), channel_id=1, source_target_pairs={{0,160},{16,176},{32,128},{48,144},{64,224},{80,240},{96,192},{112... | collective-permute-start | bytes 405512 | tf_op jit(solution)/shard_map/ppermute | solution.py:427
  92.8 0.0 collective-permute-done.5.refs_6_
  92.8 2.7 %collective-permute-start.10 = (bf16[528,128]{1,0:T(8,128)(2,1)S(1)}, bf16[528,128]{1,0:T(8,128)(2,1)S(1)}, u32[]{:S(2)}, u32[]{:S(2)}) collective-permute-start(bf16[528,128]{1,0:T(8,128)(2,1)S(1)} %get-tuple-element.38), channel_id=1, source_target_pairs={{0,176},{16,160},{32,144},{48,128},{64,240},{80,224},{96,208},{112... | collective-permute-start | bytes 405512 | tf_op jit(solution)/shard_map/ppermute | solution.py:427
  95.4 0.0 collective-permute-done.6.refs_7_
  95.4 0.5 collective-permute-start.11
  95.9 2.6 %collective-permute-done.7.refs_8_ = bf16[528,128]{1,0:T(8,128)(2,1)S(1)} collective-permute-done((bf16[528,128]{1,0:T(8,128)(2,1)S(1)}, bf16[528,128]{1,0:T(8,128)(2,1)S(1)}, u32[]{:S(2)}, u32[]{:S(2)}) %collective-permute-start.7) | collective-permute-done | bytes 135200 | tf_op jit(solution)/shard_map/ppermute | solution.py:427
  98.5 1.4 collective-permute-start.12
  99.9 0.8 collective-permute-done.8.refs_9_
  100.6 5.7 %collective-permute-start.13 = (bf16[528,128]{1,0:T(8,128)(2,1)S(1)}, bf16[528,128]{1,0:T(8,128)(2,1)S(1)}, u32[]{:S(2)}, u32[]{:S(2)}) collective-permute-start(bf16[528,128]{1,0:T(8,128)(2,1)S(1)} %get-tuple-element.41), channel_id=1, source_target_pairs={{0,224},{16,240},{32,192},{48,208},{64,160},{80,176},{96,128},{112... | collective-permute-start | bytes 405512 | tf_op jit(solution)/shard_map/ppermute | solution.py:427
  106.3 1.0 collective-permute-done.9.refs_10_
  107.3 6.3 %collective-permute-start.14 = (bf16[528,128]{1,0:T(8,128)(2,1)S(1)}, bf16[528,128]{1,0:T(8,128)(2,1)S(1)}, u32[]{:S(2)}, u32[]{:S(2)}) collective-permute-start(bf16[528,128]{1,0:T(8,128)(2,1)S(1)} %get-tuple-element.42), channel_id=1, source_target_pairs={{0,240},{16,224},{32,208},{48,192},{64,176},{80,160},{96,144},{112... | collective-permute-start | bytes 405512 | tf_op jit(solution)/shard_map/ppermute | solution.py:427
  113.6 0.9 collective-permute-done.10.refs_11_
  114.6 5.6 %collective-permute-done.11.refs_12_ = bf16[528,128]{1,0:T(8,128)(2,1)S(1)} collective-permute-done((bf16[528,128]{1,0:T(8,128)(2,1)S(1)}, bf16[528,128]{1,0:T(8,128)(2,1)S(1)}, u32[]{:S(2)}, u32[]{:S(2)}) %collective-permute-start.11) | collective-permute-done | bytes 135200 | tf_op jit(solution)/shard_map/ppermute | solution.py:427
  120.2 2.4 %collective-permute-done.12.refs_13_ = bf16[528,128]{1,0:T(8,128)(2,1)S(1)} collective-permute-done((bf16[528,128]{1,0:T(8,128)(2,1)S(1)}, bf16[528,128]{1,0:T(8,128)(2,1)S(1)}, u32[]{:S(2)}, u32[]{:S(2)}) %collective-permute-start.12) | collective-permute-done | bytes 135200 | tf_op jit(solution)/shard_map/ppermute | solution.py:427
  122.5 8.7 %collective-permute-done.13.refs_14_ = bf16[528,128]{1,0:T(8,128)(2,1)S(1)} collective-permute-done((bf16[528,128]{1,0:T(8,128)(2,1)S(1)}, bf16[528,128]{1,0:T(8,128)(2,1)S(1)}, u32[]{:S(2)}, u32[]{:S(2)}) %collective-permute-start.13) | collective-permute-done | bytes 135200 | tf_op jit(solution)/shard_map/ppermute | solution.py:427
  131.2 5.6 %collective-permute-done.14.refs_15_ = bf16[528,128]{1,0:T(8,128)(2,1)S(1)} collective-permute-done((bf16[528,128]{1,0:T(8,128)(2,1)S(1)}, bf16[528,128]{1,0:T(8,128)(2,1)S(1)}, u32[]{:S(2)}, u32[]{:S(2)}) %collective-permute-start.14) | collective-permute-done | bytes 135200 | tf_op jit(solution)/shard_map/ppermute | solution.py:427
  136.8 0.0 copy-done.2
  136.8 0.0 copy-done.3
  136.8 0.0 copy-done.4
  136.8 0.0 copy-done.5
  136.8 0.0 copy-done.6
  136.9 0.0 copy-done.7
  136.9 0.0 copy-done.8
  136.9 0.0 copy-done.9
  136.9 0.0 copy-done.10
  136.9 0.0 copy-done.11
  136.9 0.0 copy-done.12
  136.9 0.0 copy-done.13
  136.9 0.0 copy-done.14
  136.9 0.0 copy-done.15
  136.9 0.5 copy-done.16
  137.5 3.5 %shard_map.67 = (bf16[8,1024,128]{2,1,0:T(8,128)(2,1)}, f32[16,1024]{1,0:T(8,128)}) custom-call(s32[1]{0:T(128)} %bitcast.3.me_ref, bf16[528,128]{1,0:T(8,128)(2,1)} %copy-done, bf16[528,128]{1,0:T(8,128)(2,1)} %copy-done.2, bf16[528,128]{1,0:T(8,128)(2,1)} %copy-done.3, bf16[528,128]{1,0:T(8,128)(2,1)} %copy-done.4, bf16[528,128]{1,0:T(8,128)(2,1)} %copy-done.5, ...), custom_call_target="tpu_custom_call" | custom-call | flops 1000000000 | bytes 4194304 | tf_op jit(solution)/shard_map/pallas_call | solution.py:432
  141.0 9.5 %all-to-all-done.arrived_ref = bf16[256,32,256]{2,1,0:T(8,128)(2,1)} async-done(((bf16[256,32,256]{2,1,0:T(8,128)(2,1)}), bf16[256,32,256]{2,1,0:T(8,128)(2,1)}, u32[]{:S(2)}, u32[]{:S(2)}) %all-to-all-start) | async-done | bytes 4194336 | tf_op jit(solution)/shard_map/all_to_all | solution.py:408
  150.5 14.3 %shard_map.68 = bf16[256,32,128]{2,1,0:T(8,128)(2,1)} custom-call(bf16[256,32,256]{2,1,0:T(8,128)(2,1)} %all-to-all-done.arrived_ref, bf16[8,1024,128]{2,1,0:T(8,128)(2,1)} %get-tuple-element.43.q_ref, f32[16,1024]{1,0:T(8,128)} %get-tuple-element.44.scales), custom_call_target="tpu_custom_call" | custom-call | flops 4000000000 | bytes 8388608 | tf_op jit(solution)/shard_map/pallas_call | solution.py:444
  164.8 0.0 copy-start.1
  164.8 5.5 %all-to-all-start.2 = ((bf16[256,32,128]{2,1,0:T(8,128)(2,1)}), bf16[256,32,128]{2,1,0:T(8,128)(2,1)S(1)}, u32[]{:S(2)}, u32[]{:S(2)}) async-start(bf16[256,32,128]{2,1,0:T(8,128)(2,1)} %shard_map.68), calls=%async_computation.2 | async-start | bytes 4194304 | tf_op jit(solution)/shard_map/all_to_all | solution.py:461
  170.3 0.0 copy-done.1
  170.3 0.1 copy.7
  170.4 53.9 %all-to-all-done.2 = bf16[256,32,128]{2,1,0:T(8,128)(2,1)S(1)} async-done(((bf16[256,32,128]{2,1,0:T(8,128)(2,1)}), bf16[256,32,128]{2,1,0:T(8,128)(2,1)S(1)}, u32[]{:S(2)}, u32[]{:S(2)}) %all-to-all-start.2) | async-done | bytes 2097184 | tf_op jit(solution)/shard_map/all_to_all | solution.py:461
  224.3 3.5 %shard_map.69 = bf16[256,16,128]{2,1,0:T(8,128)(2,1)} custom-call(s32[256,16]{1,0:T(8,128)S(1)} %bitcast.8, bf16[16,16,32,128]{3,2,1,0:T(8,128)(2,1)S(1)} %bitcast.7), custom_call_target="tpu_custom_call" | custom-call | flops 1000000000 | bytes 3145728 | tf_op jit(solution)/shard_map/pallas_call | solution.py:463
  (13 shorter events, 0.0 us)
Async XLA Ops:
  2.9 38.6 %all-to-all-start.1 = ((bf16[16,264,128]{2,1,0:T(8,128)(2,1)}), bf16[16,264,128]{2,1,0:T(8,128)(2,1)S(1)}, u32[]{:S(2)}, u32[]{:S(2)}) async-start(bf16[16,264,128]{2,1,0:T(8,128)(2,1)} %shard_map.65), calls=%async_computation.1 | async-start | bytes 2162688 | tf_op jit(solution)/shard_map/all_to_all | solution.py:387
  41.4 109.1 %all-to-all-start = ((bf16[256,32,256]{2,1,0:T(8,128)(2,1)}), bf16[256,32,256]{2,1,0:T(8,128)(2,1)}, u32[]{:S(2)}, u32[]{:S(2)}) async-start(bf16[256,32,256]{2,1,0:T(8,128)(2,1)} %bitcast.9), calls=%async_computation | async-start | bytes 8388608 | tf_op jit(solution)/shard_map/all_to_all | solution.py:408
  56.9 0.7 copy-start
  57.5 8.4 %collective-permute-start = (bf16[528,128]{1,0:T(8,128)(2,1)S(1)}, bf16[528,128]{1,0:T(8,128)(2,1)S(1)}, u32[]{:S(2)}, u32[]{:S(2)}) collective-permute-start(bf16[528,128]{1,0:T(8,128)(2,1)S(1)} %get-tuple-element.28), channel_id=1, source_target_pairs={{0,16},{16,0},{32,48},{48,32},{64,80},{80,64},{96,112},{112,96},{1... | collective-permute-start | bytes 405512 | tf_op jit(solution)/shard_map/ppermute | solution.py:427
  58.9 25.0 %collective-permute-start.1 = (bf16[528,128]{1,0:T(8,128)(2,1)S(1)}, bf16[528,128]{1,0:T(8,128)(2,1)S(1)}, u32[]{:S(2)}, u32[]{:S(2)}) collective-permute-start(bf16[528,128]{1,0:T(8,128)(2,1)S(1)} %get-tuple-element.29), channel_id=1, source_target_pairs={{0,32},{16,48},{32,0},{48,16},{64,96},{80,112},{96,64},{112,80},{1... | collective-permute-start | bytes 405512 | tf_op jit(solution)/shard_map/ppermute | solution.py:427
  61.4 25.1 %collective-permute-start.2 = (bf16[528,128]{1,0:T(8,128)(2,1)S(1)}, bf16[528,128]{1,0:T(8,128)(2,1)S(1)}, u32[]{:S(2)}, u32[]{:S(2)}) collective-permute-start(bf16[528,128]{1,0:T(8,128)(2,1)S(1)} %get-tuple-element.30), channel_id=1, source_target_pairs={{0,48},{16,32},{32,16},{48,0},{64,112},{80,96},{96,80},{112,64},{1... | collective-permute-start | bytes 405512 | tf_op jit(solution)/shard_map/ppermute | solution.py:427
  61.4 26.7 %collective-permute-start.3 = (bf16[528,128]{1,0:T(8,128)(2,1)S(1)}, bf16[528,128]{1,0:T(8,128)(2,1)S(1)}, u32[]{:S(2)}, u32[]{:S(2)}) collective-permute-start(bf16[528,128]{1,0:T(8,128)(2,1)S(1)} %get-tuple-element.31), channel_id=1, source_target_pairs={{0,64},{16,80},{32,96},{48,112},{64,0},{80,16},{96,32},{112,48},{1... | collective-permute-start | bytes 405512 | tf_op jit(solution)/shard_map/ppermute | solution.py:427
  62.8 25.3 %collective-permute-start.4 = (bf16[528,128]{1,0:T(8,128)(2,1)S(1)}, bf16[528,128]{1,0:T(8,128)(2,1)S(1)}, u32[]{:S(2)}, u32[]{:S(2)}) collective-permute-start(bf16[528,128]{1,0:T(8,128)(2,1)S(1)} %get-tuple-element.32), channel_id=1, source_target_pairs={{0,80},{16,64},{32,112},{48,96},{64,16},{80,0},{96,48},{112,32},{1... | collective-permute-start | bytes 405512 | tf_op jit(solution)/shard_map/ppermute | solution.py:427
  66.0 70.9 %copy-start.2 = (bf16[528,128]{1,0:T(8,128)(2,1)}, bf16[528,128]{1,0:T(8,128)(2,1)S(1)}, u32[]{:S(2)}) copy-start(bf16[528,128]{1,0:T(8,128)(2,1)S(1)} %collective-permute-done.refs_1_) | copy-start | bytes 405508
  66.0 26.8 %collective-permute-start.5 = (bf16[528,128]{1,0:T(8,128)(2,1)S(1)}, bf16[528,128]{1,0:T(8,128)(2,1)S(1)}, u32[]{:S(2)}, u32[]{:S(2)}) collective-permute-start(bf16[528,128]{1,0:T(8,128)(2,1)S(1)} %get-tuple-element.33), channel_id=1, source_target_pairs={{0,96},{16,112},{32,64},{48,80},{64,32},{80,48},{96,0},{112,16},{1... | collective-permute-start | bytes 405512 | tf_op jit(solution)/shard_map/ppermute | solution.py:427
  83.9 52.9 %copy-start.3 = (bf16[528,128]{1,0:T(8,128)(2,1)}, bf16[528,128]{1,0:T(8,128)(2,1)S(1)}, u32[]{:S(2)}) copy-start(bf16[528,128]{1,0:T(8,128)(2,1)S(1)} %collective-permute-done.1.refs_2_) | copy-start | bytes 405508
  83.9 11.5 %collective-permute-start.6 = (bf16[528,128]{1,0:T(8,128)(2,1)S(1)}, bf16[528,128]{1,0:T(8,128)(2,1)S(1)}, u32[]{:S(2)}, u32[]{:S(2)}) collective-permute-start(bf16[528,128]{1,0:T(8,128)(2,1)S(1)} %get-tuple-element.34), channel_id=1, source_target_pairs={{0,112},{16,96},{32,80},{48,64},{64,48},{80,32},{96,16},{112,0},{1... | collective-permute-start | bytes 405512 | tf_op jit(solution)/shard_map/ppermute | solution.py:427
  86.5 50.4 %copy-start.4 = (bf16[528,128]{1,0:T(8,128)(2,1)}, bf16[528,128]{1,0:T(8,128)(2,1)S(1)}, u32[]{:S(2)}) copy-start(bf16[528,128]{1,0:T(8,128)(2,1)S(1)} %collective-permute-done.2.refs_3_) | copy-start | bytes 405508
  86.5 12.1 %collective-permute-start.7 = (bf16[528,128]{1,0:T(8,128)(2,1)S(1)}, bf16[528,128]{1,0:T(8,128)(2,1)S(1)}, u32[]{:S(2)}, u32[]{:S(2)}) collective-permute-start(bf16[528,128]{1,0:T(8,128)(2,1)S(1)} %get-tuple-element.35), channel_id=1, source_target_pairs={{0,128},{16,144},{32,160},{48,176},{64,192},{80,208},{96,224},{112... | collective-permute-start | bytes 405512 | tf_op jit(solution)/shard_map/ppermute | solution.py:427
  88.1 48.8 %copy-start.5 = (bf16[528,128]{1,0:T(8,128)(2,1)}, bf16[528,128]{1,0:T(8,128)(2,1)S(1)}, u32[]{:S(2)}) copy-start(bf16[528,128]{1,0:T(8,128)(2,1)S(1)} %collective-permute-done.3.refs_4_) | copy-start | bytes 405508
  88.1 12.6 %collective-permute-start.8 = (bf16[528,128]{1,0:T(8,128)(2,1)S(1)}, bf16[528,128]{1,0:T(8,128)(2,1)S(1)}, u32[]{:S(2)}, u32[]{:S(2)}) collective-permute-start(bf16[528,128]{1,0:T(8,128)(2,1)S(1)} %get-tuple-element.36), channel_id=1, source_target_pairs={{0,144},{16,128},{32,176},{48,160},{64,208},{80,192},{96,240},{112... | collective-permute-start | bytes 405512 | tf_op jit(solution)/shard_map/ppermute | solution.py:427
  88.1 48.8 %copy-start.6 = (bf16[528,128]{1,0:T(8,128)(2,1)}, bf16[528,128]{1,0:T(8,128)(2,1)S(1)}, u32[]{:S(2)}) copy-start(bf16[528,128]{1,0:T(8,128)(2,1)S(1)} %collective-permute-done.4.refs_5_) | copy-start | bytes 405508
  88.1 19.2 %collective-permute-start.9 = (bf16[528,128]{1,0:T(8,128)(2,1)S(1)}, bf16[528,128]{1,0:T(8,128)(2,1)S(1)}, u32[]{:S(2)}, u32[]{:S(2)}) collective-permute-start(bf16[528,128]{1,0:T(8,128)(2,1)S(1)} %get-tuple-element.37), channel_id=1, source_target_pairs={{0,160},{16,176},{32,128},{48,144},{64,224},{80,240},{96,192},{112... | collective-permute-start | bytes 405512 | tf_op jit(solution)/shard_map/ppermute | solution.py:427
  92.8 44.1 %copy-start.7 = (bf16[528,128]{1,0:T(8,128)(2,1)}, bf16[528,128]{1,0:T(8,128)(2,1)S(1)}, u32[]{:S(2)}) copy-start(bf16[528,128]{1,0:T(8,128)(2,1)S(1)} %collective-permute-done.5.refs_6_) | copy-start | bytes 405508
  92.8 21.8 %collective-permute-start.10 = (bf16[528,128]{1,0:T(8,128)(2,1)S(1)}, bf16[528,128]{1,0:T(8,128)(2,1)S(1)}, u32[]{:S(2)}, u32[]{:S(2)}) collective-permute-start(bf16[528,128]{1,0:T(8,128)(2,1)S(1)} %get-tuple-element.38), channel_id=1, source_target_pairs={{0,176},{16,160},{32,144},{48,128},{64,240},{80,224},{96,208},{112... | collective-permute-start | bytes 405512 | tf_op jit(solution)/shard_map/ppermute | solution.py:427
  95.4 41.4 %copy-start.8 = (bf16[528,128]{1,0:T(8,128)(2,1)}, bf16[528,128]{1,0:T(8,128)(2,1)S(1)}, u32[]{:S(2)}) copy-start(bf16[528,128]{1,0:T(8,128)(2,1)S(1)} %collective-permute-done.6.refs_7_) | copy-start | bytes 405508
  95.4 24.7 %collective-permute-start.11 = (bf16[528,128]{1,0:T(8,128)(2,1)S(1)}, bf16[528,128]{1,0:T(8,128)(2,1)S(1)}, u32[]{:S(2)}, u32[]{:S(2)}) collective-permute-start(bf16[528,128]{1,0:T(8,128)(2,1)S(1)} %get-tuple-element.39), channel_id=1, source_target_pairs={{0,192},{16,208},{32,224},{48,240},{64,128},{80,144},{96,160},{112... | collective-permute-start | bytes 405512 | tf_op jit(solution)/shard_map/ppermute | solution.py:427
  98.5 38.4 %copy-start.9 = (bf16[528,128]{1,0:T(8,128)(2,1)}, bf16[528,128]{1,0:T(8,128)(2,1)S(1)}, u32[]{:S(2)}) copy-start(bf16[528,128]{1,0:T(8,128)(2,1)S(1)} %collective-permute-done.7.refs_8_) | copy-start | bytes 405508
  98.5 24.0 %collective-permute-start.12 = (bf16[528,128]{1,0:T(8,128)(2,1)S(1)}, bf16[528,128]{1,0:T(8,128)(2,1)S(1)}, u32[]{:S(2)}, u32[]{:S(2)}) collective-permute-start(bf16[528,128]{1,0:T(8,128)(2,1)S(1)} %get-tuple-element.40), channel_id=1, source_target_pairs={{0,208},{16,192},{32,240},{48,224},{64,144},{80,128},{96,176},{112... | collective-permute-start | bytes 405512 | tf_op jit(solution)/shard_map/ppermute | solution.py:427
  100.6 36.3 %copy-start.10 = (bf16[528,128]{1,0:T(8,128)(2,1)}, bf16[528,128]{1,0:T(8,128)(2,1)S(1)}, u32[]{:S(2)}) copy-start(bf16[528,128]{1,0:T(8,128)(2,1)S(1)} %collective-permute-done.8.refs_9_) | copy-start | bytes 405508
  100.6 30.6 %collective-permute-start.13 = (bf16[528,128]{1,0:T(8,128)(2,1)S(1)}, bf16[528,128]{1,0:T(8,128)(2,1)S(1)}, u32[]{:S(2)}, u32[]{:S(2)}) collective-permute-start(bf16[528,128]{1,0:T(8,128)(2,1)S(1)} %get-tuple-element.41), channel_id=1, source_target_pairs={{0,224},{16,240},{32,192},{48,208},{64,160},{80,176},{96,128},{112... | collective-permute-start | bytes 405512 | tf_op jit(solution)/shard_map/ppermute | solution.py:427
  107.3 29.6 %copy-start.11 = (bf16[528,128]{1,0:T(8,128)(2,1)}, bf16[528,128]{1,0:T(8,128)(2,1)S(1)}, u32[]{:S(2)}) copy-start(bf16[528,128]{1,0:T(8,128)(2,1)S(1)} %collective-permute-done.9.refs_10_) | copy-start | bytes 405508
  107.3 29.5 %collective-permute-start.14 = (bf16[528,128]{1,0:T(8,128)(2,1)S(1)}, bf16[528,128]{1,0:T(8,128)(2,1)S(1)}, u32[]{:S(2)}, u32[]{:S(2)}) collective-permute-start(bf16[528,128]{1,0:T(8,128)(2,1)S(1)} %get-tuple-element.42), channel_id=1, source_target_pairs={{0,240},{16,224},{32,208},{48,192},{64,176},{80,160},{96,144},{112... | collective-permute-start | bytes 405512 | tf_op jit(solution)/shard_map/ppermute | solution.py:427
  114.6 22.3 %copy-start.12 = (bf16[528,128]{1,0:T(8,128)(2,1)}, bf16[528,128]{1,0:T(8,128)(2,1)S(1)}, u32[]{:S(2)}) copy-start(bf16[528,128]{1,0:T(8,128)(2,1)S(1)} %collective-permute-done.10.refs_11_) | copy-start | bytes 405508
  120.2 16.8 %copy-start.13 = (bf16[528,128]{1,0:T(8,128)(2,1)}, bf16[528,128]{1,0:T(8,128)(2,1)S(1)}, u32[]{:S(2)}) copy-start(bf16[528,128]{1,0:T(8,128)(2,1)S(1)} %collective-permute-done.11.refs_12_) | copy-start | bytes 405508
  122.5 14.4 %copy-start.14 = (bf16[528,128]{1,0:T(8,128)(2,1)}, bf16[528,128]{1,0:T(8,128)(2,1)S(1)}, u32[]{:S(2)}) copy-start(bf16[528,128]{1,0:T(8,128)(2,1)S(1)} %collective-permute-done.12.refs_13_) | copy-start | bytes 405508
  131.2 5.7 %copy-start.15 = (bf16[528,128]{1,0:T(8,128)(2,1)}, bf16[528,128]{1,0:T(8,128)(2,1)S(1)}, u32[]{:S(2)}) copy-start(bf16[528,128]{1,0:T(8,128)(2,1)S(1)} %collective-permute-done.13.refs_14_) | copy-start | bytes 405508
  136.8 0.7 copy-start.16
  164.8 5.5 %copy-start.1 = (s32[16,256]{1,0:T(8,128)S(1)}, s32[16,256]{1,0:T(8,128)}, u32[]{:S(2)}) copy-start(s32[16,256]{1,0:T(8,128)} %get-tuple-element.25) | copy-start | bytes 49156
  164.8 59.5 %all-to-all-start.2 = ((bf16[256,32,128]{2,1,0:T(8,128)(2,1)}), bf16[256,32,128]{2,1,0:T(8,128)(2,1)S(1)}, u32[]{:S(2)}, u32[]{:S(2)}) async-start(bf16[256,32,128]{2,1,0:T(8,128)(2,1)} %shard_map.68), calls=%async_computation.2 | async-start | bytes 4194304 | tf_op jit(solution)/shard_map/all_to_all | solution.py:461
